TPU v7x, 256 devices: a whole 4x4x8 slice. The times are simulated.
256 devices in a mesh: ctx: 8 (over z), head: 4 (over y_hi, core), sess: 8 (over y_lo, x).
Axes of the slice: x: 4, y: 4 (y_hi: 2, y_lo: 2; y = y_hi * 2 + y_lo), z: 8, core: 2. Of those that a mesh axis runs over, the one named last changes fastest.
Arguments:
- queries: bfloat16 [512, 64, 128], P(('ctx', 'sess'), 'head'), may hold values from -300 to 300
- prefix_keys: bfloat16 [8, 49152, 128], P('head', 'ctx'), may hold values from -5 to 5
- prefix_values: bfloat16 [8, 49152, 128], P('head', 'ctx'), may hold values from -6 to 6
- suffix_keys: bfloat16 [512, 8, 512, 128], P(('ctx', 'sess'), 'head'), may hold values from -7 to 7
- suffix_values: bfloat16 [512, 8, 512, 128], P(('ctx', 'sess'), 'head'), may hold values from -6 to 6
- lengths: int32 [512], P(('ctx', 'sess')), may hold values from 1 to 512, as said below
- out_weight: bfloat16 [8192, 8192], P('head', ('ctx', 'sess')), may hold values from -0.0625 to 0.0625
Outputs:
- layer_out: float32 [512, 8192], P('head', ('ctx', 'sess'))
Inputs may be any that keep to these rules, and one draw needn't show every extreme that they name: `lengths`: every session has at least one live suffix token; some session has exactly 512.
All inputs are finite; a program needn't handle non-finite values.
Results may differ from a plain program's by a relative error of at most 0.0065.
Values may be sent and summed in bfloat16 or wider, within the bound.
No kernel may reach another device: no remote copies, remote signals or barrier semaphores. Data moves between devices by JAX's collectives and lax.ppermute only.
A program may use at most 64 MiB of HBM per device.

v0:
```python
import math

import jax
import jax.numpy as jnp
from jax import lax
from jax.sharding import PartitionSpec as P


def online_update(state_carry, scores, values, einsum_form):
    run_max, run_sum, numerator = state_carry
    new_max = jnp.maximum(run_max, jnp.max(scores, axis=-1))
    factor = jnp.exp(run_max - new_max)
    weights = jnp.exp(scores - new_max[..., None])
    new_sum = run_sum * factor + jnp.sum(weights, axis=-1)
    product = jnp.einsum(
        einsum_form, weights.astype(jnp.bfloat16), values, preferred_element_type=jnp.float32
    )
    return (new_max, new_sum, numerator * factor[..., None] + product)


def per_device(
    queries, prefix_keys, prefix_values, suffix_keys, suffix_values, lengths, out_weight
):
    own_rows = queries.shape[0]
    kv_local = prefix_keys.shape[0]
    head_dim = queries.shape[2]
    group_size = queries.shape[1] // kv_local
    score_scale = 1.0 / math.sqrt(head_dim)
    gathered = lax.all_gather(queries, "ctx", axis=0, tiled=True)
    rows_total = gathered.shape[0]
    grouped = gathered.reshape(rows_total, kv_local, group_size, head_dim)
    prefix_len = prefix_keys.shape[1]
    key_block_len = min(512, prefix_len)

    def prefix_step(state_carry, block_index):
        first_key = block_index * key_block_len
        key_block = lax.dynamic_slice_in_dim(prefix_keys, first_key, key_block_len, 1)
        value_block = lax.dynamic_slice_in_dim(prefix_values, first_key, key_block_len, 1)
        scores = (
            jnp.einsum("rkgd,knd->rkgn", grouped, key_block, preferred_element_type=jnp.float32)
            * score_scale
        )
        return (online_update(state_carry, scores, value_block, "rkgn,knd->rkgd"), None)

    start_state = (
        jnp.full((rows_total, kv_local, group_size), -1e30, jnp.float32),
        jnp.zeros((rows_total, kv_local, group_size), jnp.float32),
        jnp.zeros((rows_total, kv_local, group_size, head_dim), jnp.float32),
    )
    prefix_state, unused = lax.scan(
        prefix_step, start_state, jnp.arange(prefix_len // key_block_len, dtype=jnp.int32)
    )
    run_max, run_sum, numerator = prefix_state
    max_parts, sum_parts, numer_parts = (
        lax.all_to_all(run_max, "ctx", split_axis=0, concat_axis=0, tiled=True),
        lax.all_to_all(run_sum, "ctx", split_axis=0, concat_axis=0, tiled=True),
        lax.all_to_all(numerator, "ctx", split_axis=0, concat_axis=0, tiled=True),
    )
    sources = max_parts.shape[0] // own_rows
    max_parts = max_parts.reshape(sources, own_rows, kv_local, group_size)
    sum_parts = sum_parts.reshape(sources, own_rows, kv_local, group_size)
    numer_parts = numer_parts.reshape(sources, own_rows, kv_local, group_size, head_dim)
    row_top = jnp.max(max_parts, axis=0)
    rescale = jnp.exp(max_parts - row_top[None])
    merged_sum = jnp.sum(sum_parts * rescale, axis=0)
    merged_numer = jnp.sum(numer_parts * rescale[..., None], axis=0)
    own_queries = queries.reshape(own_rows, kv_local, group_size, head_dim)
    suffix_len = suffix_keys.shape[2]
    suffix_block = min(128, suffix_len)
    block_total = (jnp.max(lengths) + suffix_block - 1) // suffix_block

    def suffix_step(block_index, state_carry):
        first_key = block_index * suffix_block
        key_block = lax.dynamic_slice_in_dim(suffix_keys, first_key, suffix_block, 2)
        value_block = lax.dynamic_slice_in_dim(suffix_values, first_key, suffix_block, 2)
        scores = (
            jnp.einsum(
                "skgd,sknd->skgn", own_queries, key_block, preferred_element_type=jnp.float32
            )
            * score_scale
        )
        position = first_key + jnp.arange(suffix_block, dtype=jnp.int32)
        live_mask = position[None, :] < lengths[:, None]
        scores = jnp.where(live_mask[:, None, None, :], scores, -1e30)
        return online_update(state_carry, scores, value_block, "skgn,sknd->skgd")

    final_state = lax.fori_loop(0, block_total, suffix_step, (row_top, merged_sum, merged_numer))
    attended = (final_state[2] / final_state[1][..., None]).astype(jnp.bfloat16)
    attended = attended.reshape(own_rows, kv_local * group_size * head_dim)
    partial_out = jnp.dot(
        lax.all_gather(attended, ("ctx", "sess"), axis=0, tiled=True),
        out_weight,
        preferred_element_type=jnp.float32,
    )
    return lax.psum_scatter(partial_out, "head", scatter_dimension=0, tiled=True)


def solution(mesh):
    return jax.shard_map(
        per_device,
        mesh=mesh,
        in_specs=(
            P(("ctx", "sess"), "head", None),
            P("head", "ctx", None),
            P("head", "ctx", None),
            P(("ctx", "sess"), "head", None, None),
            P(("ctx", "sess"), "head", None, None),
            P(("ctx", "sess")),
            P("head", ("ctx", "sess")),
        ),
        out_specs=P("head", ("ctx", "sess")),
        check_vma=False,
    )
```

profile of v0, /device:TPU:1, one launch (start us, length us, event | category | flops | bytes accessed | tf_op | source)
XLA Modules:
  0.0 490.1 jit_solution(15948177267286865824)
XLA Ops:
  6.5 23.6 %all_gather.6 = bf16[64,16,128]{2,1,0:T(8,128)(2,1)S(1)} all-gather(bf16[8,16,128]{2,1,0:T(8,128)(2,1)} %param.11), channel_id=1, replica_groups=mesh['ctx'=8,'head'=4,'sess'=8] {'ctx'}, dimensions={0}, use_global_device_ids=true | all-gather | bytes 294912 | tf_op jit(solution)/shard_map/all_gather | solution.py:29
  30.2 63.2 %while.30 = (s32[]{:T(128)}, f32[64,2,8]{0,2,1:T(8,128)S(1)}, f32[64,2,8]{0,2,1:T(8,128)S(1)}, f32[64,2,8,128]{3,0,2,1:T(8,128)S(1)}, s32[12]{0:T(128)S(1)}, /*i...) while((s32[]{:T(128)}, f32[64,2,8]{0,2,1:T(8,128)S(1)}, ...), condition=%wide.region_3.4_spmd.clone, body=%wide.region_0.3_spmd.clone.sunk | while | flops 273028096 | bytes 8192195 | solution.py:50
  30.2 0.7 dynamic_slice.44
  31.6 1.5 bitcast_reduce_fusion.2
  33.1 0.6 fusion.53
  33.7 1.8 fusion.55
  35.5 0.7 dynamic_slice.44
  36.9 1.5 bitcast_reduce_fusion.2
  38.4 0.6 fusion.53
  39.0 1.8 fusion.55
  40.8 0.7 dynamic_slice.44
  42.1 1.5 bitcast_reduce_fusion.2
  43.6 0.6 fusion.53
  44.3 1.8 fusion.55
  46.0 0.7 dynamic_slice.44
  47.4 1.5 bitcast_reduce_fusion.2
  48.9 0.6 fusion.53
  49.5 1.8 fusion.55
  51.3 0.7 dynamic_slice.44
  52.7 1.5 bitcast_reduce_fusion.2
  54.2 0.6 fusion.53
  54.8 1.8 fusion.55
  56.6 0.7 dynamic_slice.44
  57.9 1.5 bitcast_reduce_fusion.2
  60.1 1.8 fusion.55
  61.8 0.7 dynamic_slice.44
  63.2 1.5 bitcast_reduce_fusion.2
  64.7 0.6 fusion.53
  65.3 1.8 fusion.55
  67.1 0.7 dynamic_slice.44
  68.5 1.5 bitcast_reduce_fusion.2
  70.0 0.6 fusion.53
  70.6 1.8 fusion.55
  72.4 0.7 dynamic_slice.44
  73.7 1.5 bitcast_reduce_fusion.2
  75.2 0.6 fusion.53
  75.8 1.8 fusion.55
  77.6 0.7 dynamic_slice.44
  79.0 1.5 bitcast_reduce_fusion.2
  80.5 0.6 fusion.53
  81.1 1.8 fusion.55
  82.9 0.7 dynamic_slice.44
  84.3 1.5 bitcast_reduce_fusion.2
  86.4 1.8 fusion.55
  88.2 0.7 dynamic_slice.44
  89.5 1.5 bitcast_reduce_fusion.2
  91.6 1.8 fusion.55
  93.6 0.7 reshape.67
  94.3 4.6 all-to-all-start
  99.0 0.7 reshape.69
  99.7 5.6 %all-to-all-done = f32[8,1,128]{2,1,0:T(1,128)S(1)} async-done(((f32[8,1,128]{2,1,0:T(1,128)}), f32[8,1,128]{2,1,0:T(1,128)S(1)}, u32[]{:S(2)}, u32[]{:S(2)}) %all-to-all-start) | async-done | bytes 4128 | tf_op jit(solution)/shard_map/all_to_all | solution.py:55
  105.3 3.3 all-to-all-start.1
  108.7 1.1 copy.16
  109.8 5.3 %all-to-all-done.1 = f32[8,1,128]{2,1,0:T(1,128)S(1)} async-done(((f32[8,1,128]{2,1,0:T(1,128)}), f32[8,1,128]{2,1,0:T(1,128)S(1)}, u32[]{:S(2)}, u32[]{:S(2)}) %all-to-all-start.1) | async-done | bytes 4128 | tf_op jit(solution)/shard_map/all_to_all | solution.py:56
  115.1 3.5 all-to-all-start.2
  118.7 0.6 reduce_max.37
  122.4 8.3 %all-to-all-done.2 = f32[64,2,8,128]{3,2,1,0:T(8,128)S(1)} async-done(((f32[64,2,8,128]{3,2,1,0:T(8,128)}), f32[64,2,8,128]{3,2,1,0:T(8,128)S(1)}, u32[]{:S(2)}, u32[]{:S(2)}) %all-to-all-start.2) | async-done | bytes 524320 | tf_op jit(solution)/shard_map/all_to_all | solution.py:57
  130.9 3.2 while.29
  131.0 1.5 fusion.48
  132.7 1.4 convolution_add_fusion.2
  134.2 0.6 copy.29
  134.9 270.8 %all-gather.2.cloned.1.call-done = bf16[512,2048]{1,0:T(8,128)(2,1)} async-done(((bf16[8,2048]{1,0:T(8,128)(2,1)}), bf16[512,2048]{1,0:T(8,128)(2,1)}) %all-gather.2.cloned.1.call-update) | async-done | bytes 2097168 | tf_op jit(solution)/shard_map/all_gather | solution.py:91
  405.7 3.0 fusion.29
  408.8 74.5 %reduce-scatter.2.cloned.1.call-done = f32[128,128]{1,0:T(8,128)} async-done(((f32[512,128]{1,0:T(8,128)}), f32[128,128]{1,0:T(8,128)}) %reduce-scatter.2.cloned.1.call-update) | async-done | bytes 65552 | tf_op jit(solution)/shard_map/reduce_scatter | solution.py:95
  (76 shorter events, 5.4 us)
Async XLA Ops:
  6.5 399.2 %copy-start = (bf16[2048,128]{1,0:T(8,128)(2,1)S(1)}, bf16[2048,128]{1,0:T(8,128)(2,1)}, u32[]{:S(2)}) copy-start(bf16[2048,128]{1,0:T(8,128)(2,1)} %param.17) | copy-start | bytes 1572868
  93.4 25.2 %copy-start.2 = (s32[8]{0:T(128)S(1)}, s32[8]{0:T(128)}, u32[]{:S(2)}) copy-start(s32[8]{0:T(128)} %param.16) | copy-start | bytes 100
  93.4 37.5 %copy-start.1 = (bf16[8,16,128]{2,1,0:T(8,128)(2,1)S(1)}, bf16[8,16,128]{2,1,0:T(8,128)(2,1)}, u32[]{:S(2)}) copy-start(bf16[8,16,128]{2,1,0:T(8,128)(2,1)} %param.11) | copy-start | bytes 98308
  94.3 11.0 %all-to-all-start = ((f32[8,1,128]{2,1,0:T(1,128)}), f32[8,1,128]{2,1,0:T(1,128)S(1)}, u32[]{:S(2)}, u32[]{:S(2)}) async-start(f32[8,1,128]{2,1,0:T(1,128)} %reshape.67), calls=%async_computation | async-start | bytes 8192 | tf_op jit(solution)/shard_map/all_to_all | solution.py:55
  105.3 9.8 %all-to-all-start.1 = ((f32[8,1,128]{2,1,0:T(1,128)}), f32[8,1,128]{2,1,0:T(1,128)S(1)}, u32[]{:S(2)}, u32[]{:S(2)}) async-start(f32[8,1,128]{2,1,0:T(1,128)} %reshape.69), calls=%async_computation.1 | async-start | bytes 8192 | tf_op jit(solution)/shard_map/all_to_all | solution.py:56
  115.1 15.6 %all-to-all-start.2 = ((f32[64,2,8,128]{3,2,1,0:T(8,128)}), f32[64,2,8,128]{3,2,1,0:T(8,128)S(1)}, u32[]{:S(2)}, u32[]{:S(2)}) async-start(f32[64,2,8,128]{3,2,1,0:T(8,128)} %copy.16), calls=%async_computation.2 | async-start | bytes 1048576 | tf_op jit(solution)/shard_map/all_to_all | solution.py:57
  118.6 287.1 %all-gather.2.cloned.1.call-start = ((), (), s32[]{:S(2)}) async-start(), calls=%async_computation.4 | async-start | bytes 2129920 | tf_op jit(solution)/shard_map/all_gather | solution.py:91
  134.9 348.4 %reduce-scatter.2.cloned.1.call-start = ((), (), s32[]{:S(2)}) async-start(), calls=%async_computation.5 | async-start | bytes 327680 | tf_op jit(solution)/shard_map/reduce_scatter | solution.py:95
Sparse Core Ops, SparseCore 0:
  135.0 270.6 all-gather.1
  408.9 74.3 reduce-scatter.1
where the time goes:
time: 492 us; the launch traced here: 490 us
  waiting for transfers between devices  365 us (74%)
  matrix products  44.6 us (9%)
  blocking collectives  23.6 us (5%)
  between operations  14.2 us (3%)
  local copies, waits for them, and re-layouts  12.7 us (3%)
  starting transfers between devices  11.5 us (2%)
  other arithmetic  9.81 us (2%)
  loops' own time  9.15 us (2%)
    all_gather x1, waiting for transfers between devices, per_device(): lax.all_gather(attended, ('ctx', 'sess'), axis=0, tiled=True)  271 us
    reduce_scatter x1, waiting for transfers between devices, per_device(): lax.psum_scatter(partial_out, 'head', scatter_dimension=0, tiled=True)  74.5 us
    all_gather x1, blocking collectives, per_device(): gathered = lax.all_gather(queries, 'ctx', axis=0, tiled=True)  23.6 us
    dot_general x13, matrix products, online_update(): jnp.einsum(einsum_form, weights.astype(jnp.bfloat16), values, preferred_e...  22.4 us
    dot_general x12, matrix products, prefix_step(): jnp.einsum('rkgd,knd->rkgn', grouped, key_block, preferred_element_type=j...  17.7 us
  transfers between devices with their start and end apart: 5, of which 5 were waited for; matrix products, arithmetic and copies ran while one was open for 1% of the time, Pallas kernels for 0%

commit v1 on v0

v1 whole, which is shorter than its diff:
```python
import functools
import math

import jax
import jax.numpy as jnp
from jax import lax
from jax.experimental import pallas as pl
from jax.experimental.pallas import tpu as pltpu
from jax.sharding import Mesh
from jax.sharding import PartitionSpec as P

F32 = jnp.float32
BF16 = jnp.bfloat16
LOG2E = 1.4426950408889634
HEAD = ("yh", "core")
SESS = ("yl", "x")
NT = (((1,), (1,)), ((), ()))


def prefix_kernel(scale, q_ref, k_ref, v_ref, o_ref, m_ref, l_ref, acc_ref, lse_ref):
    head, block = pl.program_id(0), pl.program_id(1)
    last = pl.num_programs(1) - 1
    sources, heads, rows, dim = q_ref.shape

    @pl.when(block == 0)
    def _():
        m_ref[...] = jnp.full_like(m_ref, -1e30)
        l_ref[...] = jnp.zeros_like(l_ref)
        acc_ref[...] = jnp.zeros_like(acc_ref)

    chunk = 2
    k = k_ref[0]
    v = v_ref[0]
    for first in range(0, sources, chunk):
        span = pl.ds(first * rows, chunk * rows)
        q = q_ref[pl.ds(first, chunk), head].reshape(chunk * rows, dim)
        scores = lax.dot_general(q, k, NT, preferred_element_type=F32)
        old = m_ref[span, 0:1]
        new = jnp.maximum(old, jnp.max(scores, axis=1, keepdims=True))
        factor = jnp.exp2((old - new) * scale)
        weights = jnp.exp2((scores - new) * scale)
        l_ref[span, 0:1] = l_ref[span, 0:1] * factor + jnp.sum(weights, axis=1, keepdims=True)
        m_ref[span, 0:1] = new
        acc_ref[span, :] = acc_ref[span, :] * factor + jnp.dot(
            weights.astype(BF16), v, preferred_element_type=F32
        )

    @pl.when(block == last)
    def _():
        total = l_ref[:, 0:1]
        out = (acc_ref[...] / total).astype(BF16)
        lse = m_ref[:, 0:1] * scale + jnp.log2(total)
        lse_ref[head] = jnp.broadcast_to(lse, lse_ref.shape[1:])
        for c in range(sources):
            o_ref[c, pl.ds(head * rows, rows), :] = out[c * rows : (c + 1) * rows]

    @pl.when(jnp.logical_and(block == last, head == heads - 1))
    def _():
        for c in range(sources):
            column = jnp.concatenate(
                [lse_ref[h, c * rows : (c + 1) * rows, :] for h in range(heads)], axis=0
            )
            row = column.T[0:8]
            high = row.astype(BF16).astype(F32)
            middle = (row - high).astype(BF16).astype(F32)
            low = row - high - middle
            place = lax.broadcasted_iota(jnp.int32, row.shape, 0)
            stats = jnp.where(place == 0, high, jnp.where(place == 1, middle, low))
            o_ref[c, pl.ds(heads * rows, 8), :] = stats.astype(BF16)


def prefix_attention(q, keys, values, scale):
    sources, heads, rows, dim = q.shape
    length = keys.shape[1]
    block = 1024 if length % 1024 == 0 else length
    total_rows = sources * rows
    return pl.pallas_call(
        functools.partial(prefix_kernel, scale),
        grid=(heads, length // block),
        in_specs=[
            pl.BlockSpec(q.shape, lambda h, b: (0, 0, 0, 0)),
            pl.BlockSpec((1, block, dim), lambda h, b: (h, b, 0)),
            pl.BlockSpec((1, block, dim), lambda h, b: (h, b, 0)),
        ],
        out_specs=pl.BlockSpec((sources, heads * rows + 8, dim), lambda h, b: (0, 0, 0)),
        out_shape=jax.ShapeDtypeStruct((sources, heads * rows + 8, dim), BF16),
        scratch_shapes=[
            pltpu.VMEM((total_rows, 128), F32),
            pltpu.VMEM((total_rows, 128), F32),
            pltpu.VMEM((total_rows, dim), F32),
            pltpu.VMEM((heads, total_rows, 128), F32),
        ],
        compiler_params=pltpu.CompilerParams(
            dimension_semantics=("arbitrary", "arbitrary"), vmem_limit_bytes=32 << 20
        ),
        cost_estimate=pl.CostEstimate(
            flops=4 * heads * total_rows * length * dim,
            bytes_accessed=4 * heads * length * dim,
            transcendentals=heads * total_rows * length,
        ),
        name="prefix_attention",
    )(q, keys, values)


def suffix_kernel(scale, lengths_ref, q_ref, k_ref, v_ref, o_ref, lse_ref):
    session = pl.program_id(0)
    heads, length = k_ref.shape[1], k_ref.shape[2]
    group = q_ref.shape[1] // heads
    sessions = pl.num_programs(0)
    live = lengths_ref[session]
    for h in range(heads):
        q = q_ref[0, h * group : (h + 1) * group]
        scores = lax.dot_general(q, k_ref[0, h], NT, preferred_element_type=F32)
        position = lax.broadcasted_iota(jnp.int32, scores.shape, 1)
        scores = jnp.where(position < live, scores, -1e30)
        top = jnp.max(scores, axis=1, keepdims=True)
        weights = jnp.exp2((scores - top) * scale)
        total = jnp.sum(weights, axis=1, keepdims=True)
        out = jnp.dot(weights.astype(BF16), v_ref[0, h], preferred_element_type=F32) / total
        rows = pl.ds(h * group * o_ref.shape[0] // (heads * group) + session, group, stride=8)
        o_ref[rows, :] = out
        lse_ref[rows, :] = jnp.broadcast_to(top * scale + jnp.log2(total), out.shape)


def suffix_attention(q, keys, values, lengths, scale):
    sessions, heads, length, dim = keys.shape
    rows = q.shape[1] * sessions
    spec = pl.BlockSpec((rows, dim), lambda s, n: (0, 0))
    return pl.pallas_call(
        functools.partial(suffix_kernel, scale),
        grid_spec=pltpu.PrefetchScalarGridSpec(
            num_scalar_prefetch=1,
            grid=(sessions,),
            in_specs=[
                pl.BlockSpec((1,) + q.shape[1:], lambda s, n: (s, 0, 0)),
                pl.BlockSpec((1, heads, length, dim), lambda s, n: (s, 0, 0, 0)),
                pl.BlockSpec((1, heads, length, dim), lambda s, n: (s, 0, 0, 0)),
            ],
            out_specs=[spec, spec],
        ),
        out_shape=[jax.ShapeDtypeStruct((rows, dim), F32)] * 2,
        compiler_params=pltpu.CompilerParams(vmem_limit_bytes=16 << 20),
        cost_estimate=pl.CostEstimate(
            flops=4 * rows * length * dim,
            bytes_accessed=4 * sessions * heads * length * dim,
            transcendentals=rows * length,
        ),
        name="suffix_attention",
    )(lengths, q, keys, values)


def merge_kernel(parts_ref, suffix_ref, suffix_lse_ref, out_ref):
    sources, padded, dim = parts_ref.shape
    rows = padded - 8
    sessions = out_ref.shape[0]
    stats = []
    for c in range(sources):
        three = parts_ref[c, rows : rows + 8, :].astype(F32)
        stats.append(three[0:1] + three[1:2] + three[2:3])
    filler = jnp.full((rows - sources, rows), -3e38, F32)
    table = jnp.concatenate(stats + [filler], axis=0).T
    own = suffix_lse_ref[...]
    top = jnp.maximum(jnp.max(table, axis=1, keepdims=True), own[:, 0:1])
    shares = jnp.exp2(table - top)
    own_share = jnp.exp2(own[:, 0:1] - top)
    total = jnp.sum(shares, axis=1, keepdims=True) + own_share
    result = own_share * suffix_ref[...]
    for c in range(sources):
        result += shares[:, c : c + 1] * parts_ref[c, 0:rows, :].astype(F32)
    result = result / total
    for h in range(rows // sessions):
        out_ref[:, h * dim : (h + 1) * dim] = result[h * sessions : (h + 1) * sessions].astype(BF16)


def merge(parts, suffix, suffix_lse, sessions):
    rows, dim = suffix.shape
    return pl.pallas_call(
        merge_kernel,
        out_shape=jax.ShapeDtypeStruct((sessions, rows // sessions * dim), BF16),
        name="merge_shards",
    )(parts, suffix, suffix_lse)


def project_kernel(attended_ref, *refs):
    weights, out_ref = refs[:-1], refs[-1]
    heads, _, rows, _ = out_ref.shape
    for x, weight_ref in enumerate(weights):
        product = jnp.dot(attended_ref[...], weight_ref[...], preferred_element_type=F32)
        for h in range(heads):
            out_ref[h, x] = product[h * rows : (h + 1) * rows].astype(BF16)


def project(attended, weights, heads):
    sessions, features = attended.shape
    columns = weights[0].shape[1]
    return pl.pallas_call(
        project_kernel,
        out_shape=jax.ShapeDtypeStruct((heads, len(weights), sessions // heads, columns), BF16),
        compiler_params=pltpu.CompilerParams(vmem_limit_bytes=32 << 20),
        name="project",
    )(attended, *weights)


def finish_kernel(parts_ref, out_ref):
    for x in range(parts_ref.shape[1]):
        total = parts_ref[0, x].astype(F32)
        for h in range(1, parts_ref.shape[0]):
            total += parts_ref[h, x].astype(F32)
        out_ref[:, x] = total


def finish(parts):
    _, x, outer, sessions, columns = parts.shape
    return pl.pallas_call(
        finish_kernel,
        out_shape=jax.ShapeDtypeStruct((outer, x, sessions, columns), F32),
        name="sum_heads",
    )(parts)


def per_device(queries, prefix_keys, prefix_values, suffix_keys, suffix_values, lengths, out_weight):
    sessions, local_heads, dim = queries.shape
    kv_local = prefix_keys.shape[0]
    rows = local_heads // kv_local * sessions
    scale = LOG2E / math.sqrt(dim)
    ctx = lax.axis_size("ctx")
    heads = lax.axis_size("yh") * lax.axis_size("core")
    wide = lax.axis_size("x")
    low = lax.axis_size("yl")

    arranged = queries.transpose(1, 0, 2).reshape(1, kv_local, rows, dim)
    spread = jnp.broadcast_to(arranged, (ctx, kv_local, rows, dim))
    gathered = lax.all_to_all(spread, "ctx", 0, 0, tiled=True)
    weight_spread = jnp.broadcast_to(out_weight[None], (wide,) + out_weight.shape)
    weight_all = lax.all_to_all(weight_spread, "x", 0, 0, tiled=True)

    suffix, suffix_lse = suffix_attention(queries, suffix_keys, suffix_values, lengths, scale)
    parts = prefix_attention(gathered, prefix_keys, prefix_values, scale)
    parts = lax.all_to_all(parts, "ctx", 0, 0, tiled=True)
    attended = merge(parts, suffix, suffix_lse, sessions)

    group = ctx * low
    everyone = jnp.broadcast_to(attended[None], (group,) + attended.shape)
    everyone = lax.all_to_all(everyone, ("ctx", "yl"), 0, 0, tiled=True)
    everyone = everyone.reshape(group * sessions, attended.shape[1])
    partial_out = project(everyone, [weight_all[x] for x in range(wide)], heads)
    partial_out = partial_out.reshape(heads * wide, group * sessions // heads, out_weight.shape[1])
    partial_out = lax.all_to_all(partial_out, ("yh", "core", "x"), 0, 0, tiled=True)
    partial_out = partial_out.reshape(heads, wide, group // heads, sessions, out_weight.shape[1])
    return finish(partial_out).reshape(group * sessions * wide // heads, out_weight.shape[1])


def solution(mesh):
    fine = Mesh(mesh.devices.reshape(8, 2, 2, 2, 4), ("ctx", "yh", "core", "yl", "x"))
    both = ("ctx",) + SESS
    return jax.shard_map(
        per_device,
        mesh=fine,
        in_specs=(
            P(both, HEAD, None),
            P(HEAD, "ctx", None),
            P(HEAD, "ctx", None),
            P(both, HEAD, None, None),
            P(both, HEAD, None, None),
            P(both),
            P(HEAD, both),
        ),
        out_specs=P(HEAD, both),
        check_vma=False,
    )
```

time: 492 us -> 127 us (0.26)
  waiting for transfers between devices: 365 us -> 22.5 us
  matrix products: 44.6 us -> 0 us
  Pallas kernels: 0 us -> 32.9 us
  blocking collectives: 23.6 us -> 50.6 us
  between operations: 14.2 us -> 0.09 us
  other arithmetic: 9.81 us -> 0 us
  loops' own time: 9.15 us -> 0 us
    all_gather x1 -> x0, waiting for transfers between devices: 271 us -> none  [per_device(): lax.all_gather(attended, ('ctx', 'sess'), axis=0, tiled=True)]
    reduce_scatter x1 -> x0, waiting for transfers between devices: 74.5 us -> none  [per_device(): lax.psum_scatter(partial_out, 'head', scatter_dimension=0, tiled=True)]
    all_to_all x0 -> x3, blocking collectives: none -> 50.6 us  [the longest x1 19.2 us: per_device(): gathered = lax.all_to_all(spread, 'ctx', 0, 0, tiled=True)]
    dot_general x27 -> x0, matrix products: 44.6 us -> none  [the longest x13 22.4 us: online_update(): jnp.einsum(einsum_form, weights.astype(jnp.bfloat16), values, preferred_e...]
    pallas_call x0 -> x5, Pallas kernels: none -> 32.9 us  [the longest x1 23 us: prefix_attention(): pl.pallas_call(functools.partial(prefix_kernel, scale), grid=(heads, leng...]
    all_gather x1 -> x0, blocking collectives: 23.6 us -> none  [per_device(): gathered = lax.all_gather(queries, 'ctx', axis=0, tiled=True)]
    another operation x2 -> x0, loops' own time: 9.15 us -> none  [the longest x1 9.1 us: per_device(): lax.scan(prefix_step, start_state, jnp.arange(prefix_len // key_block_len...]
    dynamic_slice x12 -> x0, local copies, waits for them, and re-layouts: 8 us -> none  [per_device(): lax.scan(prefix_step, start_state, jnp.arange(prefix_len // key_block_len...]
  transfers between devices with their start and end apart: 5 -> 2, of which waited for: 5 -> 2; matrix products, arithmetic and copies ran while one was open for 1% -> 1% of each run, Pallas kernels for 0% -> 6%
where the time goes in v1:
time: 127 us
  blocking collectives  50.6 us (40%)
  Pallas kernels  32.9 us (26%)
  waiting for transfers between devices  22.5 us (18%)
  local copies, waits for them, and re-layouts  12.3 us (10%)
  starting transfers between devices  8.14 us (6%)
    pallas_call x1, Pallas kernels, prefix_attention(): pl.pallas_call(functools.partial(prefix_kernel, scale), grid=(heads, leng...  23 us
    all_to_all x1, blocking collectives, per_device(): gathered = lax.all_to_all(spread, 'ctx', 0, 0, tiled=True)  19.2 us
    all_to_all x1, blocking collectives, per_device(): lax.all_to_all(partial_out, ('yh', 'core', 'x'), 0, 0, tiled=True)  18.8 us
    all_to_all x1, blocking collectives, per_device(): parts = lax.all_to_all(parts, 'ctx', 0, 0, tiled=True)  12.6 us
    all_to_all x1, waiting for transfers between devices, per_device(): weight_all = lax.all_to_all(weight_spread, 'x', 0, 0, tiled=True)  12.2 us
    all_to_all x1, waiting for transfers between devices, per_device(): everyone = lax.all_to_all(everyone, ('ctx', 'yl'), 0, 0, tiled=True)  10.2 us
    unnamed x19, local copies, waits for them, and re-layouts  7.41 us
    pallas_call x1, Pallas kernels, suffix_attention(): pl.pallas_call(functools.partial(suffix_kernel, scale), grid_spec=pltpu.P...  5.29 us
  transfers between devices with their start and end apart: 2, of which 2 were waited for; matrix products, arithmetic and copies ran while one was open for 1% of the time, Pallas kernels for 6%

profile of v1, /device:TPU:1, one launch (start us, length us, event | category | flops | bytes accessed | tf_op | source)
XLA Modules:
  0.0 126.5 jit_solution(3922333431409476172)
XLA Ops:
  0.0 0.8 copy.8
  0.8 19.2 %all_to_all.25.q_ref = bf16[8,2,64,128]{3,2,1,0:T(8,128)(2,1)S(1)} all-to-all(bf16[8,2,64,128]{3,2,1,0:T(8,128)(2,1)S(1)} %broadcast_in_dim.9), channel_id=1, replica_groups=mesh['ctx'=8,'yh'=2,'core'=2,'yl'=2,'x'=4] {'ctx'}, dimensions={0} | all-to-all | bytes 524288 | tf_op jit(solution)/shard_map/all_to_all | solution.py:233
  20.0 0.0 copy-start.6
  20.0 1.9 %copy-done.6 = bf16[2,6144,128]{2,1,0:T(8,128)(2,1)S(1)} copy-done((bf16[2,6144,128]{2,1,0:T(8,128)(2,1)S(1)}, bf16[2,6144,128]{2,1,0:T(8,128)(2,1)}, u32[]{:S(2)}) %copy-start.6) | copy-done | bytes 3145752
  21.9 0.0 copy-start.7
  21.9 1.9 %copy-done.7 = bf16[2,6144,128]{2,1,0:T(8,128)(2,1)S(1)} copy-done((bf16[2,6144,128]{2,1,0:T(8,128)(2,1)S(1)}, bf16[2,6144,128]{2,1,0:T(8,128)(2,1)}, u32[]{:S(2)}) %copy-start.7) | copy-done | bytes 3145752
  23.8 0.0 copy-start.8
  23.8 23.0 %prefix_attention.1 = bf16[8,136,128]{2,1,0:T(8,128)(2,1)S(1)} custom-call(bf16[8,2,64,128]{3,2,1,0:T(8,128)(2,1)S(1)} %all_to_all.25.q_ref, bf16[2,6144,128]{2,1,0:T(8,128)(2,1)S(1)} %copy-done.6, bf16[2,6144,128]{2,1,0:T(8,128)(2,1)S(1)} %copy-done.7), custom_call_target="tpu_custom_call" | custom-call | flops 3221225472 | bytes 6291456 | tf_op jit(solution)/shard_map/prefix_attention/pallas_call | solution.py:77
  46.8 12.6 %all_to_all.26.parts_ref = bf16[8,136,128]{2,1,0:T(8,128)(2,1)} all-to-all(bf16[8,136,128]{2,1,0:T(8,128)(2,1)S(1)} %prefix_attention.1), channel_id=1, replica_groups=mesh['ctx'=8,'yh'=2,'core'=2,'yl'=2,'x'=4] {'ctx'}, dimensions={0} | all-to-all | bytes 557056 | tf_op jit(solution)/shard_map/all_to_all | solution.py:239
  59.4 0.0 copy-done.8
  59.4 1.6 %broadcast_in_dim.22 = bf16[4,2048,128]{2,1,0:T(8,128)(2,1)} broadcast(bf16[2048,128]{1,0:T(8,128)(2,1)S(1)} %copy-done.8), dimensions={1,2} | broadcast | bytes 2621440 | tf_op jit(solution)/shard_map/broadcast_in_dim | solution.py:234
  61.0 0.0 copy-start
  61.0 0.0 copy-start.2
  61.0 0.0 copy-start.5
  61.0 4.6 %all-to-all-start.3 = ((bf16[4,2048,128]{2,1,0:T(8,128)(2,1)}), bf16[4,2048,128]{2,1,0:T(8,128)(2,1)}, u32[]{:S(2)}, u32[]{:S(2)}) async-start(bf16[4,2048,128]{2,1,0:T(8,128)(2,1)} %broadcast_in_dim.22), calls=%async_computation.3 | async-start | bytes 4194304 | tf_op jit(solution)/shard_map/all_to_all | solution.py:235
  65.6 0.0 copy-done
  65.6 0.0 copy-done.2
  65.6 0.0 copy-done.5
  65.6 0.0 copy-start.1
  65.7 1.6 %copy-done.1 = bf16[8,2,512,128]{3,2,1,0:T(8,128)(2,1)S(1)} copy-done((bf16[8,2,512,128]{3,2,1,0:T(8,128)(2,1)S(1)}, bf16[8,2,512,128]{3,2,1,0:T(8,128)(2,1)}, u32[]{:S(2)}) %copy-start.1) | copy-done | bytes 2097176
  67.2 5.3 %suffix_attention.1 = (f32[128,128]{1,0:T(8,128)S(1)}, f32[128,128]{1,0:T(8,128)S(1)}) custom-call(s32[8]{0:T(128)S(1)} %copy-done.5, bf16[8,16,128]{2,1,0:T(8,128)(2,1)S(1)} %copy-done.2, bf16[8,2,512,128]{3,2,1,0:T(8,128)(2,1)S(1)} %copy-done, bf16[8,2,512,128]{3,2,1,0:T(8,128)(2,1)S(1)} %copy-done.1), custom_call_target="tpu_custom_call" | custom-call | flops 33554432 | bytes 4194304 | tf_op jit(solution)/shard_map/suffix_attention/pallas_call | solution.py:129
  72.5 0.0 copy-start.3
  72.5 0.6 copy-done.3
  73.2 0.0 copy-start.4
  73.2 0.6 copy-done.4
  73.8 2.4 %merge_shards.1 = bf16[8,2048]{1,0:T(8,128)(2,1)} custom-call(bf16[8,136,128]{2,1,0:T(8,128)(2,1)} %all_to_all.26.parts_ref, f32[128,128]{1,0:T(8,128)} %copy-done.3, f32[128,128]{1,0:T(8,128)} %copy-done.4), custom_call_target="tpu_custom_call" | custom-call | tf_op jit(solution)/shard_map/merge_shards/pallas_call | solution.py:177
  76.1 12.2 %all-to-all-done.3 = bf16[4,2048,128]{2,1,0:T(8,128)(2,1)} async-done(((bf16[4,2048,128]{2,1,0:T(8,128)(2,1)}), bf16[4,2048,128]{2,1,0:T(8,128)(2,1)}, u32[]{:S(2)}, u32[]{:S(2)}) %all-to-all-start.3) | async-done | bytes 2097184 | tf_op jit(solution)/shard_map/all_to_all | solution.py:235
  88.4 1.6 %broadcast_in_dim.10 = bf16[16,8,2048]{2,1,0:T(8,128)(2,1)} broadcast(bf16[8,2048]{1,0:T(8,128)(2,1)} %merge_shards.1), dimensions={1,2} | broadcast | bytes 557056 | tf_op jit(solution)/shard_map/broadcast_in_dim | solution.py:243
  90.0 3.6 %all-to-all-start.2 = ((bf16[16,8,2048]{2,1,0:T(8,128)(2,1)}), bf16[16,8,2048]{2,1,0:T(8,128)(2,1)S(1)}, u32[]{:S(2)}, u32[]{:S(2)}) async-start(bf16[16,8,2048]{2,1,0:T(8,128)(2,1)} %broadcast_in_dim.10), calls=%async_computation.2 | async-start | bytes 1048576 | tf_op jit(solution)/shard_map/all_to_all | solution.py:244
  93.6 1.7 %slice_bitcast_fusion = (bf16[2048,128]{1,0:T(8,128)(2,1)S(1)}, bf16[2048,128]{1,0:T(8,128)(2,1)S(1)}, bf16[2048,128]{1,0:T(8,128)(2,1)S(1)}, bf16[2048,128]{1,0:T(8,128)(2,1)S(1)}) fusion(bf16[4,2048,128]{2,1,0:T(8,128)(2,1)} %all-to-all-done.3), kind=kLoop, calls=%fused_computation | loop fusion | bytes 4194304 | tf_op jit(solution)/shard_map/squeeze | solution.py:246
  95.2 10.2 %all-to-all-done.2 = bf16[16,8,2048]{2,1,0:T(8,128)(2,1)S(1)} async-done(((bf16[16,8,2048]{2,1,0:T(8,128)(2,1)}), bf16[16,8,2048]{2,1,0:T(8,128)(2,1)S(1)}, u32[]{:S(2)}, u32[]{:S(2)}) %all-to-all-start.2) | async-done | bytes 524320 | tf_op jit(solution)/shard_map/all_to_all | solution.py:244
  105.5 0.7 project.1
  106.2 18.8 %all_to_all.27 = bf16[16,32,128]{2,1,0:T(8,128)(2,1)} all-to-all(bf16[16,32,128]{2,1,0:T(8,128)(2,1)S(1)} %bitcast.16), channel_id=1, replica_groups=mesh['ctx'=8,'yh'=2,'core'=2,'yl'=2,'x'=4] {'yh','core','x'}, dimensions={0} | all-to-all | bytes 262144 | tf_op jit(solution)/shard_map/all_to_all | solution.py:248
  125.0 1.6 %sum_heads.1 = f32[4,4,8,128]{3,2,1,0:T(8,128)} custom-call(bf16[4,4,4,8,128]{4,3,2,1,0:T(8,128)(2,1)} %bitcast.17), custom_call_target="tpu_custom_call" | custom-call | tf_op jit(solution)/shard_map/sum_heads/pallas_call | solution.py:214
  (1 shorter events, 0.0 us)
Async XLA Ops:
  20.0 1.9 %copy-start.6 = (bf16[2,6144,128]{2,1,0:T(8,128)(2,1)S(1)}, bf16[2,6144,128]{2,1,0:T(8,128)(2,1)}, u32[]{:S(2)}) copy-start(bf16[2,6144,128]{2,1,0:T(8,128)(2,1)} %k_ref.2) | copy-start | bytes 9437188
  21.9 1.9 %copy-start.7 = (bf16[2,6144,128]{2,1,0:T(8,128)(2,1)S(1)}, bf16[2,6144,128]{2,1,0:T(8,128)(2,1)}, u32[]{:S(2)}) copy-start(bf16[2,6144,128]{2,1,0:T(8,128)(2,1)} %v_ref.2) | copy-start | bytes 9437188
  23.8 35.6 %copy-start.8 = (bf16[2048,128]{1,0:T(8,128)(2,1)S(1)}, bf16[2048,128]{1,0:T(8,128)(2,1)}, u32[]{:S(2)}) copy-start(bf16[2048,128]{1,0:T(8,128)(2,1)} %param.13) | copy-start | bytes 1572868
  61.0 4.6 %copy-start = (bf16[8,2,512,128]{3,2,1,0:T(8,128)(2,1)S(1)}, bf16[8,2,512,128]{3,2,1,0:T(8,128)(2,1)}, u32[]{:S(2)}) copy-start(bf16[8,2,512,128]{3,2,1,0:T(8,128)(2,1)} %k_ref.3) | copy-start | bytes 6291460
  61.0 4.6 %copy-start.2 = (bf16[8,16,128]{2,1,0:T(8,128)(2,1)S(1)}, bf16[8,16,128]{2,1,0:T(8,128)(2,1)}, u32[]{:S(2)}) copy-start(bf16[8,16,128]{2,1,0:T(8,128)(2,1)} %q_ref.1) | copy-start | bytes 98308
  61.0 4.6 %copy-start.5 = (s32[8]{0:T(128)S(1)}, s32[8]{0:T(128)}, u32[]{:S(2)}) copy-start(s32[8]{0:T(128)} %lengths_ref.1) | copy-start | bytes 100
  61.0 27.3 %all-to-all-start.3 = ((bf16[4,2048,128]{2,1,0:T(8,128)(2,1)}), bf16[4,2048,128]{2,1,0:T(8,128)(2,1)}, u32[]{:S(2)}, u32[]{:S(2)}) async-start(bf16[4,2048,128]{2,1,0:T(8,128)(2,1)} %broadcast_in_dim.22), calls=%async_computation.3 | async-start | bytes 4194304 | tf_op jit(solution)/shard_map/all_to_all | solution.py:235
  65.6 1.6 %copy-start.1 = (bf16[8,2,512,128]{3,2,1,0:T(8,128)(2,1)S(1)}, bf16[8,2,512,128]{3,2,1,0:T(8,128)(2,1)}, u32[]{:S(2)}) copy-start(bf16[8,2,512,128]{3,2,1,0:T(8,128)(2,1)} %v_ref.3) | copy-start | bytes 6291460
  72.5 0.6 copy-start.3
  73.2 0.6 copy-start.4
  90.0 15.5 %all-to-all-start.2 = ((bf16[16,8,2048]{2,1,0:T(8,128)(2,1)}), bf16[16,8,2048]{2,1,0:T(8,128)(2,1)S(1)}, u32[]{:S(2)}, u32[]{:S(2)}) async-start(bf16[16,8,2048]{2,1,0:T(8,128)(2,1)} %broadcast_in_dim.10), calls=%async_computation.2 | async-start | bytes 1048576 | tf_op jit(solution)/shard_map/all_to_all | solution.py:244

commit v2 on v1

v2 whole, which is shorter than its diff:
```python
import functools
import math

import jax
import jax.numpy as jnp
from jax import lax
from jax.experimental import pallas as pl
from jax.experimental.pallas import tpu as pltpu
from jax.sharding import Mesh
from jax.sharding import PartitionSpec as P

F32 = jnp.float32
BF16 = jnp.bfloat16
LOG2E = 1.4426950408889634
HEAD = ("yh", "core")
SESS = ("yl", "x")
NT = (((1,), (1,)), ((), ()))


def prefix_kernel(
    scale, chunk, block, q_ref, k_hbm, v_hbm, o_ref, k_ref, v_ref, acc_ref, lse_ref, k_sem, v_sem
):
    head = pl.program_id(0)
    sources, _, rows, dim = q_ref.shape
    heads, length, _ = k_ref.shape
    tiles = [(c, k) for c in range(0, sources, chunk) for k in range(0, length, block)]

    def copy_of(source, target, sem, h, part):
        span = pl.ds(part * block, block)
        return pltpu.make_async_copy(source.at[h, span], target.at[h, span], sem.at[h, part])

    @pl.when(head == 0)
    def _():
        for h in range(heads):
            for part in range(length // block):
                copy_of(k_hbm, k_ref, k_sem, h, part).start()
                copy_of(v_hbm, v_ref, v_sem, h, part).start()

    def scores_of(tile):
        c, k = tile
        q = q_ref[c : c + chunk, 0].reshape(chunk * rows, dim)
        if c == 0:
            copy_of(k_hbm, k_ref, k_sem, head, k // block).wait()
        return lax.dot_general(q, k_ref[head, k : k + block], NT, preferred_element_type=F32)

    scores = scores_of(tiles[0])
    for index, (c, k) in enumerate(tiles):
        if c == 0:
            copy_of(v_hbm, v_ref, v_sem, head, k // block).wait()
        ahead = scores_of(tiles[index + 1]) if index + 1 < len(tiles) else None
        new = jnp.max(scores, axis=1, keepdims=True)
        if k > 0:
            new = jnp.maximum(top, new)
            factor = jnp.exp2((top - new) * scale)
        weights = jnp.exp2((scores - new) * scale)
        part = jnp.sum(weights, axis=1, keepdims=True)
        product = jnp.dot(
            weights.astype(BF16), v_ref[head, k : k + block], preferred_element_type=F32
        )
        span = slice(c * rows, (c + chunk) * rows)
        if k > 0:
            total = total * factor + part
            product = acc_ref[span] * factor + product
        else:
            total = part
        top, scores = new, ahead
        if k + block < length:
            acc_ref[span] = product
            continue
        out = (product / total).astype(BF16)
        lse = top * scale + jnp.log2(total)
        lse_ref[head, span] = jnp.broadcast_to(lse, (chunk * rows, lse_ref.shape[2]))
        for i in range(chunk):
            o_ref[c + i, pl.ds(head * rows, rows), :] = out[i * rows : (i + 1) * rows]

    @pl.when(head == heads - 1)
    def _():
        for c in range(sources):
            column = jnp.concatenate(
                [lse_ref[h, c * rows : (c + 1) * rows, :] for h in range(heads)], axis=0
            )
            row = column.T[0:8]
            high = row.astype(BF16).astype(F32)
            middle = (row - high).astype(BF16).astype(F32)
            low = row - high - middle
            place = lax.broadcasted_iota(jnp.int32, row.shape, 0)
            stats = jnp.where(place == 0, high, jnp.where(place == 1, middle, low))
            o_ref[c, pl.ds(heads * rows, 8), :] = stats.astype(BF16)


def prefix_attention(q, keys, values, scale):
    sources, heads, rows, dim = q.shape
    length = keys.shape[1]
    block = length // 2
    total_rows = sources * rows
    return pl.pallas_call(
        functools.partial(prefix_kernel, scale, 2, block),
        grid=(heads,),
        in_specs=[
            pl.BlockSpec((sources, 1, rows, dim), lambda h: (0, h, 0, 0)),
            pl.BlockSpec(memory_space=pl.ANY),
            pl.BlockSpec(memory_space=pl.ANY),
        ],
        out_specs=pl.BlockSpec((sources, heads * rows + 8, dim), lambda h: (0, 0, 0)),
        out_shape=jax.ShapeDtypeStruct((sources, heads * rows + 8, dim), BF16),
        scratch_shapes=[
            pltpu.VMEM(keys.shape, BF16),
            pltpu.VMEM(values.shape, BF16),
            pltpu.VMEM((total_rows, dim), F32),
            pltpu.VMEM((heads, total_rows, 128), F32),
            pltpu.SemaphoreType.DMA((heads, length // block)),
            pltpu.SemaphoreType.DMA((heads, length // block)),
        ],
        compiler_params=pltpu.CompilerParams(
            dimension_semantics=("arbitrary",), vmem_limit_bytes=58 << 20
        ),
        cost_estimate=pl.CostEstimate(
            flops=4 * heads * total_rows * length * dim,
            bytes_accessed=4 * heads * length * dim,
            transcendentals=heads * total_rows * length,
        ),
        name="prefix_attention",
    )(q, keys, values)


def suffix_kernel(scale, lengths_ref, q_ref, k_ref, v_ref, o_ref, lse_ref):
    step = pl.program_id(0)
    count, heads, length = k_ref.shape[0], k_ref.shape[1], k_ref.shape[2]
    group = q_ref.shape[1] // heads
    sessions = pl.num_programs(0) * count
    pairs = [(s, h) for s in range(count) for h in range(heads)]
    all_scores = [
        lax.dot_general(
            q_ref[s, h * group : (h + 1) * group], k_ref[s, h], NT, preferred_element_type=F32
        )
        for s, h in pairs
    ]
    position = lax.broadcasted_iota(jnp.int32, (group, length), 1)
    softened = []
    for (s, h), scores in zip(pairs, all_scores):
        scores = jnp.where(position < lengths_ref[step * count + s], scores, -1e30)
        top = jnp.max(scores, axis=1, keepdims=True)
        weights = jnp.exp2((scores - top) * scale)
        softened.append((top, jnp.sum(weights, axis=1, keepdims=True), weights.astype(BF16)))
    for (s, h), (top, total, weights) in zip(pairs, softened):
        out = jnp.dot(weights, v_ref[s, h], preferred_element_type=F32) / total
        rows = pl.ds(h * group * sessions + step * count + s, group, stride=sessions)
        o_ref[rows, :] = out
        lse_ref[rows, :] = jnp.broadcast_to(top * scale + jnp.log2(total), out.shape)


def suffix_attention(q, keys, values, lengths, scale):
    sessions, heads, length, dim = keys.shape
    rows = q.shape[1] * sessions
    count = 4
    spec = pl.BlockSpec((rows, dim), lambda s, n: (0, 0))
    return pl.pallas_call(
        functools.partial(suffix_kernel, scale),
        grid_spec=pltpu.PrefetchScalarGridSpec(
            num_scalar_prefetch=1,
            grid=(sessions // count,),
            in_specs=[
                pl.BlockSpec((count,) + q.shape[1:], lambda s, n: (s, 0, 0)),
                pl.BlockSpec((count, heads, length, dim), lambda s, n: (s, 0, 0, 0)),
                pl.BlockSpec((count, heads, length, dim), lambda s, n: (s, 0, 0, 0)),
            ],
            out_specs=[spec, spec],
        ),
        out_shape=[jax.ShapeDtypeStruct((rows, dim), F32)] * 2,
        compiler_params=pltpu.CompilerParams(vmem_limit_bytes=56 << 20),
        cost_estimate=pl.CostEstimate(
            flops=4 * rows * length * dim,
            bytes_accessed=4 * sessions * heads * length * dim,
            transcendentals=rows * length,
        ),
        name="suffix_attention",
    )(lengths, q, keys, values)


def merge_kernel(parts_ref, suffix_ref, suffix_lse_ref, out_ref):
    sources, padded, dim = parts_ref.shape
    rows = padded - 8
    copies, sessions, _ = out_ref.shape
    stats = []
    for c in range(sources):
        three = parts_ref[c, rows : rows + 8, :].astype(F32)
        stats.append(three[0:1] + three[1:2] + three[2:3])
    filler = jnp.full((rows - sources, rows), -3e38, F32)
    table = jnp.concatenate(stats + [filler], axis=0).T
    own = suffix_lse_ref[...]
    top = jnp.maximum(jnp.max(table, axis=1, keepdims=True), own[:, 0:1])
    shares = jnp.exp2(table - top)
    own_share = jnp.exp2(own[:, 0:1] - top)
    total = jnp.sum(shares, axis=1, keepdims=True) + own_share
    result = own_share * suffix_ref[...]
    for c in range(sources):
        result += shares[:, c : c + 1] * parts_ref[c, 0:rows, :].astype(F32)
    result = result / total
    for h in range(rows // sessions):
        piece = result[h * sessions : (h + 1) * sessions].astype(BF16)
        for copy in range(copies):
            out_ref[copy, :, h * dim : (h + 1) * dim] = piece


def merge(parts, suffix, suffix_lse, sessions, copies):
    rows, dim = suffix.shape
    return pl.pallas_call(
        merge_kernel,
        out_shape=jax.ShapeDtypeStruct((copies, sessions, rows // sessions * dim), BF16),
        name="merge_shards",
    )(parts, suffix, suffix_lse)


def project_kernel(attended_ref, weight_ref, out_ref):
    product = jnp.dot(attended_ref[...], weight_ref[0], preferred_element_type=F32)
    heads, _, rows, _ = out_ref.shape
    for h in range(heads):
        out_ref[h, 0] = product[h * rows : (h + 1) * rows].astype(BF16)


def project(attended, weights, heads):
    sessions, features = attended.shape
    wide, _, columns = weights.shape
    rows = sessions // heads
    return pl.pallas_call(
        project_kernel,
        grid=(wide,),
        in_specs=[
            pl.BlockSpec((sessions, features), lambda x: (0, 0)),
            pl.BlockSpec((1, features, columns), lambda x: (x, 0, 0)),
        ],
        out_specs=pl.BlockSpec((heads, 1, rows, columns), lambda x: (0, x, 0, 0)),
        out_shape=jax.ShapeDtypeStruct((heads, wide, rows, columns), BF16),
        compiler_params=pltpu.CompilerParams(vmem_limit_bytes=16 << 20),
        name="project",
    )(attended, weights)


def finish_kernel(parts_ref, out_ref):
    for x in range(parts_ref.shape[1]):
        total = parts_ref[0, x].astype(F32)
        for h in range(1, parts_ref.shape[0]):
            total += parts_ref[h, x].astype(F32)
        out_ref[:, x] = total


def finish(parts):
    _, x, outer, sessions, columns = parts.shape
    return pl.pallas_call(
        finish_kernel,
        out_shape=jax.ShapeDtypeStruct((outer, x, sessions, columns), F32),
        name="sum_heads",
    )(parts)


def per_device(queries, prefix_keys, prefix_values, suffix_keys, suffix_values, lengths, out_weight):
    sessions, local_heads, dim = queries.shape
    kv_local = prefix_keys.shape[0]
    rows = local_heads // kv_local * sessions
    scale = LOG2E / math.sqrt(dim)
    ctx = lax.axis_size("ctx")
    heads = lax.axis_size("yh") * lax.axis_size("core")
    wide = lax.axis_size("x")
    low = lax.axis_size("yl")

    arranged = queries.transpose(1, 0, 2).reshape(1, kv_local, rows, dim)
    spread = jnp.broadcast_to(arranged, (ctx, kv_local, rows, dim))
    gathered = lax.all_to_all(spread, "ctx", 0, 0, tiled=True)
    weight_all = lax.all_gather(out_weight, "x", axis=0)

    suffix, suffix_lse = suffix_attention(queries, suffix_keys, suffix_values, lengths, scale)
    gathered, suffix, suffix_lse = lax.optimization_barrier((gathered, suffix, suffix_lse))
    parts = prefix_attention(gathered, prefix_keys, prefix_values, scale)
    parts = lax.all_to_all(parts, "ctx", 0, 0, tiled=True)

    group = ctx * low
    everyone = merge(parts, suffix, suffix_lse, sessions, group)
    everyone, weight_all = lax.optimization_barrier((everyone, weight_all))
    everyone = lax.all_to_all(everyone, ("ctx", "yl"), 0, 0, tiled=True)
    everyone = everyone.reshape(group * sessions, local_heads * dim)
    partial_out = project(everyone, weight_all, heads)
    partial_out = partial_out.reshape(heads * wide, group * sessions // heads, out_weight.shape[1])
    partial_out = lax.all_to_all(partial_out, ("yh", "core", "x"), 0, 0, tiled=True)
    partial_out = partial_out.reshape(heads, wide, group // heads, sessions, out_weight.shape[1])
    return finish(partial_out).reshape(group * sessions * wide // heads, out_weight.shape[1])


def solution(mesh):
    fine = Mesh(mesh.devices.reshape(8, 2, 2, 2, 4), ("ctx", "yh", "core", "yl", "x"))
    both = ("ctx",) + SESS
    return jax.shard_map(
        per_device,
        mesh=fine,
        in_specs=(
            P(both, HEAD, None),
            P(HEAD, "ctx", None),
            P(HEAD, "ctx", None),
            P(both, HEAD, None, None),
            P(both, HEAD, None, None),
            P(both),
            P(HEAD, both),
        ),
        out_specs=P(HEAD, both),
        check_vma=False,
    )
```

time: 127 us -> 105 us (0.83)
  waiting for transfers between devices: 22.5 us -> 6.98 us
  between operations: 0.09 us -> 13.4 us
  Pallas kernels: 32.9 us -> 21.7 us
  local copies, waits for them, and re-layouts: 12.3 us -> 3.81 us
    all_to_all x2 -> x1, waiting for transfers between devices: 22.5 us -> 6.27 us  [per_device(): gathered = lax.all_to_all(spread, 'ctx', 0, 0, tiled=True)]
    pallas_call x3, Pallas kernels: 26.1 us -> 16.1 us  [the longest x1 12.3 us: prefix_attention(): pl.pallas_call(functools.partial(prefix_kernel, scale, 2, block), grid=(h...]
    unnamed x19 -> x5, local copies, waits for them, and re-layouts: 7.41 us -> 3.06 us
    broadcast_in_dim x2 -> x0, local copies, waits for them, and re-layouts: 3.2 us -> none  [the longest x1 1.61 us: per_device(): everyone = jnp.broadcast_to(attended[None], (group,) + attended.shape)]
    all_to_all x1, blocking collectives: 19.2 us -> 16.1 us  [per_device(): everyone = lax.all_to_all(everyone, ('ctx', 'yl'), 0, 0, tiled=True)]
    squeeze x1 -> x0, local copies, waits for them, and re-layouts: 1.67 us -> none  [per_device(): partial_out = project(everyone, [weight_all[x] for x in range(wide)], heads)]
    all_to_all x2 -> x1, starting transfers between devices: 8.14 us -> 9.01 us  [per_device(): gathered = lax.all_to_all(spread, 'ctx', 0, 0, tiled=True)]
  transfers between devices with their start and end apart: 2 -> 2, of which waited for: 2 -> 1; matrix products, arithmetic and copies ran while one was open for 1% -> 1% of each run, Pallas kernels for 6% -> 18%
where the time goes in v2:
time: 105 us
  blocking collectives  49.7 us (47%)
  Pallas kernels  21.7 us (21%)
  between operations  13.4 us (13%)
  starting transfers between devices  9.02 us (9%)
  waiting for transfers between devices  6.98 us (7%)
  local copies, waits for them, and re-layouts  3.81 us (4%)
    all_to_all x1, blocking collectives, per_device(): lax.all_to_all(partial_out, ('yh', 'core', 'x'), 0, 0, tiled=True)  20 us
    all_to_all x1, blocking collectives, per_device(): everyone = lax.all_to_all(everyone, ('ctx', 'yl'), 0, 0, tiled=True)  16.1 us
    all_to_all x1, blocking collectives, per_device(): parts = lax.all_to_all(parts, 'ctx', 0, 0, tiled=True)  13.6 us
    pallas_call x1, Pallas kernels, prefix_attention(): pl.pallas_call(functools.partial(prefix_kernel, scale, 2, block), grid=(h...  12.3 us
    all_to_all x1, starting transfers between devices, per_device(): gathered = lax.all_to_all(spread, 'ctx', 0, 0, tiled=True)  9.01 us
    all_to_all x1, waiting for transfers between devices, per_device(): gathered = lax.all_to_all(spread, 'ctx', 0, 0, tiled=True)  6.27 us
    pallas_call x1, Pallas kernels, suffix_attention(): pl.pallas_call(functools.partial(suffix_kernel, scale), grid_spec=pltpu.P...  4.1 us
    unnamed x5, local copies, waits for them, and re-layouts  3.06 us
  transfers between devices with their start and end apart: 2, of which 1 were waited for; matrix products, arithmetic and copies ran while one was open for 1% of the time, Pallas kernels for 18%

profile of v2, /device:TPU:1, one launch (start us, length us, event | category | flops | bytes accessed | tf_op | source)
XLA Modules:
  0.0 104.6 jit_solution(5517502825030056941)
XLA Ops:
  6.5 0.0 all-gather.3.cloned.1.call-start
  6.5 0.7 all-gather.3.cloned.1.call-update
  7.3 0.8 copy.8
  8.0 0.7 broadcast_in_dim.8
  8.8 9.0 %all-to-all-start = ((bf16[8,2,64,128]{3,2,1,0:T(8,128)(2,1)}), bf16[8,2,64,128]{3,2,1,0:T(8,128)(2,1)S(1)}, u32[]{:S(2)}, u32[]{:S(2)}) async-start(bf16[8,2,64,128]{3,2,1,0:T(8,128)(2,1)} %broadcast_in_dim.8), calls=%async_computation | async-start | bytes 524288 | tf_op jit(solution)/shard_map/all_to_all | solution.py:268
  17.8 4.1 %suffix_attention.1 = (f32[128,128]{1,0:T(8,128)}, f32[128,128]{1,0:T(8,128)}) custom-call(s32[8]{0:T(128)} %lengths_ref.1, bf16[8,16,128]{2,1,0:T(8,128)(2,1)} %q_ref.1, bf16[8,2,512,128]{3,2,1,0:T(8,128)(2,1)} %k_ref.1, bf16[8,2,512,128]{3,2,1,0:T(8,128)(2,1)} %v_ref.1), custom_call_target="tpu_custom_call" | custom-call | flops 33554432 | bytes 4194304 | tf_op jit(solution)/shard_map/suffix_attention/pallas_call | solution.py:157
  21.9 6.3 %all-to-all-done.q_ref = bf16[8,2,64,128]{3,2,1,0:T(8,128)(2,1)S(1)} async-done(((bf16[8,2,64,128]{3,2,1,0:T(8,128)(2,1)}), bf16[8,2,64,128]{3,2,1,0:T(8,128)(2,1)S(1)}, u32[]{:S(2)}, u32[]{:S(2)}) %all-to-all-start) | async-done | bytes 262176 | tf_op jit(solution)/shard_map/all_to_all | solution.py:268
  28.2 0.0 copy-start.1
  28.2 0.7 copy-done.1
  28.9 12.3 %prefix_attention.1 = bf16[8,136,128]{2,1,0:T(8,128)(2,1)} custom-call(bf16[8,2,64,128]{3,2,1,0:T(8,128)(2,1)} %copy-done.1, bf16[2,6144,128]{2,1,0:T(8,128)(2,1)} %k_hbm.1, bf16[2,6144,128]{2,1,0:T(8,128)(2,1)} %v_hbm.1), custom_call_target="tpu_custom_call" | custom-call | flops 3221225472 | bytes 6291456 | tf_op jit(solution)/shard_map/prefix_attention/pallas_call | solution.py:96
  41.1 13.6 %all_to_all.20.parts_ref = bf16[8,136,128]{2,1,0:T(8,128)(2,1)} all-to-all(bf16[8,136,128]{2,1,0:T(8,128)(2,1)} %prefix_attention.1), channel_id=1, replica_groups=mesh['ctx'=8,'yh'=2,'core'=2,'yl'=2,'x'=4] {'ctx'}, dimensions={0} | all-to-all | bytes 557056 | tf_op jit(solution)/shard_map/all_to_all | solution.py:274
  54.7 2.6 %merge_shards.1 = bf16[16,8,2048]{2,1,0:T(8,128)(2,1)} custom-call(bf16[8,136,128]{2,1,0:T(8,128)(2,1)} %all_to_all.20.parts_ref, f32[128,128]{1,0:T(8,128)} %get-tuple-element.15.suffix_ref, f32[128,128]{1,0:T(8,128)} %get-tuple-element.16.suffix_lse_ref), custom_call_target="tpu_custom_call" | custom-call | tf_op jit(solution)/shard_map/merge_shards/pallas_call | solution.py:207
  57.3 0.0 all-gather.3.cloned.1.call-done
  57.3 16.1 %all_to_all.21 = bf16[16,8,2048]{2,1,0:T(8,128)(2,1)S(1)} all-to-all(bf16[16,8,2048]{2,1,0:T(8,128)(2,1)} %merge_shards.1), channel_id=1, replica_groups=mesh['ctx'=8,'yh'=2,'core'=2,'yl'=2,'x'=4] {'ctx','yl'}, dimensions={0} | all-to-all | bytes 1048576 | tf_op jit(solution)/shard_map/all_to_all | solution.py:279
  73.4 0.0 copy-start
  73.4 1.6 %copy-done = bf16[8192,128]{1,0:T(8,128)(2,1)S(1)} copy-done((bf16[8192,128]{1,0:T(8,128)(2,1)S(1)}, bf16[8192,128]{1,0:T(8,128)(2,1)}, u32[]{:S(2)}) %copy-start) | copy-done | bytes 2097176
  75.0 1.2 %project.1 = bf16[4,4,32,128]{3,2,1,0:T(8,128)(2,1)S(1)} custom-call(bf16[128,2048]{1,0:T(8,128)(2,1)S(1)} %bitcast.9, bf16[4,2048,128]{2,1,0:T(8,128)(2,1)S(1)} %bitcast.8), custom_call_target="tpu_custom_call" | custom-call | tf_op jit(solution)/shard_map/project/pallas_call | solution.py:225
  76.2 20.0 %all_to_all.22 = bf16[16,32,128]{2,1,0:T(8,128)(2,1)} all-to-all(bf16[16,32,128]{2,1,0:T(8,128)(2,1)S(1)} %bitcast.10), channel_id=1, replica_groups=mesh['ctx'=8,'yh'=2,'core'=2,'yl'=2,'x'=4] {'yh','core','x'}, dimensions={0} | all-to-all | bytes 262144 | tf_op jit(solution)/shard_map/all_to_all | solution.py:283
  96.2 1.6 %sum_heads.1 = f32[4,4,8,128]{3,2,1,0:T(8,128)} custom-call(bf16[4,4,4,8,128]{4,3,2,1,0:T(8,128)(2,1)} %bitcast.11), custom_call_target="tpu_custom_call" | custom-call | tf_op jit(solution)/shard_map/sum_heads/pallas_call | solution.py:249
Async XLA Ops:
  6.5 50.8 %all-gather.3.cloned.1.call-start = ((), (), s32[]{:S(2)}) async-start(), calls=%async_computation.4 | async-start | bytes 2621440 | tf_op jit(solution)/shard_map/all_gather | solution.py:269
  8.8 19.4 %all-to-all-start = ((bf16[8,2,64,128]{3,2,1,0:T(8,128)(2,1)}), bf16[8,2,64,128]{3,2,1,0:T(8,128)(2,1)S(1)}, u32[]{:S(2)}, u32[]{:S(2)}) async-start(bf16[8,2,64,128]{3,2,1,0:T(8,128)(2,1)} %broadcast_in_dim.8), calls=%async_computation | async-start | bytes 524288 | tf_op jit(solution)/shard_map/all_to_all | solution.py:268
  28.2 0.7 copy-start.1
  73.4 1.6 %copy-start = (bf16[8192,128]{1,0:T(8,128)(2,1)S(1)}, bf16[8192,128]{1,0:T(8,128)(2,1)}, u32[]{:S(2)}) copy-start(bf16[8192,128]{1,0:T(8,128)(2,1)} %all-gather.3.cloned.1.call-done) | copy-start | bytes 6291460
Sparse Core Ops, SparseCore 0:
  9.2 37.1 all-gather.2

commit v3 on v2

--- a/solution.py
+++ b/solution.py
@@ -98,8 +98,8 @@
         grid=(heads,),
         in_specs=[
             pl.BlockSpec((sources, 1, rows, dim), lambda h: (0, h, 0, 0)),
-            pl.BlockSpec(memory_space=pl.ANY),
-            pl.BlockSpec(memory_space=pl.ANY),
+            pl.BlockSpec(memory_space=pltpu.HBM),
+            pl.BlockSpec(memory_space=pltpu.HBM),
         ],
         out_specs=pl.BlockSpec((sources, heads * rows + 8, dim), lambda h: (0, 0, 0)),
         out_shape=jax.ShapeDtypeStruct((sources, heads * rows + 8, dim), BF16),
@@ -112,7 +112,7 @@
             pltpu.SemaphoreType.DMA((heads, length // block)),
         ],
         compiler_params=pltpu.CompilerParams(
-            dimension_semantics=("arbitrary",), vmem_limit_bytes=58 << 20
+            dimension_semantics=("arbitrary",), vmem_limit_bytes=32 << 20
         ),
         cost_estimate=pl.CostEstimate(
             flops=4 * heads * total_rows * length * dim,
@@ -120,7 +120,11 @@
             transcendentals=heads * total_rows * length,
         ),
         name="prefix_attention",
-    )(q, keys, values)
+    )(
+        q,
+        pltpu.with_memory_space_constraint(keys, pltpu.HBM),
+        pltpu.with_memory_space_constraint(values, pltpu.HBM),
+    )
 
 
 def suffix_kernel(scale, lengths_ref, q_ref, k_ref, v_ref, o_ref, lse_ref):
@@ -211,29 +215,27 @@
     )(parts, suffix, suffix_lse)
 
 
-def project_kernel(attended_ref, weight_ref, out_ref):
-    product = jnp.dot(attended_ref[...], weight_ref[0], preferred_element_type=F32)
-    heads, _, rows, _ = out_ref.shape
-    for h in range(heads):
-        out_ref[h, 0] = product[h * rows : (h + 1) * rows].astype(BF16)
-
-
-def project(attended, weights, heads):
+def project_kernel(place_ref, attended_ref, *refs):
+    weights, out_ref = refs[:-1], refs[-1]
+    heads, wide, rows, columns = out_ref.shape
+    for k, weight_ref in enumerate(weights):
+        product = jnp.dot(attended_ref[...], weight_ref[...], preferred_element_type=F32)
+        x = lax.rem(place_ref[0] + (wide - k), wide)
+        out_ref[:, x] = product.astype(BF16).reshape(heads, rows, columns)
+
+
+def project(place, attended, weights, heads):
     sessions, features = attended.shape
-    wide, _, columns = weights.shape
-    rows = sessions // heads
+    columns = weights[0].shape[1]
+    vmem = pl.BlockSpec(memory_space=pltpu.VMEM)
     return pl.pallas_call(
         project_kernel,
-        grid=(wide,),
-        in_specs=[
-            pl.BlockSpec((sessions, features), lambda x: (0, 0)),
-            pl.BlockSpec((1, features, columns), lambda x: (x, 0, 0)),
-        ],
-        out_specs=pl.BlockSpec((heads, 1, rows, columns), lambda x: (0, x, 0, 0)),
-        out_shape=jax.ShapeDtypeStruct((heads, wide, rows, columns), BF16),
+        in_specs=[pl.BlockSpec(memory_space=pltpu.SMEM)] + [vmem] * (1 + len(weights)),
+        out_specs=vmem,
+        out_shape=jax.ShapeDtypeStruct((heads, len(weights), sessions // heads, columns), BF16),
         compiler_params=pltpu.CompilerParams(vmem_limit_bytes=16 << 20),
         name="project",
-    )(attended, weights)
+    )(place, attended, *weights)
 
 
 def finish_kernel(parts_ref, out_ref):
@@ -266,7 +268,10 @@
     arranged = queries.transpose(1, 0, 2).reshape(1, kv_local, rows, dim)
     spread = jnp.broadcast_to(arranged, (ctx, kv_local, rows, dim))
     gathered = lax.all_to_all(spread, "ctx", 0, 0, tiled=True)
-    weight_all = lax.all_gather(out_weight, "x", axis=0)
+    weights = [out_weight]
+    for k in range(1, wide):
+        pairs = [(x, (x + k) % wide) for x in range(wide)]
+        weights.append(lax.ppermute(out_weight, "x", pairs))
 
     suffix, suffix_lse = suffix_attention(queries, suffix_keys, suffix_values, lengths, scale)
     gathered, suffix, suffix_lse = lax.optimization_barrier((gathered, suffix, suffix_lse))
@@ -275,10 +280,11 @@
 
     group = ctx * low
     everyone = merge(parts, suffix, suffix_lse, sessions, group)
-    everyone, weight_all = lax.optimization_barrier((everyone, weight_all))
+    everyone, weights = lax.optimization_barrier((everyone, weights))
     everyone = lax.all_to_all(everyone, ("ctx", "yl"), 0, 0, tiled=True)
     everyone = everyone.reshape(group * sessions, local_heads * dim)
-    partial_out = project(everyone, weight_all, heads)
+    place = lax.axis_index("x").astype(jnp.int32).reshape(1)
+    partial_out = project(place, everyone, weights, heads)
     partial_out = partial_out.reshape(heads * wide, group * sessions // heads, out_weight.shape[1])
     partial_out = lax.all_to_all(partial_out, ("yh", "core", "x"), 0, 0, tiled=True)
     partial_out = partial_out.reshape(heads, wide, group // heads, sessions, out_weight.shape[1])

time: 105 us -> 85.7 us (0.82)
  blocking collectives: 49.7 us -> 32.6 us
  between operations: 13.4 us -> 0.04 us
  starting transfers between devices: 9.02 us -> 17.4 us
  waiting for transfers between devices: 6.98 us -> 14 us
  local copies, waits for them, and re-layouts: 3.81 us -> 1.52 us
  Pallas kernels: 21.7 us -> 19.6 us
    all_to_all x1 -> x0, blocking collectives: 16.1 us -> none  [per_device(): everyone = lax.all_to_all(everyone, ('ctx', 'yl'), 0, 0, tiled=True)]
    all_to_all x0 -> x1, waiting for transfers between devices: none -> 12.5 us  [per_device(): everyone = lax.all_to_all(everyone, ('ctx', 'yl'), 0, 0, tiled=True)]
    all_to_all x1, waiting for transfers between devices: 6.27 us -> 1.45 us  [per_device(): gathered = lax.all_to_all(spread, 'ctx', 0, 0, tiled=True)]
    ppermute x0 -> x3, starting transfers between devices: none -> 4.81 us  [per_device(): weights.append(lax.ppermute(out_weight, 'x', pairs))]
    all_to_all x0 -> x1, starting transfers between devices: none -> 3.58 us  [per_device(): everyone = lax.all_to_all(everyone, ('ctx', 'yl'), 0, 0, tiled=True)]
    unnamed x5 -> x3, local copies, waits for them, and re-layouts: 3.06 us -> 0.77 us
    all_to_all x1, blocking collectives: 20 us -> 18 us  [per_device(): lax.all_to_all(partial_out, ('yh', 'core', 'x'), 0, 0, tiled=True)]
    pallas_call x1, Pallas kernels: 12.3 us -> 10.7 us  [prefix_attention(): pl.pallas_call(functools.partial(prefix_kernel, scale, 2, block), grid=(h...]
  transfers between devices with their start and end apart: 2 -> 5, of which waited for: 1 -> 2; matrix products, arithmetic and copies ran while one was open for 1% -> 0% of each run, Pallas kernels for 18% -> 20%
where the time goes in v3:
time: 85.7 us; the launch traced here: 85.2 us
  blocking collectives  32.6 us (38%)
  Pallas kernels  19.6 us (23%)
  starting transfers between devices  17.4 us (20%)
  waiting for transfers between devices  14 us (16%)
  local copies, waits for them, and re-layouts  1.52 us (2%)
    all_to_all x1, blocking collectives, per_device(): lax.all_to_all(partial_out, ('yh', 'core', 'x'), 0, 0, tiled=True)  18 us
    all_to_all x1, blocking collectives, per_device(): parts = lax.all_to_all(parts, 'ctx', 0, 0, tiled=True)  14.6 us
    all_to_all x1, waiting for transfers between devices, per_device(): everyone = lax.all_to_all(everyone, ('ctx', 'yl'), 0, 0, tiled=True)  12.5 us
    pallas_call x1, Pallas kernels, prefix_attention(): pl.pallas_call(functools.partial(prefix_kernel, scale, 2, block), grid=(h...  10.7 us
    all_to_all x1, starting transfers between devices, per_device(): gathered = lax.all_to_all(spread, 'ctx', 0, 0, tiled=True)  9.01 us
    ppermute x3, starting transfers between devices, per_device(): weights.append(lax.ppermute(out_weight, 'x', pairs))  4.81 us
    pallas_call x1, Pallas kernels, suffix_attention(): pl.pallas_call(functools.partial(suffix_kernel, scale), grid_spec=pltpu.P...  4.1 us
    all_to_all x1, starting transfers between devices, per_device(): everyone = lax.all_to_all(everyone, ('ctx', 'yl'), 0, 0, tiled=True)  3.58 us
  transfers between devices with their start and end apart: 5, of which 2 were waited for; matrix products, arithmetic and copies ran while one was open for 0% of the time, Pallas kernels for 20%

profile of v3, /device:TPU:1, one launch (start us, length us, event | category | flops | bytes accessed | tf_op | source)
XLA Modules:
  0.0 85.2 jit_solution(8862538536858222588)
XLA Ops:
  0.0 0.8 copy.8
  0.8 0.7 broadcast_in_dim.8
  1.5 9.0 %all-to-all-start = ((bf16[8,2,64,128]{3,2,1,0:T(8,128)(2,1)}), bf16[8,2,64,128]{3,2,1,0:T(8,128)(2,1)S(1)}, u32[]{:S(2)}, u32[]{:S(2)}) async-start(bf16[8,2,64,128]{3,2,1,0:T(8,128)(2,1)} %broadcast_in_dim.8), calls=%async_computation | async-start | bytes 524288 | tf_op jit(solution)/shard_map/all_to_all | solution.py:270
  10.5 1.2 %collective-permute-start = (bf16[2048,128]{1,0:T(8,128)(2,1)}, bf16[2048,128]{1,0:T(8,128)(2,1)S(1)}, u32[]{:S(2)}, u32[]{:S(2)}) collective-permute-start(bf16[2048,128]{1,0:T(8,128)(2,1)} %refs_0_), channel_id=1, source_target_pairs={{0,1},{1,2},{2,3},{3,0},{4,5},{5,6},{6,7},{7,4},{8,9},{9,10},{10,1... | collective-permute-start | bytes 1572872 | tf_op jit(solution)/shard_map/ppermute | solution.py:274
  11.7 2.5 %collective-permute-start.1 = (bf16[2048,128]{1,0:T(8,128)(2,1)}, bf16[2048,128]{1,0:T(8,128)(2,1)S(1)}, u32[]{:S(2)}, u32[]{:S(2)}) collective-permute-start(bf16[2048,128]{1,0:T(8,128)(2,1)} %refs_0_), channel_id=1, source_target_pairs={{0,2},{1,3},{2,0},{3,1},{4,6},{5,7},{6,4},{7,5},{8,10},{9,11},{10,... | collective-permute-start | bytes 1572872 | tf_op jit(solution)/shard_map/ppermute | solution.py:274
  14.2 1.2 %collective-permute-start.2 = (bf16[2048,128]{1,0:T(8,128)(2,1)}, bf16[2048,128]{1,0:T(8,128)(2,1)S(1)}, u32[]{:S(2)}, u32[]{:S(2)}) collective-permute-start(bf16[2048,128]{1,0:T(8,128)(2,1)} %refs_0_), channel_id=1, source_target_pairs={{0,3},{1,0},{2,1},{3,2},{4,7},{5,4},{6,5},{7,6},{8,11},{9,8},{10,9... | collective-permute-start | bytes 1572872 | tf_op jit(solution)/shard_map/ppermute | solution.py:274
  15.3 4.1 %suffix_attention.1 = (f32[128,128]{1,0:T(8,128)}, f32[128,128]{1,0:T(8,128)}) custom-call(s32[8]{0:T(128)} %lengths_ref.1, bf16[8,16,128]{2,1,0:T(8,128)(2,1)} %q_ref.1, bf16[8,2,512,128]{3,2,1,0:T(8,128)(2,1)} %k_ref.1, bf16[8,2,512,128]{3,2,1,0:T(8,128)(2,1)} %v_ref.1), custom_call_target="tpu_custom_call" | custom-call | flops 33554432 | bytes 4194304 | tf_op jit(solution)/shard_map/suffix_attention/pallas_call | solution.py:161
  19.5 1.5 %all-to-all-done.q_ref = bf16[8,2,64,128]{3,2,1,0:T(8,128)(2,1)S(1)} async-done(((bf16[8,2,64,128]{3,2,1,0:T(8,128)(2,1)}), bf16[8,2,64,128]{3,2,1,0:T(8,128)(2,1)S(1)}, u32[]{:S(2)}, u32[]{:S(2)}) %all-to-all-start) | async-done | bytes 262176 | tf_op jit(solution)/shard_map/all_to_all | solution.py:270
  20.9 0.0 copy-start
  20.9 10.7 %prefix_attention.1 = bf16[8,136,128]{2,1,0:T(8,128)(2,1)S(1)} custom-call(bf16[8,2,64,128]{3,2,1,0:T(8,128)(2,1)S(1)} %all-to-all-done.q_ref, bf16[2,6144,128]{2,1,0:T(8,128)(2,1)} %k_hbm.1, bf16[2,6144,128]{2,1,0:T(8,128)(2,1)} %v_hbm.1), custom_call_target="tpu_custom_call" | custom-call | flops 3221225472 | bytes 6291456 | tf_op jit(solution)/shard_map/prefix_attention/pallas_call | solution.py:96
  31.6 14.6 %all_to_all.20.parts_ref = bf16[8,136,128]{2,1,0:T(8,128)(2,1)} all-to-all(bf16[8,136,128]{2,1,0:T(8,128)(2,1)S(1)} %prefix_attention.1), channel_id=1, replica_groups=mesh['ctx'=8,'yh'=2,'core'=2,'yl'=2,'x'=4] {'ctx'}, dimensions={0} | all-to-all | bytes 557056 | tf_op jit(solution)/shard_map/all_to_all | solution.py:279
  46.3 2.6 %merge_shards.1 = bf16[16,8,2048]{2,1,0:T(8,128)(2,1)} custom-call(bf16[8,136,128]{2,1,0:T(8,128)(2,1)} %all_to_all.20.parts_ref, f32[128,128]{1,0:T(8,128)} %get-tuple-element.18.suffix_ref, f32[128,128]{1,0:T(8,128)} %get-tuple-element.19.suffix_lse_ref), custom_call_target="tpu_custom_call" | custom-call | tf_op jit(solution)/shard_map/merge_shards/pallas_call | solution.py:211
  48.8 0.0 collective-permute-done.refs_1_
  48.9 0.0 collective-permute-done.1.refs_2_
  48.9 0.0 collective-permute-done.2.refs_3_
  48.9 3.6 %all-to-all-start.2 = ((bf16[16,8,2048]{2,1,0:T(8,128)(2,1)}), bf16[16,8,2048]{2,1,0:T(8,128)(2,1)S(1)}, u32[]{:S(2)}, u32[]{:S(2)}) async-start(bf16[16,8,2048]{2,1,0:T(8,128)(2,1)} %merge_shards.1), calls=%async_computation.2 | async-start | bytes 1048576 | tf_op jit(solution)/shard_map/all_to_all | solution.py:284
  52.5 12.5 %all-to-all-done.2 = bf16[16,8,2048]{2,1,0:T(8,128)(2,1)S(1)} async-done(((bf16[16,8,2048]{2,1,0:T(8,128)(2,1)}), bf16[16,8,2048]{2,1,0:T(8,128)(2,1)S(1)}, u32[]{:S(2)}, u32[]{:S(2)}) %all-to-all-start.2) | async-done | bytes 524320 | tf_op jit(solution)/shard_map/all_to_all | solution.py:284
  65.0 0.0 copy-done
  65.0 0.7 project.1
  65.7 18.0 %all_to_all.21 = bf16[16,32,128]{2,1,0:T(8,128)(2,1)} all-to-all(bf16[16,32,128]{2,1,0:T(8,128)(2,1)S(1)} %bitcast.9), channel_id=1, replica_groups=mesh['ctx'=8,'yh'=2,'core'=2,'yl'=2,'x'=4] {'yh','core','x'}, dimensions={0} | all-to-all | bytes 262144 | tf_op jit(solution)/shard_map/all_to_all | solution.py:289
  83.6 1.6 %sum_heads.1 = f32[4,4,8,128]{3,2,1,0:T(8,128)} custom-call(bf16[4,4,4,8,128]{4,3,2,1,0:T(8,128)(2,1)} %bitcast.10), custom_call_target="tpu_custom_call" | custom-call | tf_op jit(solution)/shard_map/sum_heads/pallas_call | solution.py:251
Async XLA Ops:
  1.5 19.4 %all-to-all-start = ((bf16[8,2,64,128]{3,2,1,0:T(8,128)(2,1)}), bf16[8,2,64,128]{3,2,1,0:T(8,128)(2,1)S(1)}, u32[]{:S(2)}, u32[]{:S(2)}) async-start(bf16[8,2,64,128]{3,2,1,0:T(8,128)(2,1)} %broadcast_in_dim.8), calls=%async_computation | async-start | bytes 524288 | tf_op jit(solution)/shard_map/all_to_all | solution.py:270
  10.5 38.3 %collective-permute-start = (bf16[2048,128]{1,0:T(8,128)(2,1)}, bf16[2048,128]{1,0:T(8,128)(2,1)S(1)}, u32[]{:S(2)}, u32[]{:S(2)}) collective-permute-start(bf16[2048,128]{1,0:T(8,128)(2,1)} %refs_0_), channel_id=1, source_target_pairs={{0,1},{1,2},{2,3},{3,0},{4,5},{5,6},{6,7},{7,4},{8,9},{9,10},{10,1... | collective-permute-start | bytes 1572872 | tf_op jit(solution)/shard_map/ppermute | solution.py:274
  11.7 37.1 %collective-permute-start.1 = (bf16[2048,128]{1,0:T(8,128)(2,1)}, bf16[2048,128]{1,0:T(8,128)(2,1)S(1)}, u32[]{:S(2)}, u32[]{:S(2)}) collective-permute-start(bf16[2048,128]{1,0:T(8,128)(2,1)} %refs_0_), channel_id=1, source_target_pairs={{0,2},{1,3},{2,0},{3,1},{4,6},{5,7},{6,4},{7,5},{8,10},{9,11},{10,... | collective-permute-start | bytes 1572872 | tf_op jit(solution)/shard_map/ppermute | solution.py:274
  14.2 34.7 %collective-permute-start.2 = (bf16[2048,128]{1,0:T(8,128)(2,1)}, bf16[2048,128]{1,0:T(8,128)(2,1)S(1)}, u32[]{:S(2)}, u32[]{:S(2)}) collective-permute-start(bf16[2048,128]{1,0:T(8,128)(2,1)} %refs_0_), channel_id=1, source_target_pairs={{0,3},{1,0},{2,1},{3,2},{4,7},{5,4},{6,5},{7,6},{8,11},{9,8},{10,9... | collective-permute-start | bytes 1572872 | tf_op jit(solution)/shard_map/ppermute | solution.py:274
  20.9 44.1 %copy-start = (bf16[2048,128]{1,0:T(8,128)(2,1)S(1)}, bf16[2048,128]{1,0:T(8,128)(2,1)}, u32[]{:S(2)}) copy-start(bf16[2048,128]{1,0:T(8,128)(2,1)} %refs_0_) | copy-start | bytes 1572868
  48.9 16.1 %all-to-all-start.2 = ((bf16[16,8,2048]{2,1,0:T(8,128)(2,1)}), bf16[16,8,2048]{2,1,0:T(8,128)(2,1)S(1)}, u32[]{:S(2)}, u32[]{:S(2)}) async-start(bf16[16,8,2048]{2,1,0:T(8,128)(2,1)} %merge_shards.1), calls=%async_computation.2 | async-start | bytes 1048576 | tf_op jit(solution)/shard_map/all_to_all | solution.py:284

commit v4 on v3

--- a/solution.py
+++ b/solution.py
@@ -18,11 +18,14 @@
 
 
 def prefix_kernel(
-    scale, chunk, block, q_ref, k_hbm, v_hbm, o_ref, k_ref, v_ref, acc_ref, lse_ref, k_sem, v_sem
+    scale, chunk, block, all_q_ref, k_hbm, v_hbm, o_ref, q_ref, k_ref, v_ref, acc_ref, lse_ref,
+    k_sem, v_sem
 ):
     head = pl.program_id(0)
-    sources, _, rows, dim = q_ref.shape
+    sources, sessions, local_heads, dim = all_q_ref.shape
     heads, length, _ = k_ref.shape
+    group = local_heads // heads
+    rows = sessions * group
     tiles = [(c, k) for c in range(0, sources, chunk) for k in range(0, length, block)]
 
     def copy_of(source, target, sem, h, part):
@@ -35,10 +38,12 @@
             for part in range(length // block):
                 copy_of(k_hbm, k_ref, k_sem, h, part).start()
                 copy_of(v_hbm, v_ref, v_sem, h, part).start()
+            part = all_q_ref[:, :, h * group : (h + 1) * group, :]
+            q_ref[h] = part.reshape(sources * rows, dim)
 
     def scores_of(tile):
         c, k = tile
-        q = q_ref[c : c + chunk, 0].reshape(chunk * rows, dim)
+        q = q_ref[head, c * rows : (c + chunk) * rows]
         if c == 0:
             copy_of(k_hbm, k_ref, k_sem, head, k // block).wait()
         return lax.dot_general(q, k_ref[head, k : k + block], NT, preferred_element_type=F32)
@@ -89,21 +94,23 @@
 
 
 def prefix_attention(q, keys, values, scale):
-    sources, heads, rows, dim = q.shape
-    length = keys.shape[1]
+    sources, sessions, local_heads, dim = q.shape
+    heads, length, _ = keys.shape
+    rows = sessions * local_heads // heads
     block = length // 2
     total_rows = sources * rows
     return pl.pallas_call(
         functools.partial(prefix_kernel, scale, 2, block),
         grid=(heads,),
         in_specs=[
-            pl.BlockSpec((sources, 1, rows, dim), lambda h: (0, h, 0, 0)),
+            pl.BlockSpec(q.shape, lambda h: (0, 0, 0, 0)),
             pl.BlockSpec(memory_space=pltpu.HBM),
             pl.BlockSpec(memory_space=pltpu.HBM),
         ],
         out_specs=pl.BlockSpec((sources, heads * rows + 8, dim), lambda h: (0, 0, 0)),
         out_shape=jax.ShapeDtypeStruct((sources, heads * rows + 8, dim), BF16),
         scratch_shapes=[
+            pltpu.VMEM((heads, total_rows, dim), BF16),
             pltpu.VMEM(keys.shape, BF16),
             pltpu.VMEM(values.shape, BF16),
             pltpu.VMEM((total_rows, dim), F32),
@@ -148,7 +155,7 @@
         softened.append((top, jnp.sum(weights, axis=1, keepdims=True), weights.astype(BF16)))
     for (s, h), (top, total, weights) in zip(pairs, softened):
         out = jnp.dot(weights, v_ref[s, h], preferred_element_type=F32) / total
-        rows = pl.ds(h * group * sessions + step * count + s, group, stride=sessions)
+        rows = pl.ds((h * sessions + step * count + s) * group, group)
         o_ref[rows, :] = out
         lse_ref[rows, :] = jnp.broadcast_to(top * scale + jnp.log2(total), out.shape)
 
@@ -171,17 +178,22 @@
             out_specs=[spec, spec],
         ),
         out_shape=[jax.ShapeDtypeStruct((rows, dim), F32)] * 2,
-        compiler_params=pltpu.CompilerParams(vmem_limit_bytes=56 << 20),
+        compiler_params=pltpu.CompilerParams(vmem_limit_bytes=16 << 20),
         cost_estimate=pl.CostEstimate(
             flops=4 * rows * length * dim,
             bytes_accessed=4 * sessions * heads * length * dim,
             transcendentals=rows * length,
         ),
         name="suffix_attention",
-    )(lengths, q, keys, values)
-
-
-def merge_kernel(parts_ref, suffix_ref, suffix_lse_ref, out_ref):
+    )(
+        lengths,
+        q,
+        pltpu.with_memory_space_constraint(keys, pltpu.HBM),
+        pltpu.with_memory_space_constraint(values, pltpu.HBM),
+    )
+
+
+def merge_kernel(heads, parts_ref, suffix_ref, suffix_lse_ref, out_ref, result_ref):
     sources, padded, dim = parts_ref.shape
     rows = padded - 8
     copies, sessions, _ = out_ref.shape
@@ -199,17 +211,23 @@
     result = own_share * suffix_ref[...]
     for c in range(sources):
         result += shares[:, c : c + 1] * parts_ref[c, 0:rows, :].astype(F32)
-    result = result / total
-    for h in range(rows // sessions):
-        piece = result[h * sessions : (h + 1) * sessions].astype(BF16)
-        for copy in range(copies):
-            out_ref[copy, :, h * dim : (h + 1) * dim] = piece
-
-
-def merge(parts, suffix, suffix_lse, sessions, copies):
+    result_ref[...] = result / total
+    group = rows // sessions // heads
+    for h in range(heads):
+        for g in range(group):
+            first = h * sessions * group + g
+            piece = result_ref[pl.ds(first, sessions, stride=group), :].astype(BF16)
+            column = (h * group + g) * dim
+            for copy in range(copies):
+                out_ref[copy, :, column : column + dim] = piece
+
+
+def merge(parts, suffix, suffix_lse, sessions, heads, copies):
     rows, dim = suffix.shape
     return pl.pallas_call(
-        merge_kernel,
+        functools.partial(merge_kernel, heads),
+        scratch_shapes=[pltpu.VMEM((rows, dim), F32)],
+        compiler_params=pltpu.CompilerParams(vmem_limit_bytes=16 << 20),
         out_shape=jax.ShapeDtypeStruct((copies, sessions, rows // sessions * dim), BF16),
         name="merge_shards",
     )(parts, suffix, suffix_lse)
@@ -251,6 +269,7 @@
     return pl.pallas_call(
         finish_kernel,
         out_shape=jax.ShapeDtypeStruct((outer, x, sessions, columns), F32),
+        compiler_params=pltpu.CompilerParams(vmem_limit_bytes=16 << 20),
         name="sum_heads",
     )(parts)
 
@@ -258,32 +277,30 @@
 def per_device(queries, prefix_keys, prefix_values, suffix_keys, suffix_values, lengths, out_weight):
     sessions, local_heads, dim = queries.shape
     kv_local = prefix_keys.shape[0]
-    rows = local_heads // kv_local * sessions
     scale = LOG2E / math.sqrt(dim)
     ctx = lax.axis_size("ctx")
     heads = lax.axis_size("yh") * lax.axis_size("core")
     wide = lax.axis_size("x")
     low = lax.axis_size("yl")
 
-    arranged = queries.transpose(1, 0, 2).reshape(1, kv_local, rows, dim)
-    spread = jnp.broadcast_to(arranged, (ctx, kv_local, rows, dim))
-    gathered = lax.all_to_all(spread, "ctx", 0, 0, tiled=True)
+    spread = jnp.broadcast_to(queries[None], (ctx,) + queries.shape)
+    gathered = lax.all_to_all(spread, "ctx", 0, 0, tiled=False)
     weights = [out_weight]
     for k in range(1, wide):
         pairs = [(x, (x + k) % wide) for x in range(wide)]
         weights.append(lax.ppermute(out_weight, "x", pairs))
 
+    parts = prefix_attention(gathered, prefix_keys, prefix_values, scale)
+    place = lax.axis_index("x").astype(jnp.int32).reshape(1)
+    parts, queries, place = lax.optimization_barrier((parts, queries, place))
+    parts = lax.all_to_all(parts, "ctx", 0, 0, tiled=True)
     suffix, suffix_lse = suffix_attention(queries, suffix_keys, suffix_values, lengths, scale)
-    gathered, suffix, suffix_lse = lax.optimization_barrier((gathered, suffix, suffix_lse))
-    parts = prefix_attention(gathered, prefix_keys, prefix_values, scale)
-    parts = lax.all_to_all(parts, "ctx", 0, 0, tiled=True)
 
     group = ctx * low
-    everyone = merge(parts, suffix, suffix_lse, sessions, group)
-    everyone, weights = lax.optimization_barrier((everyone, weights))
+    everyone = merge(parts, suffix, suffix_lse, sessions, kv_local, group)
+    everyone, weights, place = lax.optimization_barrier((everyone, weights, place))
     everyone = lax.all_to_all(everyone, ("ctx", "yl"), 0, 0, tiled=True)
     everyone = everyone.reshape(group * sessions, local_heads * dim)
-    place = lax.axis_index("x").astype(jnp.int32).reshape(1)
     partial_out = project(place, everyone, weights, heads)
     partial_out = partial_out.reshape(heads * wide, group * sessions // heads, out_weight.shape[1])
     partial_out = lax.all_to_all(partial_out, ("yh", "core", "x"), 0, 0, tiled=True)

time: 85.7 us -> 83 us (0.968)
  Pallas kernels: 19.6 us -> 16.8 us
  waiting for transfers between devices: 14 us -> 11.2 us
  blocking collectives: 32.6 us -> 35.1 us
    all_to_all x2, waiting for transfers between devices: 14 us -> 11.2 us  [the longest x1 6.22 us: per_device(): parts = lax.all_to_all(parts, 'ctx', 0, 0, tiled=True)]
    pallas_call x1, Pallas kernels: 2.59 us -> 0.82 us  [merge(): pl.pallas_call(functools.partial(merge_kernel, heads), scratch_shapes=[pl...]
    all_to_all x1, blocking collectives: 18 us -> 19.3 us  [per_device(): lax.all_to_all(partial_out, ('yh', 'core', 'x'), 0, 0, tiled=True)]
    all_to_all x1, blocking collectives: 14.6 us -> 15.8 us  [per_device(): everyone = lax.all_to_all(everyone, ('ctx', 'yl'), 0, 0, tiled=True)]
    pallas_call x1, Pallas kernels: 1.55 us -> 0.65 us  [finish(): pl.pallas_call(finish_kernel, out_shape=jax.ShapeDtypeStruct((outer, x, s...]
  transfers between devices with their start and end apart: 5 -> 5, of which waited for: 2 -> 2; matrix products, arithmetic and copies ran while one was open for 0% -> 0% of each run, Pallas kernels for 20% -> 19%
where the time goes in v4:
time: 83 us; the launch traced here: 82.6 us
  blocking collectives  35.1 us (42%)
  starting transfers between devices  17.9 us (22%)
  Pallas kernels  16.8 us (20%)
  waiting for transfers between devices  11.2 us (13%)
  local copies, waits for them, and re-layouts  1.52 us (2%)
    all_to_all x1, blocking collectives, per_device(): lax.all_to_all(partial_out, ('yh', 'core', 'x'), 0, 0, tiled=True)  19.3 us
    all_to_all x1, blocking collectives, per_device(): everyone = lax.all_to_all(everyone, ('ctx', 'yl'), 0, 0, tiled=True)  15.8 us
    pallas_call x1, Pallas kernels, prefix_attention(): pl.pallas_call(functools.partial(prefix_kernel, scale, 2, block), grid=(h...  11.3 us
    all_to_all x1, starting transfers between devices, per_device(): gathered = lax.all_to_all(spread, 'ctx', 0, 0, tiled=False)  9.01 us
    all_to_all x1, waiting for transfers between devices, per_device(): parts = lax.all_to_all(parts, 'ctx', 0, 0, tiled=True)  6.22 us
    ppermute x3, starting transfers between devices, per_device(): weights.append(lax.ppermute(out_weight, 'x', pairs))  5.42 us
    all_to_all x1, waiting for transfers between devices, per_device(): gathered = lax.all_to_all(spread, 'ctx', 0, 0, tiled=False)  4.94 us
    all_to_all x1, starting transfers between devices, per_device(): parts = lax.all_to_all(parts, 'ctx', 0, 0, tiled=True)  3.43 us
  transfers between devices with their start and end apart: 5, of which 2 were waited for; matrix products, arithmetic and copies ran while one was open for 0% of the time, Pallas kernels for 19%

profile of v4, /device:TPU:1, one launch (start us, length us, event | category | flops | bytes accessed | tf_op | source)
XLA Modules:
  0.0 82.6 jit_solution(12368743156519104564)
XLA Ops:
  0.0 1.5 %broadcast_in_dim.2 = bf16[8,8,16,128]{3,2,1,0:T(8,128)(2,1)} broadcast(bf16[8,16,128]{2,1,0:T(8,128)(2,1)} %q_ref), dimensions={1,2,3} | broadcast | bytes 294912 | tf_op jit(solution)/shard_map/broadcast_in_dim | solution.py:286
  1.5 9.0 %all-to-all-start = ((bf16[8,8,16,128]{3,2,1,0:T(8,128)(2,1)}), bf16[8,8,16,128]{3,2,1,0:T(8,128)(2,1)S(1)}, u32[]{:S(2)}, u32[]{:S(2)}) async-start(bf16[8,8,16,128]{3,2,1,0:T(8,128)(2,1)} %broadcast_in_dim.2), calls=%async_computation | async-start | bytes 524288 | tf_op jit(solution)/shard_map/all_to_all | solution.py:287
  10.5 2.7 %collective-permute-start.1 = (bf16[2048,128]{1,0:T(8,128)(2,1)}, bf16[2048,128]{1,0:T(8,128)(2,1)S(1)}, u32[]{:S(2)}, u32[]{:S(2)}) collective-permute-start(bf16[2048,128]{1,0:T(8,128)(2,1)} %refs_0_), channel_id=1, source_target_pairs={{0,2},{1,3},{2,0},{3,1},{4,6},{5,7},{6,4},{7,5},{8,10},{9,11},{10,... | collective-permute-start | bytes 1572872 | tf_op jit(solution)/shard_map/ppermute | solution.py:291
  13.3 0.3 collective-permute-start
  13.6 2.4 %collective-permute-start.2 = (bf16[2048,128]{1,0:T(8,128)(2,1)}, bf16[2048,128]{1,0:T(8,128)(2,1)S(1)}, u32[]{:S(2)}, u32[]{:S(2)}) collective-permute-start(bf16[2048,128]{1,0:T(8,128)(2,1)} %refs_0_), channel_id=1, source_target_pairs={{0,3},{1,0},{2,1},{3,2},{4,7},{5,4},{6,5},{7,6},{8,11},{9,8},{10,9... | collective-permute-start | bytes 1572872 | tf_op jit(solution)/shard_map/ppermute | solution.py:291
  15.9 0.0 copy-start.1
  15.9 0.0 copy-start.2
  15.9 4.9 %all-to-all-done.all_q_ref = bf16[8,8,16,128]{3,2,1,0:T(8,128)(2,1)S(1)} async-done(((bf16[8,8,16,128]{3,2,1,0:T(8,128)(2,1)}), bf16[8,8,16,128]{3,2,1,0:T(8,128)(2,1)S(1)}, u32[]{:S(2)}, u32[]{:S(2)}) %all-to-all-start) | async-done | bytes 262176 | tf_op jit(solution)/shard_map/all_to_all | solution.py:287
  20.9 11.3 %prefix_attention.1 = bf16[8,136,128]{2,1,0:T(8,128)(2,1)} custom-call(bf16[8,8,16,128]{3,2,1,0:T(8,128)(2,1)S(1)} %all-to-all-done.all_q_ref, bf16[2,6144,128]{2,1,0:T(8,128)(2,1)} %k_hbm.1, bf16[2,6144,128]{2,1,0:T(8,128)(2,1)} %v_hbm.1), custom_call_target="tpu_custom_call" | custom-call | flops 3221225472 | bytes 6291456 | tf_op jit(solution)/shard_map/prefix_attention/pallas_call | solution.py:102
  32.2 3.4 %all-to-all-start.1 = ((bf16[8,136,128]{2,1,0:T(8,128)(2,1)}), bf16[8,136,128]{2,1,0:T(8,128)(2,1)S(1)}, u32[]{:S(2)}, u32[]{:S(2)}) async-start(bf16[8,136,128]{2,1,0:T(8,128)(2,1)} %prefix_attention.1), calls=%async_computation.1 | async-start | bytes 557056 | tf_op jit(solution)/shard_map/all_to_all | solution.py:296
  35.7 0.0 copy-done.1
  35.7 0.0 copy-done.2
  35.7 0.0 copy-start
  35.7 3.3 %suffix_attention.1 = (f32[128,128]{1,0:T(8,128)S(1)}, f32[128,128]{1,0:T(8,128)S(1)}) custom-call(s32[8]{0:T(128)S(1)} %copy-done.2, bf16[8,16,128]{2,1,0:T(8,128)(2,1)S(1)} %copy-done.1, bf16[8,2,512,128]{3,2,1,0:T(8,128)(2,1)} %k_ref.1, bf16[8,2,512,128]{3,2,1,0:T(8,128)(2,1)} %v_ref.1), custom_call_target="tpu_custom_call" | custom-call | flops 33554432 | bytes 4194304 | tf_op jit(solution)/shard_map/suffix_attention/pallas_call | solution.py:168
  39.0 6.2 %all-to-all-done.1.parts_ref = bf16[8,136,128]{2,1,0:T(8,128)(2,1)S(1)} async-done(((bf16[8,136,128]{2,1,0:T(8,128)(2,1)}), bf16[8,136,128]{2,1,0:T(8,128)(2,1)S(1)}, u32[]{:S(2)}, u32[]{:S(2)}) %all-to-all-start.1) | async-done | bytes 278560 | tf_op jit(solution)/shard_map/all_to_all | solution.py:296
  45.2 0.8 merge_shards.1
  46.1 0.0 collective-permute-done.1.refs_2_
  46.1 0.0 collective-permute-done.refs_1_
  46.1 0.0 collective-permute-done.2.refs_3_
  46.1 15.8 %all_to_all.20 = bf16[16,8,2048]{2,1,0:T(8,128)(2,1)S(1)} all-to-all(bf16[16,8,2048]{2,1,0:T(8,128)(2,1)S(1)} %merge_shards.1), channel_id=1, replica_groups=mesh['ctx'=8,'yh'=2,'core'=2,'yl'=2,'x'=4] {'ctx','yl'}, dimensions={0} | all-to-all | bytes 1048576 | tf_op jit(solution)/shard_map/all_to_all | solution.py:302
  61.9 0.0 copy-done
  61.9 0.7 project.1
  62.6 19.3 %all_to_all.21 = bf16[16,32,128]{2,1,0:T(8,128)(2,1)S(1)} all-to-all(bf16[16,32,128]{2,1,0:T(8,128)(2,1)S(1)} %bitcast.6), channel_id=1, replica_groups=mesh['ctx'=8,'yh'=2,'core'=2,'yl'=2,'x'=4] {'yh','core','x'}, dimensions={0} | all-to-all | bytes 262144 | tf_op jit(solution)/shard_map/all_to_all | solution.py:306
  81.9 0.6 sum_heads.1
Async XLA Ops:
  1.5 19.4 %all-to-all-start = ((bf16[8,8,16,128]{3,2,1,0:T(8,128)(2,1)}), bf16[8,8,16,128]{3,2,1,0:T(8,128)(2,1)S(1)}, u32[]{:S(2)}, u32[]{:S(2)}) async-start(bf16[8,8,16,128]{3,2,1,0:T(8,128)(2,1)} %broadcast_in_dim.2), calls=%async_computation | async-start | bytes 524288 | tf_op jit(solution)/shard_map/all_to_all | solution.py:287
  10.5 35.5 %collective-permute-start.1 = (bf16[2048,128]{1,0:T(8,128)(2,1)}, bf16[2048,128]{1,0:T(8,128)(2,1)S(1)}, u32[]{:S(2)}, u32[]{:S(2)}) collective-permute-start(bf16[2048,128]{1,0:T(8,128)(2,1)} %refs_0_), channel_id=1, source_target_pairs={{0,2},{1,3},{2,0},{3,1},{4,6},{5,7},{6,4},{7,5},{8,10},{9,11},{10,... | collective-permute-start | bytes 1572872 | tf_op jit(solution)/shard_map/ppermute | solution.py:291
  13.3 32.8 %collective-permute-start = (bf16[2048,128]{1,0:T(8,128)(2,1)}, bf16[2048,128]{1,0:T(8,128)(2,1)S(1)}, u32[]{:S(2)}, u32[]{:S(2)}) collective-permute-start(bf16[2048,128]{1,0:T(8,128)(2,1)} %refs_0_), channel_id=1, source_target_pairs={{0,1},{1,2},{2,3},{3,0},{4,5},{5,6},{6,7},{7,4},{8,9},{9,10},{10,1... | collective-permute-start | bytes 1572872 | tf_op jit(solution)/shard_map/ppermute | solution.py:291
  13.6 32.5 %collective-permute-start.2 = (bf16[2048,128]{1,0:T(8,128)(2,1)}, bf16[2048,128]{1,0:T(8,128)(2,1)S(1)}, u32[]{:S(2)}, u32[]{:S(2)}) collective-permute-start(bf16[2048,128]{1,0:T(8,128)(2,1)} %refs_0_), channel_id=1, source_target_pairs={{0,3},{1,0},{2,1},{3,2},{4,7},{5,4},{6,5},{7,6},{8,11},{9,8},{10,9... | collective-permute-start | bytes 1572872 | tf_op jit(solution)/shard_map/ppermute | solution.py:291
  15.9 19.7 %copy-start.1 = (bf16[8,16,128]{2,1,0:T(8,128)(2,1)S(1)}, bf16[8,16,128]{2,1,0:T(8,128)(2,1)}, u32[]{:S(2)}) copy-start(bf16[8,16,128]{2,1,0:T(8,128)(2,1)} %q_ref) | copy-start | bytes 98308
  15.9 19.7 %copy-start.2 = (s32[8]{0:T(128)S(1)}, s32[8]{0:T(128)}, u32[]{:S(2)}) copy-start(s32[8]{0:T(128)} %lengths_ref.1) | copy-start | bytes 100
  32.2 13.0 %all-to-all-start.1 = ((bf16[8,136,128]{2,1,0:T(8,128)(2,1)}), bf16[8,136,128]{2,1,0:T(8,128)(2,1)S(1)}, u32[]{:S(2)}, u32[]{:S(2)}) async-start(bf16[8,136,128]{2,1,0:T(8,128)(2,1)} %prefix_attention.1), calls=%async_computation.1 | async-start | bytes 557056 | tf_op jit(solution)/shard_map/all_to_all | solution.py:296
  35.7 26.2 %copy-start = (bf16[2048,128]{1,0:T(8,128)(2,1)S(1)}, bf16[2048,128]{1,0:T(8,128)(2,1)}, u32[]{:S(2)}) copy-start(bf16[2048,128]{1,0:T(8,128)(2,1)} %refs_0_) | copy-start | bytes 1572868

commit v5 on v4

--- a/solution.py
+++ b/solution.py
@@ -17,104 +17,205 @@
 NT = (((1,), (1,)), ((), ()))
 
 
+def soft_tiles(scale, tiles, scores_of, values_of, acc_ref, finish):
+    scores = scores_of(*tiles[0])
+    for index, (span, part) in enumerate(tiles):
+        following = tiles[index + 1] if index + 1 < len(tiles) else None
+        ahead = scores_of(*following) if following else None
+        new = jnp.max(scores, axis=1, keepdims=True)
+        if part > 0:
+            new = jnp.maximum(top, new)
+            factor = jnp.exp2((top - new) * scale)
+        weights = jnp.exp2((scores - new) * scale)
+        share = jnp.sum(weights, axis=1, keepdims=True)
+        product = jnp.dot(
+            weights.astype(BF16), values_of(span, part), preferred_element_type=F32
+        )
+        if part > 0:
+            total = total * factor + share
+            product = acc_ref[span] * factor + product
+        else:
+            total = share
+        top, scores = new, ahead
+        if following is None or following[0] != span:
+            finish(span, product / total, top * scale + jnp.log2(total))
+        else:
+            acc_ref[span] = product
+
+
+def start_copies(block, sources, targets, sems):
+    heads, length, _ = targets[0].shape
+    for h in range(heads):
+        for part in range(length // block):
+            for source, target, sem in zip(sources, targets, sems):
+                copy_part(block, source, target, sem, h, part).start()
+
+
+def copy_part(block, source, target, sem, h, part):
+    span = pl.ds(part * block, block)
+    return pltpu.make_async_copy(source.at[h, span], target.at[h, span], sem.at[h, part])
+
+
+def own_kernel(
+    scale, block, q_ref, k_hbm, v_hbm, o_ref, lse_ref, k_ref, v_ref, acc_ref, k_sem, v_sem
+):
+    sessions, local_heads, dim = q_ref.shape
+    heads, length, _ = k_ref.shape
+    group = local_heads // heads
+    rows = sessions * group
+    parts = length // block
+
+    start_copies(block, (k_hbm, v_hbm), (k_ref, v_ref), (k_sem, v_sem))
+
+    def scores_of(span, part):
+        h = span.start // rows
+        copy_part(block, k_hbm, k_ref, k_sem, h, part).wait()
+        q = q_ref[:, h * group : (h + 1) * group, :].reshape(rows, dim)
+        keys = k_ref[h, part * block : (part + 1) * block]
+        return lax.dot_general(q, keys, NT, preferred_element_type=F32)
+
+    def values_of(span, part):
+        h = span.start // rows
+        copy_part(block, v_hbm, v_ref, v_sem, h, part).wait()
+        return v_ref[h, part * block : (part + 1) * block]
+
+    def finish(span, out, lse):
+        h = span.start // rows
+        o_ref[h] = out.astype(BF16)
+        lse_ref[h] = jnp.broadcast_to(lse, (rows, dim))
+
+    spans = [slice(h * rows, (h + 1) * rows) for h in range(heads)]
+    tiles = [(span, part) for span in spans for part in range(parts)]
+    soft_tiles(scale, tiles, scores_of, values_of, acc_ref, finish)
+
+
+def own_attention(q, keys, values, scale):
+    sessions, local_heads, dim = q.shape
+    heads, length, _ = keys.shape
+    rows = sessions * local_heads // heads
+    block = length // 2
+    vmem = pl.BlockSpec(memory_space=pltpu.VMEM)
+    hbm = pl.BlockSpec(memory_space=pltpu.HBM)
+    return pl.pallas_call(
+        functools.partial(own_kernel, scale, block),
+        in_specs=[vmem, hbm, hbm],
+        out_specs=[vmem] * 2,
+        out_shape=[
+            jax.ShapeDtypeStruct((heads, rows, dim), BF16),
+            jax.ShapeDtypeStruct((heads, rows, dim), F32),
+        ],
+        scratch_shapes=[
+            pltpu.VMEM(keys.shape, BF16),
+            pltpu.VMEM(values.shape, BF16),
+            pltpu.VMEM((heads * rows, dim), F32),
+            pltpu.SemaphoreType.DMA((heads, length // block)),
+            pltpu.SemaphoreType.DMA((heads, length // block)),
+        ],
+        compiler_params=pltpu.CompilerParams(vmem_limit_bytes=24 << 20),
+        cost_estimate=pl.CostEstimate(
+            flops=4 * heads * rows * length * dim,
+            bytes_accessed=4 * heads * length * dim,
+            transcendentals=heads * rows * length,
+        ),
+        name="own_attention",
+    )(
+        q,
+        pltpu.with_memory_space_constraint(keys, pltpu.HBM),
+        pltpu.with_memory_space_constraint(values, pltpu.HBM),
+    )
+
+
 def prefix_kernel(
-    scale, chunk, block, all_q_ref, k_hbm, v_hbm, o_ref, q_ref, k_ref, v_ref, acc_ref, lse_ref,
-    k_sem, v_sem
+    scale, chunk, block, me_ref, all_q_ref, k_hbm, v_hbm, own_ref, own_lse_ref, o_ref,
+    k_ref, v_ref, q_ref, acc_ref, lse_ref, k_sem, v_sem,
 ):
     head = pl.program_id(0)
     sources, sessions, local_heads, dim = all_q_ref.shape
     heads, length, _ = k_ref.shape
     group = local_heads // heads
     rows = sessions * group
-    tiles = [(c, k) for c in range(0, sources, chunk) for k in range(0, length, block)]
-
-    def copy_of(source, target, sem, h, part):
-        span = pl.ds(part * block, block)
-        return pltpu.make_async_copy(source.at[h, span], target.at[h, span], sem.at[h, part])
+    others = sources - 1
+    place = [lax.rem(me_ref[0] + (1 + j), sources) for j in range(sources)]
 
     @pl.when(head == 0)
     def _():
-        for h in range(heads):
-            for part in range(length // block):
-                copy_of(k_hbm, k_ref, k_sem, h, part).start()
-                copy_of(v_hbm, v_ref, v_sem, h, part).start()
-            part = all_q_ref[:, :, h * group : (h + 1) * group, :]
-            q_ref[h] = part.reshape(sources * rows, dim)
-
-    def scores_of(tile):
-        c, k = tile
-        q = q_ref[head, c * rows : (c + chunk) * rows]
-        if c == 0:
-            copy_of(k_hbm, k_ref, k_sem, head, k // block).wait()
-        return lax.dot_general(q, k_ref[head, k : k + block], NT, preferred_element_type=F32)
-
-    scores = scores_of(tiles[0])
-    for index, (c, k) in enumerate(tiles):
-        if c == 0:
-            copy_of(v_hbm, v_ref, v_sem, head, k // block).wait()
-        ahead = scores_of(tiles[index + 1]) if index + 1 < len(tiles) else None
-        new = jnp.max(scores, axis=1, keepdims=True)
-        if k > 0:
-            new = jnp.maximum(top, new)
-            factor = jnp.exp2((top - new) * scale)
-        weights = jnp.exp2((scores - new) * scale)
-        part = jnp.sum(weights, axis=1, keepdims=True)
-        product = jnp.dot(
-            weights.astype(BF16), v_ref[head, k : k + block], preferred_element_type=F32
-        )
-        span = slice(c * rows, (c + chunk) * rows)
-        if k > 0:
-            total = total * factor + part
-            product = acc_ref[span] * factor + product
-        else:
-            total = part
-        top, scores = new, ahead
-        if k + block < length:
-            acc_ref[span] = product
-            continue
-        out = (product / total).astype(BF16)
-        lse = top * scale + jnp.log2(total)
-        lse_ref[head, span] = jnp.broadcast_to(lse, (chunk * rows, lse_ref.shape[2]))
-        for i in range(chunk):
-            o_ref[c + i, pl.ds(head * rows, rows), :] = out[i * rows : (i + 1) * rows]
+        start_copies(block, (k_hbm, v_hbm), (k_ref, v_ref), (k_sem, v_sem))
+        for j in range(others):
+            for h in range(heads):
+                part = all_q_ref[place[j], :, h * group : (h + 1) * group, :]
+                q_ref[h, j * rows : (j + 1) * rows] = part.reshape(rows, dim)
+
+    def scores_of(span, part):
+        if span.start == 0:
+            copy_part(block, k_hbm, k_ref, k_sem, head, part).wait()
+        keys = k_ref[head, part * block : (part + 1) * block]
+        return lax.dot_general(q_ref[head, span], keys, NT, preferred_element_type=F32)
+
+    def values_of(span, part):
+        if span.start == 0:
+            copy_part(block, v_hbm, v_ref, v_sem, head, part).wait()
+        return v_ref[head, part * block : (part + 1) * block]
+
+    def finish(span, out, lse):
+        lse_ref[head, span] = jnp.broadcast_to(lse, (lse.shape[0], lse_ref.shape[2]))
+        out = out.astype(BF16)
+        for i in range(out.shape[0] // rows):
+            source = place[span.start // rows + i]
+            o_ref[source, pl.ds(head * rows, rows), :] = out[i * rows : (i + 1) * rows]
+
+    spans = [
+        slice(j * rows, min(j + chunk, others) * rows) for j in range(0, others, chunk)
+    ]
+    tiles = [(span, part) for span in spans for part in range(length // block)]
+    soft_tiles(scale, tiles, scores_of, values_of, acc_ref, finish)
 
     @pl.when(head == heads - 1)
     def _():
-        for c in range(sources):
-            column = jnp.concatenate(
-                [lse_ref[h, c * rows : (c + 1) * rows, :] for h in range(heads)], axis=0
-            )
-            row = column.T[0:8]
+        for h in range(heads):
+            o_ref[place[others], h * rows : (h + 1) * rows, :] = own_ref[h]
+        for j in range(sources):
+            pieces = [
+                lse_ref[h, j * rows : (j + 1) * rows, :] if j < others else own_lse_ref[h]
+                for h in range(heads)
+            ]
+            row = jnp.concatenate(pieces, axis=0).T[0:8]
             high = row.astype(BF16).astype(F32)
             middle = (row - high).astype(BF16).astype(F32)
             low = row - high - middle
-            place = lax.broadcasted_iota(jnp.int32, row.shape, 0)
-            stats = jnp.where(place == 0, high, jnp.where(place == 1, middle, low))
-            o_ref[c, pl.ds(heads * rows, 8), :] = stats.astype(BF16)
-
-
-def prefix_attention(q, keys, values, scale):
+            index = lax.broadcasted_iota(jnp.int32, row.shape, 0)
+            stats = jnp.where(index == 0, high, jnp.where(index == 1, middle, low))
+            o_ref[place[j], heads * rows : heads * rows + 8, :] = stats.astype(BF16)
+
+
+def prefix_attention(me, q, keys, values, own, own_lse, scale):
     sources, sessions, local_heads, dim = q.shape
     heads, length, _ = keys.shape
     rows = sessions * local_heads // heads
     block = length // 2
-    total_rows = sources * rows
+    other_rows = (sources - 1) * rows
+
+    def whole(shape):
+        return pl.BlockSpec(shape, lambda h: (0,) * len(shape))
+
     return pl.pallas_call(
         functools.partial(prefix_kernel, scale, 2, block),
         grid=(heads,),
         in_specs=[
-            pl.BlockSpec(q.shape, lambda h: (0, 0, 0, 0)),
+            pl.BlockSpec(memory_space=pltpu.SMEM),
+            whole(q.shape),
             pl.BlockSpec(memory_space=pltpu.HBM),
             pl.BlockSpec(memory_space=pltpu.HBM),
+            whole(own.shape),
+            whole(own_lse.shape),
         ],
-        out_specs=pl.BlockSpec((sources, heads * rows + 8, dim), lambda h: (0, 0, 0)),
+        out_specs=whole((sources, heads * rows + 8, dim)),
         out_shape=jax.ShapeDtypeStruct((sources, heads * rows + 8, dim), BF16),
         scratch_shapes=[
-            pltpu.VMEM((heads, total_rows, dim), BF16),
             pltpu.VMEM(keys.shape, BF16),
             pltpu.VMEM(values.shape, BF16),
-            pltpu.VMEM((total_rows, dim), F32),
-            pltpu.VMEM((heads, total_rows, 128), F32),
+            pltpu.VMEM((heads, other_rows, dim), BF16),
+            pltpu.VMEM((other_rows, dim), F32),
+            pltpu.VMEM((heads, other_rows, 128), F32),
             pltpu.SemaphoreType.DMA((heads, length // block)),
             pltpu.SemaphoreType.DMA((heads, length // block)),
         ],
@@ -122,15 +223,18 @@
             dimension_semantics=("arbitrary",), vmem_limit_bytes=32 << 20
         ),
         cost_estimate=pl.CostEstimate(
-            flops=4 * heads * total_rows * length * dim,
+            flops=4 * heads * other_rows * length * dim,
             bytes_accessed=4 * heads * length * dim,
-            transcendentals=heads * total_rows * length,
+            transcendentals=heads * other_rows * length,
         ),
         name="prefix_attention",
     )(
+        me,
         q,
         pltpu.with_memory_space_constraint(keys, pltpu.HBM),
         pltpu.with_memory_space_constraint(values, pltpu.HBM),
+        own,
+        own_lse,
     )
 
 
@@ -283,14 +387,20 @@
     wide = lax.axis_size("x")
     low = lax.axis_size("yl")
 
-    spread = jnp.broadcast_to(queries[None], (ctx,) + queries.shape)
-    gathered = lax.all_to_all(spread, "ctx", 0, 0, tiled=False)
+    flat = queries.reshape(1, sessions * local_heads, dim)
+    spread = jnp.broadcast_to(flat, (ctx, sessions * local_heads, dim))
+    gathered = lax.all_to_all(spread, "ctx", 0, 0, tiled=True)
+    gathered = gathered.reshape(ctx, sessions, local_heads, dim)
     weights = [out_weight]
     for k in range(1, wide):
         pairs = [(x, (x + k) % wide) for x in range(wide)]
         weights.append(lax.ppermute(out_weight, "x", pairs))
 
-    parts = prefix_attention(gathered, prefix_keys, prefix_values, scale)
+    own, own_lse = own_attention(queries, prefix_keys, prefix_values, scale)
+    me = lax.axis_index("ctx").astype(jnp.int32).reshape(1)
+    parts = prefix_attention(
+        me, gathered, prefix_keys, prefix_values, own, own_lse, scale
+    )
     place = lax.axis_index("x").astype(jnp.int32).reshape(1)
     parts, queries, place = lax.optimization_barrier((parts, queries, place))
     parts = lax.all_to_all(parts, "ctx", 0, 0, tiled=True)

time: 83 us -> 84.3 us (1.016)
  waiting for transfers between devices: 11.2 us -> 6.49 us
  Pallas kernels: 16.8 us -> 20.8 us
  starting transfers between devices: 17.9 us -> 21.1 us
  blocking collectives: 35.1 us -> 33.1 us
    all_to_all x1, waiting for transfers between devices: 4.94 us -> 0.1 us  [per_device(): gathered = lax.all_to_all(spread, 'ctx', 0, 0, tiled=True)]
    pallas_call x0 -> x1, Pallas kernels: none -> 4.08 us  [own_attention(): pl.pallas_call(functools.partial(own_kernel, scale, block), in_specs=[vme...]
    all_to_all x1, starting transfers between devices: 3.43 us -> 6.63 us  [per_device(): parts = lax.all_to_all(parts, 'ctx', 0, 0, tiled=True)]
    all_to_all x1, blocking collectives: 19.3 us -> 16.7 us  [per_device(): lax.all_to_all(partial_out, ('yh', 'core', 'x'), 0, 0, tiled=True)]
  transfers between devices with their start and end apart: 5 -> 5, of which waited for: 2 -> 2; matrix products, arithmetic and copies ran while one was open for 0% -> 0% of each run, Pallas kernels for 19% -> 23%
where the time goes in v5:
time: 84.3 us; the launch traced here: 83.8 us
  blocking collectives  33.1 us (39%)
  starting transfers between devices  21.1 us (25%)
  Pallas kernels  20.8 us (25%)
  waiting for transfers between devices  6.49 us (8%)
  local copies, waits for them, and re-layouts  2.27 us (3%)
    all_to_all x1, blocking collectives, per_device(): lax.all_to_all(partial_out, ('yh', 'core', 'x'), 0, 0, tiled=True)  16.7 us
    all_to_all x1, blocking collectives, per_device(): everyone = lax.all_to_all(everyone, ('ctx', 'yl'), 0, 0, tiled=True)  16.4 us
    pallas_call x1, Pallas kernels, prefix_attention(): pl.pallas_call(functools.partial(prefix_kernel, scale, 2, block), grid=(h...  11.2 us
    all_to_all x1, starting transfers between devices, per_device(): gathered = lax.all_to_all(spread, 'ctx', 0, 0, tiled=True)  9.01 us
    all_to_all x1, starting transfers between devices, per_device(): parts = lax.all_to_all(parts, 'ctx', 0, 0, tiled=True)  6.63 us
    all_to_all x1, waiting for transfers between devices, per_device(): parts = lax.all_to_all(parts, 'ctx', 0, 0, tiled=True)  6.38 us
    ppermute x3, starting transfers between devices, per_device(): weights.append(lax.ppermute(out_weight, 'x', pairs))  5.42 us
    pallas_call x1, Pallas kernels, own_attention(): pl.pallas_call(functools.partial(own_kernel, scale, block), in_specs=[vme...  4.08 us
  transfers between devices with their start and end apart: 5, of which 2 were waited for; matrix products, arithmetic and copies ran while one was open for 0% of the time, Pallas kernels for 23%

profile of v5, /device:TPU:1, one launch (start us, length us, event | category | flops | bytes accessed | tf_op | source)
XLA Modules:
  0.0 83.8 jit_solution(15807734807186423600)
XLA Ops:
  0.0 1.5 %broadcast_in_dim.8 = bf16[8,128,128]{2,1,0:T(8,128)(2,1)} broadcast(bf16[128,128]{1,0:T(8,128)(2,1)} %bitcast.11), dimensions={1,2} | broadcast | bytes 294912 | tf_op jit(solution)/shard_map/broadcast_in_dim | solution.py:391
  1.5 9.0 %all-to-all-start = ((bf16[8,128,128]{2,1,0:T(8,128)(2,1)}), bf16[8,128,128]{2,1,0:T(8,128)(2,1)S(1)}, u32[]{:S(2)}, u32[]{:S(2)}) async-start(bf16[8,128,128]{2,1,0:T(8,128)(2,1)} %broadcast_in_dim.8), calls=%async_computation | async-start | bytes 524288 | tf_op jit(solution)/shard_map/all_to_all | solution.py:392
  10.5 2.7 %collective-permute-start.1 = (bf16[2048,128]{1,0:T(8,128)(2,1)}, bf16[2048,128]{1,0:T(8,128)(2,1)S(1)}, u32[]{:S(2)}, u32[]{:S(2)}) collective-permute-start(bf16[2048,128]{1,0:T(8,128)(2,1)} %refs_0_), channel_id=1, source_target_pairs={{0,2},{1,3},{2,0},{3,1},{4,6},{5,7},{6,4},{7,5},{8,10},{9,11},{10,... | collective-permute-start | bytes 1572872 | tf_op jit(solution)/shard_map/ppermute | solution.py:397
  13.3 0.3 collective-permute-start
  13.6 2.4 %collective-permute-start.2 = (bf16[2048,128]{1,0:T(8,128)(2,1)}, bf16[2048,128]{1,0:T(8,128)(2,1)S(1)}, u32[]{:S(2)}, u32[]{:S(2)}) collective-permute-start(bf16[2048,128]{1,0:T(8,128)(2,1)} %refs_0_), channel_id=1, source_target_pairs={{0,3},{1,0},{2,1},{3,2},{4,7},{5,4},{6,5},{7,6},{8,11},{9,8},{10,9... | collective-permute-start | bytes 1572872 | tf_op jit(solution)/shard_map/ppermute | solution.py:397
  15.9 0.0 copy-start.1
  15.9 0.8 copy-done.1
  16.7 4.1 %own_attention.1 = (bf16[2,64,128]{2,1,0:T(8,128)(2,1)S(1)}, f32[2,64,128]{2,1,0:T(8,128)S(1)}) custom-call(bf16[8,16,128]{2,1,0:T(8,128)(2,1)S(1)} %copy-done.1, bf16[2,6144,128]{2,1,0:T(8,128)(2,1)} %k_hbm.3, bf16[2,6144,128]{2,1,0:T(8,128)(2,1)} %v_hbm.3), custom_call_target="tpu_custom_call" | custom-call | flops 402653184 | bytes 6291456 | tf_op jit(solution)/shard_map/own_attention/pallas_call | solution.py:99
  20.8 0.1 all-to-all-done
  20.9 0.0 copy-start.2
  20.9 0.0 copy-start.3
  20.9 11.2 %prefix_attention.1 = bf16[8,136,128]{2,1,0:T(8,128)(2,1)} custom-call(s32[1]{0:T(128)} %bitcast.me_ref, bf16[8,8,16,128]{3,2,1,0:T(8,128)(2,1)S(1)} %bitcast.12, bf16[2,6144,128]{2,1,0:T(8,128)(2,1)} %k_hbm.3, bf16[2,6144,128]{2,1,0:T(8,128)(2,1)} %v_hbm.3, bf16[2,64,128]{2,1,0:T(8,128)(2,1)S(1)} %get-tuple-element.18.own_ref, ...), custom_call_target="tpu_custom_call" | custom-call | flops 2818572288 | bytes 6291456 | tf_op jit(solution)/shard_map/prefix_attention/pallas_call | solution.py:200
  32.1 6.6 %all-to-all-start.1 = ((bf16[8,136,128]{2,1,0:T(8,128)(2,1)}), bf16[8,136,128]{2,1,0:T(8,128)(2,1)S(1)}, u32[]{:S(2)}, u32[]{:S(2)}) async-start(bf16[8,136,128]{2,1,0:T(8,128)(2,1)} %prefix_attention.1), calls=%async_computation.1 | async-start | bytes 557056 | tf_op jit(solution)/shard_map/all_to_all | solution.py:406
  38.7 0.0 copy-done.2
  38.7 0.0 copy-done.3
  38.7 0.0 copy-start
  38.7 3.3 %suffix_attention.1 = (f32[128,128]{1,0:T(8,128)S(1)}, f32[128,128]{1,0:T(8,128)S(1)}) custom-call(s32[8]{0:T(128)S(1)} %copy-done.3, bf16[8,16,128]{2,1,0:T(8,128)(2,1)S(1)} %copy-done.2, bf16[8,2,512,128]{3,2,1,0:T(8,128)(2,1)} %k_ref.1, bf16[8,2,512,128]{3,2,1,0:T(8,128)(2,1)} %v_ref.1), custom_call_target="tpu_custom_call" | custom-call | flops 33554432 | bytes 4194304 | tf_op jit(solution)/shard_map/suffix_attention/pallas_call | solution.py:272
  42.0 6.4 %all-to-all-done.1.parts_ref = bf16[8,136,128]{2,1,0:T(8,128)(2,1)S(1)} async-done(((bf16[8,136,128]{2,1,0:T(8,128)(2,1)}), bf16[8,136,128]{2,1,0:T(8,128)(2,1)S(1)}, u32[]{:S(2)}, u32[]{:S(2)}) %all-to-all-start.1) | async-done | bytes 278560 | tf_op jit(solution)/shard_map/all_to_all | solution.py:406
  48.4 0.8 merge_shards.1
  49.3 0.0 collective-permute-done.1.refs_2_
  49.3 0.0 collective-permute-done.refs_1_
  49.3 0.0 collective-permute-done.2.refs_3_
  49.3 16.4 %all_to_all.20 = bf16[16,8,2048]{2,1,0:T(8,128)(2,1)S(1)} all-to-all(bf16[16,8,2048]{2,1,0:T(8,128)(2,1)S(1)} %merge_shards.1), channel_id=1, replica_groups=mesh['ctx'=8,'yh'=2,'core'=2,'yl'=2,'x'=4] {'ctx','yl'}, dimensions={0} | all-to-all | bytes 1048576 | tf_op jit(solution)/shard_map/all_to_all | solution.py:412
  65.7 0.0 copy-done
  65.7 0.7 project.1
  66.5 16.7 %all_to_all.21 = bf16[16,32,128]{2,1,0:T(8,128)(2,1)S(1)} all-to-all(bf16[16,32,128]{2,1,0:T(8,128)(2,1)S(1)} %bitcast.9), channel_id=1, replica_groups=mesh['ctx'=8,'yh'=2,'core'=2,'yl'=2,'x'=4] {'yh','core','x'}, dimensions={0} | all-to-all | bytes 262144 | tf_op jit(solution)/shard_map/all_to_all | solution.py:416
  83.1 0.6 sum_heads.1
Async XLA Ops:
  1.5 19.4 %all-to-all-start = ((bf16[8,128,128]{2,1,0:T(8,128)(2,1)}), bf16[8,128,128]{2,1,0:T(8,128)(2,1)S(1)}, u32[]{:S(2)}, u32[]{:S(2)}) async-start(bf16[8,128,128]{2,1,0:T(8,128)(2,1)} %broadcast_in_dim.8), calls=%async_computation | async-start | bytes 524288 | tf_op jit(solution)/shard_map/all_to_all | solution.py:392
  10.5 38.7 %collective-permute-start.1 = (bf16[2048,128]{1,0:T(8,128)(2,1)}, bf16[2048,128]{1,0:T(8,128)(2,1)S(1)}, u32[]{:S(2)}, u32[]{:S(2)}) collective-permute-start(bf16[2048,128]{1,0:T(8,128)(2,1)} %refs_0_), channel_id=1, source_target_pairs={{0,2},{1,3},{2,0},{3,1},{4,6},{5,7},{6,4},{7,5},{8,10},{9,11},{10,... | collective-permute-start | bytes 1572872 | tf_op jit(solution)/shard_map/ppermute | solution.py:397
  13.3 36.0 %collective-permute-start = (bf16[2048,128]{1,0:T(8,128)(2,1)}, bf16[2048,128]{1,0:T(8,128)(2,1)S(1)}, u32[]{:S(2)}, u32[]{:S(2)}) collective-permute-start(bf16[2048,128]{1,0:T(8,128)(2,1)} %refs_0_), channel_id=1, source_target_pairs={{0,1},{1,2},{2,3},{3,0},{4,5},{5,6},{6,7},{7,4},{8,9},{9,10},{10,1... | collective-permute-start | bytes 1572872 | tf_op jit(solution)/shard_map/ppermute | solution.py:397
  13.6 35.7 %collective-permute-start.2 = (bf16[2048,128]{1,0:T(8,128)(2,1)}, bf16[2048,128]{1,0:T(8,128)(2,1)S(1)}, u32[]{:S(2)}, u32[]{:S(2)}) collective-permute-start(bf16[2048,128]{1,0:T(8,128)(2,1)} %refs_0_), channel_id=1, source_target_pairs={{0,3},{1,0},{2,1},{3,2},{4,7},{5,4},{6,5},{7,6},{8,11},{9,8},{10,9... | collective-permute-start | bytes 1572872 | tf_op jit(solution)/shard_map/ppermute | solution.py:397
  15.9 0.8 copy-start.1
  20.9 17.8 %copy-start.2 = (bf16[8,16,128]{2,1,0:T(8,128)(2,1)S(1)}, bf16[8,16,128]{2,1,0:T(8,128)(2,1)}, u32[]{:S(2)}) copy-start(bf16[8,16,128]{2,1,0:T(8,128)(2,1)} %q_ref.2) | copy-start | bytes 98308
  20.9 17.8 %copy-start.3 = (s32[8]{0:T(128)S(1)}, s32[8]{0:T(128)}, u32[]{:S(2)}) copy-start(s32[8]{0:T(128)} %lengths_ref.1) | copy-start | bytes 100
  32.1 16.3 %all-to-all-start.1 = ((bf16[8,136,128]{2,1,0:T(8,128)(2,1)}), bf16[8,136,128]{2,1,0:T(8,128)(2,1)S(1)}, u32[]{:S(2)}, u32[]{:S(2)}) async-start(bf16[8,136,128]{2,1,0:T(8,128)(2,1)} %prefix_attention.1), calls=%async_computation.1 | async-start | bytes 557056 | tf_op jit(solution)/shard_map/all_to_all | solution.py:406
  38.7 27.0 %copy-start = (bf16[2048,128]{1,0:T(8,128)(2,1)S(1)}, bf16[2048,128]{1,0:T(8,128)(2,1)}, u32[]{:S(2)}) copy-start(bf16[2048,128]{1,0:T(8,128)(2,1)} %refs_0_) | copy-start | bytes 1572868

commit v6 on v4

--- a/solution.py
+++ b/solution.py
@@ -17,90 +17,117 @@
 NT = (((1,), (1,)), ((), ()))
 
 
+TN = (((0,), (0,)), ((), ()))
+SAFE_TOTAL = 2.0**100
+
+
 def prefix_kernel(
-    scale, chunk, block, all_q_ref, k_hbm, v_hbm, o_ref, q_ref, k_ref, v_ref, acc_ref, lse_ref,
-    k_sem, v_sem
+    scale, tile, first, all_q_ref, k_hbm, v_hbm, o_ref, q_ref, k_ref, v_ref, acc_ref, top_ref,
+    total_ref, lse_ref, k_sem, v_sem,
 ):
     head = pl.program_id(0)
     sources, sessions, local_heads, dim = all_q_ref.shape
     heads, length, _ = k_ref.shape
     group = local_heads // heads
     rows = sessions * group
-    tiles = [(c, k) for c in range(0, sources, chunk) for k in range(0, length, block)]
+    parts = [(0, first), (first, length - first)]
 
     def copy_of(source, target, sem, h, part):
-        span = pl.ds(part * block, block)
+        span = pl.ds(*parts[part])
         return pltpu.make_async_copy(source.at[h, span], target.at[h, span], sem.at[h, part])
 
     @pl.when(head == 0)
     def _():
         for h in range(heads):
-            for part in range(length // block):
+            for part in range(len(parts)):
                 copy_of(k_hbm, k_ref, k_sem, h, part).start()
                 copy_of(v_hbm, v_ref, v_sem, h, part).start()
+        for h in range(heads):
             part = all_q_ref[:, :, h * group : (h + 1) * group, :]
             q_ref[h] = part.reshape(sources * rows, dim)
 
-    def scores_of(tile):
-        c, k = tile
-        q = q_ref[head, c * rows : (c + chunk) * rows]
-        if c == 0:
-            copy_of(k_hbm, k_ref, k_sem, head, k // block).wait()
-        return lax.dot_general(q, k_ref[head, k : k + block], NT, preferred_element_type=F32)
-
-    scores = scores_of(tiles[0])
-    for index, (c, k) in enumerate(tiles):
-        if c == 0:
-            copy_of(v_hbm, v_ref, v_sem, head, k // block).wait()
-        ahead = scores_of(tiles[index + 1]) if index + 1 < len(tiles) else None
-        new = jnp.max(scores, axis=1, keepdims=True)
-        if k > 0:
-            new = jnp.maximum(top, new)
-            factor = jnp.exp2((top - new) * scale)
-        weights = jnp.exp2((scores - new) * scale)
-        part = jnp.sum(weights, axis=1, keepdims=True)
-        product = jnp.dot(
-            weights.astype(BF16), v_ref[head, k : k + block], preferred_element_type=F32
-        )
-        span = slice(c * rows, (c + chunk) * rows)
-        if k > 0:
-            total = total * factor + part
-            product = acc_ref[span] * factor + product
+    def scores_of(start):
+        keys = k_ref[head, pl.ds(start, tile), :]
+        return lax.dot_general(keys, q_ref[head], NT, preferred_element_type=F32)
+
+    def product_of(weights, start):
+        values = v_ref[head, pl.ds(start, tile), :]
+        return lax.dot_general(values, weights.astype(BF16), TN, preferred_element_type=F32)
+
+    copy_of(k_hbm, k_ref, k_sem, head, 0).wait()
+    scores = scores_of(0)
+    top = jnp.max(scores, axis=0, keepdims=True)
+    for start in range(0, length, tile):
+        if start == 0:
+            copy_of(v_hbm, v_ref, v_sem, head, 0).wait()
+        if start == first:
+            copy_of(v_hbm, v_ref, v_sem, head, 1).wait()
+        if start + tile == first:
+            copy_of(k_hbm, k_ref, k_sem, head, 1).wait()
+        ahead = scores_of(start + tile) if start + tile < length else None
+        weights = jnp.exp2((scores - top) * scale)
+        share = jnp.sum(weights, axis=0, keepdims=True)
+        product = product_of(weights, start)
+        if start == 0:
+            total = share
+            acc_ref[...] = product
         else:
-            total = part
-        top, scores = new, ahead
-        if k + block < length:
-            acc_ref[span] = product
-            continue
-        out = (product / total).astype(BF16)
-        lse = top * scale + jnp.log2(total)
-        lse_ref[head, span] = jnp.broadcast_to(lse, (chunk * rows, lse_ref.shape[2]))
-        for i in range(chunk):
-            o_ref[c + i, pl.ds(head * rows, rows), :] = out[i * rows : (i + 1) * rows]
+            total = total + share
+            acc_ref[...] = acc_ref[...] + product
+        scores = ahead
+    top_ref[...] = top
+    total_ref[...] = total
+
+    unsafe = jnp.max(jnp.where(total <= SAFE_TOTAL, 0.0, 1.0))
+
+    @pl.when(unsafe > 0.0)
+    def _():
+        top_ref[...] = jnp.full_like(top_ref, -1e30)
+        total_ref[...] = jnp.zeros_like(total_ref)
+        acc_ref[...] = jnp.zeros_like(acc_ref)
+
+        def step(index, carry):
+            start = pl.multiple_of(index * tile, tile)
+            scores = scores_of(start)
+            old = top_ref[...]
+            new = jnp.maximum(old, jnp.max(scores, axis=0, keepdims=True))
+            factor = jnp.exp2((old - new) * scale)
+            weights = jnp.exp2((scores - new) * scale)
+            total_ref[...] = total_ref[...] * factor + jnp.sum(weights, axis=0, keepdims=True)
+            acc_ref[...] = acc_ref[...] * factor + product_of(weights, start)
+            top_ref[...] = new
+            return carry
+
+        lax.fori_loop(0, length // tile, step, 0)
+
+    out = (acc_ref[...] / total_ref[...]).T.astype(BF16)
+    lse_ref[head] = jnp.broadcast_to(
+        top_ref[...] * scale + jnp.log2(total_ref[...]), lse_ref.shape[1:]
+    )
+    for c in range(sources):
+        o_ref[c, pl.ds(head * rows, rows), :] = out[c * rows : (c + 1) * rows]
 
     @pl.when(head == heads - 1)
     def _():
         for c in range(sources):
-            column = jnp.concatenate(
-                [lse_ref[h, c * rows : (c + 1) * rows, :] for h in range(heads)], axis=0
+            row = jnp.concatenate(
+                [lse_ref[h, :, c * rows : (c + 1) * rows] for h in range(heads)], axis=1
             )
-            row = column.T[0:8]
             high = row.astype(BF16).astype(F32)
             middle = (row - high).astype(BF16).astype(F32)
             low = row - high - middle
             place = lax.broadcasted_iota(jnp.int32, row.shape, 0)
             stats = jnp.where(place == 0, high, jnp.where(place == 1, middle, low))
-            o_ref[c, pl.ds(heads * rows, 8), :] = stats.astype(BF16)
+            o_ref[c, heads * rows : heads * rows + 8, :] = stats.astype(BF16)
 
 
 def prefix_attention(q, keys, values, scale):
     sources, sessions, local_heads, dim = q.shape
     heads, length, _ = keys.shape
     rows = sessions * local_heads // heads
-    block = length // 2
     total_rows = sources * rows
     return pl.pallas_call(
-        functools.partial(prefix_kernel, scale, 2, block),
+        functools.partial(prefix_kernel, scale, length // 12, length // 6),
         grid=(heads,),
         in_specs=[
             pl.BlockSpec(q.shape, lambda h: (0, 0, 0, 0)),
@@ -113,10 +140,12 @@
             pltpu.VMEM((heads, total_rows, dim), BF16),
             pltpu.VMEM(keys.shape, BF16),
             pltpu.VMEM(values.shape, BF16),
-            pltpu.VMEM((total_rows, dim), F32),
-            pltpu.VMEM((heads, total_rows, 128), F32),
-            pltpu.SemaphoreType.DMA((heads, length // block)),
-            pltpu.SemaphoreType.DMA((heads, length // block)),
+            pltpu.VMEM((dim, total_rows), F32),
+            pltpu.VMEM((1, total_rows), F32),
+            pltpu.VMEM((1, total_rows), F32),
+            pltpu.VMEM((heads, 8, total_rows), F32),
+            pltpu.SemaphoreType.DMA((heads, 2)),
+            pltpu.SemaphoreType.DMA((heads, 2)),
         ],
         compiler_params=pltpu.CompilerParams(
             dimension_semantics=("arbitrary",), vmem_limit_bytes=32 << 20
@@ -274,6 +303,27 @@
     )(parts)
 
 
+def spread_kernel(q_ref, out_ref, sem):
+    copies = [
+        pltpu.make_async_copy(q_ref, out_ref.at[c], sem.at[c]) for c in range(out_ref.shape[0])
+    ]
+    for copy in copies:
+        copy.start()
+    for copy in copies:
+        copy.wait()
+
+
+def spread(queries, copies):
+    return pl.pallas_call(
+        spread_kernel,
+        in_specs=[pl.BlockSpec(memory_space=pl.ANY)],
+        out_specs=pl.BlockSpec(memory_space=pl.ANY),
+        out_shape=jax.ShapeDtypeStruct((copies,) + queries.shape, queries.dtype),
+        scratch_shapes=[pltpu.SemaphoreType.DMA((copies,))],
+        name="spread_queries",
+    )(queries)
+
+
 def per_device(queries, prefix_keys, prefix_values, suffix_keys, suffix_values, lengths, out_weight):
     sessions, local_heads, dim = queries.shape
     kv_local = prefix_keys.shape[0]
@@ -283,8 +333,7 @@
     wide = lax.axis_size("x")
     low = lax.axis_size("yl")
 
-    spread = jnp.broadcast_to(queries[None], (ctx,) + queries.shape)
-    gathered = lax.all_to_all(spread, "ctx", 0, 0, tiled=False)
+    gathered = lax.all_to_all(spread(queries, ctx), "ctx", 0, 0, tiled=False)
     weights = [out_weight]
     for k in range(1, wide):
         pairs = [(x, (x + k) % wide) for x in range(wide)]

time: 83 us -> 87.8 us (1.058)
  Pallas kernels: 16.8 us -> 23.2 us
  local copies, waits for them, and re-layouts: 1.52 us -> 0.01 us
    pallas_call x1 -> x2, Pallas kernels: 11.3 us -> 17.8 us  [the longest x1 9.11 us: spread(): pl.pallas_call(spread_kernel, in_specs=[pl.BlockSpec(memory_space=pl.ANY)...]
    broadcast_in_dim x1 -> x0, local copies, waits for them, and re-layouts: 1.5 us -> none  [per_device(): spread = jnp.broadcast_to(queries[None], (ctx,) + queries.shape)]
  transfers between devices with their start and end apart: 5 -> 5, of which waited for: 2 -> 2; matrix products, arithmetic and copies ran while one was open for 0% -> 0% of each run, Pallas kernels for 19% -> 15%
where the time goes in v6:
time: 87.8 us; the launch traced here: 87.5 us
  blocking collectives  35.1 us (40%)
  Pallas kernels  23.2 us (26%)
  starting transfers between devices  17.9 us (20%)
  waiting for transfers between devices  11.2 us (13%)
    all_to_all x1, blocking collectives, per_device(): lax.all_to_all(partial_out, ('yh', 'core', 'x'), 0, 0, tiled=True)  19.3 us
    all_to_all x1, blocking collectives, per_device(): everyone = lax.all_to_all(everyone, ('ctx', 'yl'), 0, 0, tiled=True)  15.8 us
    pallas_call x1, Pallas kernels, spread(): pl.pallas_call(spread_kernel, in_specs=[pl.BlockSpec(memory_space=pl.ANY)...  9.11 us
    all_to_all x1, starting transfers between devices, per_device(): gathered = lax.all_to_all(spread(queries, ctx), 'ctx', 0, 0, tiled=False)  9.03 us
    pallas_call x1, Pallas kernels, prefix_attention(): pl.pallas_call(functools.partial(prefix_kernel, scale, length // 12, leng...  8.64 us
    all_to_all x1, waiting for transfers between devices, per_device(): parts = lax.all_to_all(parts, 'ctx', 0, 0, tiled=True)  6.22 us
    ppermute x3, starting transfers between devices, per_device(): weights.append(lax.ppermute(out_weight, 'x', pairs))  5.42 us
    all_to_all x1, waiting for transfers between devices, per_device(): gathered = lax.all_to_all(spread(queries, ctx), 'ctx', 0, 0, tiled=False)  4.94 us
  transfers between devices with their start and end apart: 5, of which 2 were waited for; matrix products, arithmetic and copies ran while one was open for 0% of the time, Pallas kernels for 15%

profile of v6, /device:TPU:1, one launch (start us, length us, event | category | flops | bytes accessed | tf_op | source)
XLA Modules:
  0.0 87.5 jit_solution(9925325690587898942)
XLA Ops:
  0.0 9.1 %spread_queries.1 = bf16[8,8,16,128]{3,2,1,0:T(8,128)(2,1)} custom-call(bf16[8,16,128]{2,1,0:T(8,128)(2,1)} %q_ref.2), custom_call_target="tpu_custom_call" | custom-call | tf_op jit(solution)/shard_map/spread_queries/pallas_call | solution.py:317
  9.1 9.0 %all-to-all-start = ((bf16[8,8,16,128]{3,2,1,0:T(8,128)(2,1)}), bf16[8,8,16,128]{3,2,1,0:T(8,128)(2,1)S(1)}, u32[]{:S(2)}, u32[]{:S(2)}) async-start(bf16[8,8,16,128]{3,2,1,0:T(8,128)(2,1)} %spread_queries.1), calls=%async_computation | async-start | bytes 524288 | tf_op jit(solution)/shard_map/all_to_all | solution.py:336
  18.1 2.7 %collective-permute-start.1 = (bf16[2048,128]{1,0:T(8,128)(2,1)}, bf16[2048,128]{1,0:T(8,128)(2,1)S(1)}, u32[]{:S(2)}, u32[]{:S(2)}) collective-permute-start(bf16[2048,128]{1,0:T(8,128)(2,1)} %refs_0_), channel_id=1, source_target_pairs={{0,2},{1,3},{2,0},{3,1},{4,6},{5,7},{6,4},{7,5},{8,10},{9,11},{10,... | collective-permute-start | bytes 1572872 | tf_op jit(solution)/shard_map/ppermute | solution.py:340
  20.9 0.3 collective-permute-start
  21.2 2.4 %collective-permute-start.2 = (bf16[2048,128]{1,0:T(8,128)(2,1)}, bf16[2048,128]{1,0:T(8,128)(2,1)S(1)}, u32[]{:S(2)}, u32[]{:S(2)}) collective-permute-start(bf16[2048,128]{1,0:T(8,128)(2,1)} %refs_0_), channel_id=1, source_target_pairs={{0,3},{1,0},{2,1},{3,2},{4,7},{5,4},{6,5},{7,6},{8,11},{9,8},{10,9... | collective-permute-start | bytes 1572872 | tf_op jit(solution)/shard_map/ppermute | solution.py:340
  23.6 0.0 copy-start.1
  23.6 0.0 copy-start.2
  23.6 4.9 %all-to-all-done.all_q_ref = bf16[8,8,16,128]{3,2,1,0:T(8,128)(2,1)S(1)} async-done(((bf16[8,8,16,128]{3,2,1,0:T(8,128)(2,1)}), bf16[8,8,16,128]{3,2,1,0:T(8,128)(2,1)S(1)}, u32[]{:S(2)}, u32[]{:S(2)}) %all-to-all-start) | async-done | bytes 262176 | tf_op jit(solution)/shard_map/all_to_all | solution.py:336
  28.5 8.6 %prefix_attention.1 = bf16[8,136,128]{2,1,0:T(8,128)(2,1)} custom-call(bf16[8,8,16,128]{3,2,1,0:T(8,128)(2,1)S(1)} %all-to-all-done.all_q_ref, bf16[2,6144,128]{2,1,0:T(8,128)(2,1)} %k_hbm.1, bf16[2,6144,128]{2,1,0:T(8,128)(2,1)} %v_hbm.1), custom_call_target="tpu_custom_call" | custom-call | flops 3221225472 | bytes 6291456 | tf_op jit(solution)/shard_map/prefix_attention/pallas_call | solution.py:129
  37.2 3.4 %all-to-all-start.1 = ((bf16[8,136,128]{2,1,0:T(8,128)(2,1)}), bf16[8,136,128]{2,1,0:T(8,128)(2,1)S(1)}, u32[]{:S(2)}, u32[]{:S(2)}) async-start(bf16[8,136,128]{2,1,0:T(8,128)(2,1)} %prefix_attention.1), calls=%async_computation.1 | async-start | bytes 557056 | tf_op jit(solution)/shard_map/all_to_all | solution.py:345
  40.6 0.0 copy-done.1
  40.6 0.0 copy-done.2
  40.6 0.0 copy-start
  40.6 3.3 %suffix_attention.1 = (f32[128,128]{1,0:T(8,128)S(1)}, f32[128,128]{1,0:T(8,128)S(1)}) custom-call(s32[8]{0:T(128)S(1)} %copy-done.2, bf16[8,16,128]{2,1,0:T(8,128)(2,1)S(1)} %copy-done.1, bf16[8,2,512,128]{3,2,1,0:T(8,128)(2,1)} %k_ref.1, bf16[8,2,512,128]{3,2,1,0:T(8,128)(2,1)} %v_ref.1), custom_call_target="tpu_custom_call" | custom-call | flops 33554432 | bytes 4194304 | tf_op jit(solution)/shard_map/suffix_attention/pallas_call | solution.py:197
  44.0 6.2 %all-to-all-done.1.parts_ref = bf16[8,136,128]{2,1,0:T(8,128)(2,1)S(1)} async-done(((bf16[8,136,128]{2,1,0:T(8,128)(2,1)}), bf16[8,136,128]{2,1,0:T(8,128)(2,1)S(1)}, u32[]{:S(2)}, u32[]{:S(2)}) %all-to-all-start.1) | async-done | bytes 278560 | tf_op jit(solution)/shard_map/all_to_all | solution.py:345
  50.2 0.8 merge_shards.1
  51.0 0.0 collective-permute-done.1.refs_2_
  51.0 0.0 collective-permute-done.refs_1_
  51.0 0.0 collective-permute-done.2.refs_3_
  51.0 15.8 %all_to_all.20 = bf16[16,8,2048]{2,1,0:T(8,128)(2,1)S(1)} all-to-all(bf16[16,8,2048]{2,1,0:T(8,128)(2,1)S(1)} %merge_shards.1), channel_id=1, replica_groups=mesh['ctx'=8,'yh'=2,'core'=2,'yl'=2,'x'=4] {'ctx','yl'}, dimensions={0} | all-to-all | bytes 1048576 | tf_op jit(solution)/shard_map/all_to_all | solution.py:351
  66.8 0.0 copy-done
  66.8 0.7 project.1
  67.5 19.3 %all_to_all.21 = bf16[16,32,128]{2,1,0:T(8,128)(2,1)S(1)} all-to-all(bf16[16,32,128]{2,1,0:T(8,128)(2,1)S(1)} %bitcast.6), channel_id=1, replica_groups=mesh['ctx'=8,'yh'=2,'core'=2,'yl'=2,'x'=4] {'yh','core','x'}, dimensions={0} | all-to-all | bytes 262144 | tf_op jit(solution)/shard_map/all_to_all | solution.py:355
  86.8 0.6 sum_heads.1
Async XLA Ops:
  9.1 19.4 %all-to-all-start = ((bf16[8,8,16,128]{3,2,1,0:T(8,128)(2,1)}), bf16[8,8,16,128]{3,2,1,0:T(8,128)(2,1)S(1)}, u32[]{:S(2)}, u32[]{:S(2)}) async-start(bf16[8,8,16,128]{3,2,1,0:T(8,128)(2,1)} %spread_queries.1), calls=%async_computation | async-start | bytes 524288 | tf_op jit(solution)/shard_map/all_to_all | solution.py:336
  18.1 32.9 %collective-permute-start.1 = (bf16[2048,128]{1,0:T(8,128)(2,1)}, bf16[2048,128]{1,0:T(8,128)(2,1)S(1)}, u32[]{:S(2)}, u32[]{:S(2)}) collective-permute-start(bf16[2048,128]{1,0:T(8,128)(2,1)} %refs_0_), channel_id=1, source_target_pairs={{0,2},{1,3},{2,0},{3,1},{4,6},{5,7},{6,4},{7,5},{8,10},{9,11},{10,... | collective-permute-start | bytes 1572872 | tf_op jit(solution)/shard_map/ppermute | solution.py:340
  20.9 30.1 %collective-permute-start = (bf16[2048,128]{1,0:T(8,128)(2,1)}, bf16[2048,128]{1,0:T(8,128)(2,1)S(1)}, u32[]{:S(2)}, u32[]{:S(2)}) collective-permute-start(bf16[2048,128]{1,0:T(8,128)(2,1)} %refs_0_), channel_id=1, source_target_pairs={{0,1},{1,2},{2,3},{3,0},{4,5},{5,6},{6,7},{7,4},{8,9},{9,10},{10,1... | collective-permute-start | bytes 1572872 | tf_op jit(solution)/shard_map/ppermute | solution.py:340
  21.2 29.8 %collective-permute-start.2 = (bf16[2048,128]{1,0:T(8,128)(2,1)}, bf16[2048,128]{1,0:T(8,128)(2,1)S(1)}, u32[]{:S(2)}, u32[]{:S(2)}) collective-permute-start(bf16[2048,128]{1,0:T(8,128)(2,1)} %refs_0_), channel_id=1, source_target_pairs={{0,3},{1,0},{2,1},{3,2},{4,7},{5,4},{6,5},{7,6},{8,11},{9,8},{10,9... | collective-permute-start | bytes 1572872 | tf_op jit(solution)/shard_map/ppermute | solution.py:340
  23.6 17.0 %copy-start.1 = (bf16[8,16,128]{2,1,0:T(8,128)(2,1)S(1)}, bf16[8,16,128]{2,1,0:T(8,128)(2,1)}, u32[]{:S(2)}) copy-start(bf16[8,16,128]{2,1,0:T(8,128)(2,1)} %q_ref.2) | copy-start | bytes 98308
  23.6 17.0 %copy-start.2 = (s32[8]{0:T(128)S(1)}, s32[8]{0:T(128)}, u32[]{:S(2)}) copy-start(s32[8]{0:T(128)} %lengths_ref.1) | copy-start | bytes 100
  37.2 13.0 %all-to-all-start.1 = ((bf16[8,136,128]{2,1,0:T(8,128)(2,1)}), bf16[8,136,128]{2,1,0:T(8,128)(2,1)S(1)}, u32[]{:S(2)}, u32[]{:S(2)}) async-start(bf16[8,136,128]{2,1,0:T(8,128)(2,1)} %prefix_attention.1), calls=%async_computation.1 | async-start | bytes 557056 | tf_op jit(solution)/shard_map/all_to_all | solution.py:345
  40.6 26.2 %copy-start = (bf16[2048,128]{1,0:T(8,128)(2,1)S(1)}, bf16[2048,128]{1,0:T(8,128)(2,1)}, u32[]{:S(2)}) copy-start(bf16[2048,128]{1,0:T(8,128)(2,1)} %refs_0_) | copy-start | bytes 1572868

commit v7 on v6

--- a/solution.py
+++ b/solution.py
@@ -303,23 +303,16 @@
     )(parts)
 
 
-def spread_kernel(q_ref, out_ref, sem):
-    copies = [
-        pltpu.make_async_copy(q_ref, out_ref.at[c], sem.at[c]) for c in range(out_ref.shape[0])
-    ]
-    for copy in copies:
-        copy.start()
-    for copy in copies:
-        copy.wait()
+def spread_kernel(q_ref, out_ref):
+    q = q_ref[...]
+    for c in range(out_ref.shape[0]):
+        out_ref[c] = q
 
 
 def spread(queries, copies):
     return pl.pallas_call(
         spread_kernel,
-        in_specs=[pl.BlockSpec(memory_space=pl.ANY)],
-        out_specs=pl.BlockSpec(memory_space=pl.ANY),
         out_shape=jax.ShapeDtypeStruct((copies,) + queries.shape, queries.dtype),
-        scratch_shapes=[pltpu.SemaphoreType.DMA((copies,))],
         name="spread_queries",
     )(queries)
 

time: 87.8 us -> 80.3 us (0.915)
  Pallas kernels: 23.2 us -> 15.6 us
    pallas_call x1, Pallas kernels: 9.11 us -> 1.5 us  [spread(): pl.pallas_call(spread_kernel, out_shape=jax.ShapeDtypeStruct((copies,) +...]
  transfers between devices with their start and end apart: 5 -> 5, of which waited for: 2 -> 2; matrix products, arithmetic and copies ran while one was open for 0% -> 0% of each run, Pallas kernels for 15% -> 16%
where the time goes in v7:
time: 80.3 us; the launch traced here: 79.8 us
  blocking collectives  35.1 us (44%)
  starting transfers between devices  17.9 us (22%)
  Pallas kernels  15.6 us (19%)
  waiting for transfers between devices  11.2 us (14%)
    all_to_all x1, blocking collectives, per_device(): lax.all_to_all(partial_out, ('yh', 'core', 'x'), 0, 0, tiled=True)  19.3 us
    all_to_all x1, blocking collectives, per_device(): everyone = lax.all_to_all(everyone, ('ctx', 'yl'), 0, 0, tiled=True)  15.8 us
    all_to_all x1, starting transfers between devices, per_device(): gathered = lax.all_to_all(spread(queries, ctx), 'ctx', 0, 0, tiled=False)  9.01 us
    pallas_call x1, Pallas kernels, prefix_attention(): pl.pallas_call(functools.partial(prefix_kernel, scale, length // 12, leng...  8.64 us
    all_to_all x1, waiting for transfers between devices, per_device(): parts = lax.all_to_all(parts, 'ctx', 0, 0, tiled=True)  6.22 us
    ppermute x3, starting transfers between devices, per_device(): weights.append(lax.ppermute(out_weight, 'x', pairs))  5.42 us
    all_to_all x1, waiting for transfers between devices, per_device(): gathered = lax.all_to_all(spread(queries, ctx), 'ctx', 0, 0, tiled=False)  4.94 us
    all_to_all x1, starting transfers between devices, per_device(): parts = lax.all_to_all(parts, 'ctx', 0, 0, tiled=True)  3.43 us
  transfers between devices with their start and end apart: 5, of which 2 were waited for; matrix products, arithmetic and copies ran while one was open for 0% of the time, Pallas kernels for 16%

profile of v7, /device:TPU:1, one launch (start us, length us, event | category | flops | bytes accessed | tf_op | source)
XLA Modules:
  0.0 79.8 jit_solution(13268927140216896882)
XLA Ops:
  0.0 1.5 %spread_queries.1 = bf16[8,8,16,128]{3,2,1,0:T(8,128)(2,1)} custom-call(bf16[8,16,128]{2,1,0:T(8,128)(2,1)} %q_ref.2), custom_call_target="tpu_custom_call" | custom-call | tf_op jit(solution)/shard_map/spread_queries/pallas_call | solution.py:313
  1.5 9.0 %all-to-all-start = ((bf16[8,8,16,128]{3,2,1,0:T(8,128)(2,1)}), bf16[8,8,16,128]{3,2,1,0:T(8,128)(2,1)S(1)}, u32[]{:S(2)}, u32[]{:S(2)}) async-start(bf16[8,8,16,128]{3,2,1,0:T(8,128)(2,1)} %spread_queries.1), calls=%async_computation | async-start | bytes 524288 | tf_op jit(solution)/shard_map/all_to_all | solution.py:329
  10.5 2.7 %collective-permute-start.1 = (bf16[2048,128]{1,0:T(8,128)(2,1)}, bf16[2048,128]{1,0:T(8,128)(2,1)S(1)}, u32[]{:S(2)}, u32[]{:S(2)}) collective-permute-start(bf16[2048,128]{1,0:T(8,128)(2,1)} %refs_0_), channel_id=1, source_target_pairs={{0,2},{1,3},{2,0},{3,1},{4,6},{5,7},{6,4},{7,5},{8,10},{9,11},{10,... | collective-permute-start | bytes 1572872 | tf_op jit(solution)/shard_map/ppermute | solution.py:333
  13.3 0.3 collective-permute-start
  13.6 2.4 %collective-permute-start.2 = (bf16[2048,128]{1,0:T(8,128)(2,1)}, bf16[2048,128]{1,0:T(8,128)(2,1)S(1)}, u32[]{:S(2)}, u32[]{:S(2)}) collective-permute-start(bf16[2048,128]{1,0:T(8,128)(2,1)} %refs_0_), channel_id=1, source_target_pairs={{0,3},{1,0},{2,1},{3,2},{4,7},{5,4},{6,5},{7,6},{8,11},{9,8},{10,9... | collective-permute-start | bytes 1572872 | tf_op jit(solution)/shard_map/ppermute | solution.py:333
  15.9 0.0 copy-start.1
  15.9 0.0 copy-start.2
  15.9 4.9 %all-to-all-done.all_q_ref = bf16[8,8,16,128]{3,2,1,0:T(8,128)(2,1)S(1)} async-done(((bf16[8,8,16,128]{3,2,1,0:T(8,128)(2,1)}), bf16[8,8,16,128]{3,2,1,0:T(8,128)(2,1)S(1)}, u32[]{:S(2)}, u32[]{:S(2)}) %all-to-all-start) | async-done | bytes 262176 | tf_op jit(solution)/shard_map/all_to_all | solution.py:329
  20.9 8.6 %prefix_attention.1 = bf16[8,136,128]{2,1,0:T(8,128)(2,1)} custom-call(bf16[8,8,16,128]{3,2,1,0:T(8,128)(2,1)S(1)} %all-to-all-done.all_q_ref, bf16[2,6144,128]{2,1,0:T(8,128)(2,1)} %k_hbm.1, bf16[2,6144,128]{2,1,0:T(8,128)(2,1)} %v_hbm.1), custom_call_target="tpu_custom_call" | custom-call | flops 3221225472 | bytes 6291456 | tf_op jit(solution)/shard_map/prefix_attention/pallas_call | solution.py:129
  29.5 3.4 %all-to-all-start.1 = ((bf16[8,136,128]{2,1,0:T(8,128)(2,1)}), bf16[8,136,128]{2,1,0:T(8,128)(2,1)S(1)}, u32[]{:S(2)}, u32[]{:S(2)}) async-start(bf16[8,136,128]{2,1,0:T(8,128)(2,1)} %prefix_attention.1), calls=%async_computation.1 | async-start | bytes 557056 | tf_op jit(solution)/shard_map/all_to_all | solution.py:338
  33.0 0.0 copy-done.1
  33.0 0.0 copy-done.2
  33.0 0.0 copy-start
  33.0 3.3 %suffix_attention.1 = (f32[128,128]{1,0:T(8,128)S(1)}, f32[128,128]{1,0:T(8,128)S(1)}) custom-call(s32[8]{0:T(128)S(1)} %copy-done.2, bf16[8,16,128]{2,1,0:T(8,128)(2,1)S(1)} %copy-done.1, bf16[8,2,512,128]{3,2,1,0:T(8,128)(2,1)} %k_ref.1, bf16[8,2,512,128]{3,2,1,0:T(8,128)(2,1)} %v_ref.1), custom_call_target="tpu_custom_call" | custom-call | flops 33554432 | bytes 4194304 | tf_op jit(solution)/shard_map/suffix_attention/pallas_call | solution.py:197
  36.3 6.2 %all-to-all-done.1.parts_ref = bf16[8,136,128]{2,1,0:T(8,128)(2,1)S(1)} async-done(((bf16[8,136,128]{2,1,0:T(8,128)(2,1)}), bf16[8,136,128]{2,1,0:T(8,128)(2,1)S(1)}, u32[]{:S(2)}, u32[]{:S(2)}) %all-to-all-start.1) | async-done | bytes 278560 | tf_op jit(solution)/shard_map/all_to_all | solution.py:338
  42.5 0.8 %merge_shards.1 = bf16[16,8,2048]{2,1,0:T(8,128)(2,1)S(1)} custom-call(bf16[8,136,128]{2,1,0:T(8,128)(2,1)S(1)} %all-to-all-done.1.parts_ref, f32[128,128]{1,0:T(8,128)S(1)} %get-tuple-element.18.suffix_ref, f32[128,128]{1,0:T(8,128)S(1)} %get-tuple-element.19.suffix_lse_ref), custom_call_target="tpu_custom_call" | custom-call | tf_op jit(solution)/shard_map/merge_shards/pallas_call | solution.py:256
  43.4 0.0 collective-permute-done.1.refs_2_
  43.4 0.0 collective-permute-done.refs_1_
  43.4 0.0 collective-permute-done.2.refs_3_
  43.4 15.8 %all_to_all.20 = bf16[16,8,2048]{2,1,0:T(8,128)(2,1)S(1)} all-to-all(bf16[16,8,2048]{2,1,0:T(8,128)(2,1)S(1)} %merge_shards.1), channel_id=1, replica_groups=mesh['ctx'=8,'yh'=2,'core'=2,'yl'=2,'x'=4] {'ctx','yl'}, dimensions={0} | all-to-all | bytes 1048576 | tf_op jit(solution)/shard_map/all_to_all | solution.py:344
  59.2 0.0 copy-done
  59.2 0.7 project.1
  59.9 19.3 %all_to_all.21 = bf16[16,32,128]{2,1,0:T(8,128)(2,1)S(1)} all-to-all(bf16[16,32,128]{2,1,0:T(8,128)(2,1)S(1)} %bitcast.6), channel_id=1, replica_groups=mesh['ctx'=8,'yh'=2,'core'=2,'yl'=2,'x'=4] {'yh','core','x'}, dimensions={0} | all-to-all | bytes 262144 | tf_op jit(solution)/shard_map/all_to_all | solution.py:348
  79.2 0.6 sum_heads.1
Async XLA Ops:
  1.5 19.4 %all-to-all-start = ((bf16[8,8,16,128]{3,2,1,0:T(8,128)(2,1)}), bf16[8,8,16,128]{3,2,1,0:T(8,128)(2,1)S(1)}, u32[]{:S(2)}, u32[]{:S(2)}) async-start(bf16[8,8,16,128]{3,2,1,0:T(8,128)(2,1)} %spread_queries.1), calls=%async_computation | async-start | bytes 524288 | tf_op jit(solution)/shard_map/all_to_all | solution.py:329
  10.5 32.9 %collective-permute-start.1 = (bf16[2048,128]{1,0:T(8,128)(2,1)}, bf16[2048,128]{1,0:T(8,128)(2,1)S(1)}, u32[]{:S(2)}, u32[]{:S(2)}) collective-permute-start(bf16[2048,128]{1,0:T(8,128)(2,1)} %refs_0_), channel_id=1, source_target_pairs={{0,2},{1,3},{2,0},{3,1},{4,6},{5,7},{6,4},{7,5},{8,10},{9,11},{10,... | collective-permute-start | bytes 1572872 | tf_op jit(solution)/shard_map/ppermute | solution.py:333
  13.3 30.1 %collective-permute-start = (bf16[2048,128]{1,0:T(8,128)(2,1)}, bf16[2048,128]{1,0:T(8,128)(2,1)S(1)}, u32[]{:S(2)}, u32[]{:S(2)}) collective-permute-start(bf16[2048,128]{1,0:T(8,128)(2,1)} %refs_0_), channel_id=1, source_target_pairs={{0,1},{1,2},{2,3},{3,0},{4,5},{5,6},{6,7},{7,4},{8,9},{9,10},{10,1... | collective-permute-start | bytes 1572872 | tf_op jit(solution)/shard_map/ppermute | solution.py:333
  13.6 29.8 %collective-permute-start.2 = (bf16[2048,128]{1,0:T(8,128)(2,1)}, bf16[2048,128]{1,0:T(8,128)(2,1)S(1)}, u32[]{:S(2)}, u32[]{:S(2)}) collective-permute-start(bf16[2048,128]{1,0:T(8,128)(2,1)} %refs_0_), channel_id=1, source_target_pairs={{0,3},{1,0},{2,1},{3,2},{4,7},{5,4},{6,5},{7,6},{8,11},{9,8},{10,9... | collective-permute-start | bytes 1572872 | tf_op jit(solution)/shard_map/ppermute | solution.py:333
  15.9 17.0 %copy-start.1 = (bf16[8,16,128]{2,1,0:T(8,128)(2,1)S(1)}, bf16[8,16,128]{2,1,0:T(8,128)(2,1)}, u32[]{:S(2)}) copy-start(bf16[8,16,128]{2,1,0:T(8,128)(2,1)} %q_ref.2) | copy-start | bytes 98308
  15.9 17.0 %copy-start.2 = (s32[8]{0:T(128)S(1)}, s32[8]{0:T(128)}, u32[]{:S(2)}) copy-start(s32[8]{0:T(128)} %lengths_ref.1) | copy-start | bytes 100
  29.5 13.0 %all-to-all-start.1 = ((bf16[8,136,128]{2,1,0:T(8,128)(2,1)}), bf16[8,136,128]{2,1,0:T(8,128)(2,1)S(1)}, u32[]{:S(2)}, u32[]{:S(2)}) async-start(bf16[8,136,128]{2,1,0:T(8,128)(2,1)} %prefix_attention.1), calls=%async_computation.1 | async-start | bytes 557056 | tf_op jit(solution)/shard_map/all_to_all | solution.py:338
  33.0 26.2 %copy-start = (bf16[2048,128]{1,0:T(8,128)(2,1)S(1)}, bf16[2048,128]{1,0:T(8,128)(2,1)}, u32[]{:S(2)}) copy-start(bf16[2048,128]{1,0:T(8,128)(2,1)} %refs_0_) | copy-start | bytes 1572868

commit v8 on v6

--- a/solution.py
+++ b/solution.py
@@ -22,7 +22,7 @@
 
 
 def prefix_kernel(
-    scale, tile, first, all_q_ref, k_hbm, v_hbm, o_ref, q_ref, k_ref, v_ref, acc_ref, top_ref,
+    scale, tile, first, all_q_ref, k_first, v_first, k_hbm, v_hbm, o_ref, q_ref, k_ref, v_ref, acc_ref, top_ref,
     total_ref, lse_ref, k_sem, v_sem,
 ):
     head = pl.program_id(0)
@@ -30,7 +30,7 @@
     heads, length, _ = k_ref.shape
     group = local_heads // heads
     rows = sessions * group
-    parts = [(0, first), (first, length - first)]
+    parts = [(tile, first - tile), (first, length - first)]
 
     def copy_of(source, target, sem, h, part):
         span = pl.ds(*parts[part])
@@ -46,19 +46,22 @@
             part = all_q_ref[:, :, h * group : (h + 1) * group, :]
             q_ref[h] = part.reshape(sources * rows, dim)
 
-    def scores_of(start):
-        keys = k_ref[head, pl.ds(start, tile), :]
+    def scores_of(start, keys=None):
+        if keys is None:
+            keys = k_ref[head, pl.ds(start, tile), :]
         return lax.dot_general(keys, q_ref[head], NT, preferred_element_type=F32)
 
-    def product_of(weights, start):
-        values = v_ref[head, pl.ds(start, tile), :]
+    def product_of(weights, start, values=None):
+        if values is None:
+            values = v_ref[head, pl.ds(start, tile), :]
         return lax.dot_general(values, weights.astype(BF16), TN, preferred_element_type=F32)
 
-    copy_of(k_hbm, k_ref, k_sem, head, 0).wait()
-    scores = scores_of(0)
+    scores = scores_of(0, k_first[head])
     top = jnp.max(scores, axis=0, keepdims=True)
     for start in range(0, length, tile):
         if start == 0:
+            copy_of(k_hbm, k_ref, k_sem, head, 0).wait()
+        if start == tile:
             copy_of(v_hbm, v_ref, v_sem, head, 0).wait()
         if start == first:
             copy_of(v_hbm, v_ref, v_sem, head, 1).wait()
@@ -67,7 +70,7 @@
         ahead = scores_of(start + tile) if start + tile < length else None
         weights = jnp.exp2((scores - top) * scale)
         share = jnp.sum(weights, axis=0, keepdims=True)
-        product = product_of(weights, start)
+        product = product_of(weights, start, v_first[head] if start == 0 else None)
         if start == 0:
             total = share
             acc_ref[...] = product
@@ -85,6 +88,8 @@
         top_ref[...] = jnp.full_like(top_ref, -1e30)
         total_ref[...] = jnp.zeros_like(total_ref)
         acc_ref[...] = jnp.zeros_like(acc_ref)
+        k_ref[head, :tile] = k_first[head]
+        v_ref[head, :tile] = v_first[head]
 
         def step(index, carry):
             start = pl.multiple_of(index * tile, tile)
@@ -121,16 +126,18 @@
             o_ref[c, heads * rows : heads * rows + 8, :] = stats.astype(BF16)
 
 
-def prefix_attention(q, keys, values, scale):
+def prefix_attention(q, k_first, v_first, keys, values, scale):
     sources, sessions, local_heads, dim = q.shape
     heads, length, _ = keys.shape
     rows = sessions * local_heads // heads
     total_rows = sources * rows
     return pl.pallas_call(
-        functools.partial(prefix_kernel, scale, length // 12, length // 6),
+        functools.partial(prefix_kernel, scale, k_first.shape[1], 2 * k_first.shape[1]),
         grid=(heads,),
         in_specs=[
             pl.BlockSpec(q.shape, lambda h: (0, 0, 0, 0)),
+            pl.BlockSpec(k_first.shape, lambda h: (0, 0, 0)),
+            pl.BlockSpec(v_first.shape, lambda h: (0, 0, 0)),
             pl.BlockSpec(memory_space=pltpu.HBM),
             pl.BlockSpec(memory_space=pltpu.HBM),
         ],
@@ -158,6 +165,8 @@
         name="prefix_attention",
     )(
         q,
+        k_first,
+        v_first,
         pltpu.with_memory_space_constraint(keys, pltpu.HBM),
         pltpu.with_memory_space_constraint(values, pltpu.HBM),
     )
@@ -316,7 +325,7 @@
 def spread(queries, copies):
     return pl.pallas_call(
         spread_kernel,
-        in_specs=[pl.BlockSpec(memory_space=pl.ANY)],
+        in_specs=[pl.BlockSpec(memory_space=pltpu.VMEM)],
         out_specs=pl.BlockSpec(memory_space=pl.ANY),
         out_shape=jax.ShapeDtypeStruct((copies,) + queries.shape, queries.dtype),
         scratch_shapes=[pltpu.SemaphoreType.DMA((copies,))],
@@ -339,7 +348,9 @@
         pairs = [(x, (x + k) % wide) for x in range(wide)]
         weights.append(lax.ppermute(out_weight, "x", pairs))
 
-    parts = prefix_attention(gathered, prefix_keys, prefix_values, scale)
+    tile = prefix_keys.shape[1] // 12
+    k_first, v_first = prefix_keys[:, :tile], prefix_values[:, :tile]
+    parts = prefix_attention(gathered, k_first, v_first, prefix_keys, prefix_values, scale)
     place = lax.axis_index("x").astype(jnp.int32).reshape(1)
     parts, queries, place = lax.optimization_barrier((parts, queries, place))
     parts = lax.all_to_all(parts, "ctx", 0, 0, tiled=True)

time: 87.8 us -> 80.3 us (0.915)
  Pallas kernels: 23.2 us -> 15.6 us
  local copies, waits for them, and re-layouts: 0.01 us -> 1.96 us
  waiting for transfers between devices: 11.2 us -> 9.36 us
    pallas_call x2, Pallas kernels: 17.8 us -> 10.1 us  [the longest x1 8.59 us: prefix_attention(): pl.pallas_call(functools.partial(prefix_kernel, scale, k_first.shape[1],...]
    all_to_all x1, waiting for transfers between devices: 4.94 us -> 2.98 us  [per_device(): gathered = lax.all_to_all(spread(queries, ctx), 'ctx', 0, 0, tiled=False)]
    slice x0 -> x2, local copies, waits for them, and re-layouts: none -> 1.94 us  [per_device(): k_first, v_first = (prefix_keys[:, :tile], prefix_values[:, :tile])]
    all_to_all x1, blocking collectives: 19.3 us -> 18.2 us  [per_device(): lax.all_to_all(partial_out, ('yh', 'core', 'x'), 0, 0, tiled=True)]
  transfers between devices with their start and end apart: 5 -> 5, of which waited for: 2 -> 2; matrix products, arithmetic and copies ran while one was open for 0% -> 2% of each run, Pallas kernels for 15% -> 16%
where the time goes in v8:
time: 80.3 us; the launch traced here: 79.8 us
  blocking collectives  34.7 us (43%)
  starting transfers between devices  18.2 us (23%)
  Pallas kernels  15.6 us (19%)
  waiting for transfers between devices  9.36 us (12%)
  local copies, waits for them, and re-layouts  1.96 us (2%)
    all_to_all x1, blocking collectives, per_device(): lax.all_to_all(partial_out, ('yh', 'core', 'x'), 0, 0, tiled=True)  18.2 us
    all_to_all x1, blocking collectives, per_device(): everyone = lax.all_to_all(everyone, ('ctx', 'yl'), 0, 0, tiled=True)  16.5 us
    all_to_all x1, starting transfers between devices, per_device(): gathered = lax.all_to_all(spread(queries, ctx), 'ctx', 0, 0, tiled=False)  9.03 us
    pallas_call x1, Pallas kernels, prefix_attention(): pl.pallas_call(functools.partial(prefix_kernel, scale, k_first.shape[1],...  8.59 us
    all_to_all x1, waiting for transfers between devices, per_device(): parts = lax.all_to_all(parts, 'ctx', 0, 0, tiled=True)  6.37 us
    ppermute x3, starting transfers between devices, per_device(): weights.append(lax.ppermute(out_weight, 'x', pairs))  5.42 us
    all_to_all x1, starting transfers between devices, per_device(): parts = lax.all_to_all(parts, 'ctx', 0, 0, tiled=True)  3.71 us
    pallas_call x1, Pallas kernels, suffix_attention(): pl.pallas_call(functools.partial(suffix_kernel, scale), grid_spec=pltpu.P...  3.31 us
  transfers between devices with their start and end apart: 5, of which 2 were waited for; matrix products, arithmetic and copies ran while one was open for 2% of the time, Pallas kernels for 16%

profile of v8, /device:TPU:1, one launch (start us, length us, event | category | flops | bytes accessed | tf_op | source)
XLA Modules:
  0.0 79.8 jit_solution(15006592710397575948)
XLA Ops:
  0.0 1.5 %spread_queries.1 = bf16[8,8,16,128]{3,2,1,0:T(8,128)(2,1)} custom-call(bf16[8,16,128]{2,1,0:T(8,128)(2,1)} %q_ref.2), custom_call_target="tpu_custom_call" | custom-call | tf_op jit(solution)/shard_map/spread_queries/pallas_call | solution.py:326
  1.5 9.0 %all-to-all-start = ((bf16[8,8,16,128]{3,2,1,0:T(8,128)(2,1)}), bf16[8,8,16,128]{3,2,1,0:T(8,128)(2,1)S(1)}, u32[]{:S(2)}, u32[]{:S(2)}) async-start(bf16[8,8,16,128]{3,2,1,0:T(8,128)(2,1)} %spread_queries.1), calls=%async_computation | async-start | bytes 524288 | tf_op jit(solution)/shard_map/all_to_all | solution.py:345
  10.6 2.7 %collective-permute-start.1 = (bf16[2048,128]{1,0:T(8,128)(2,1)}, bf16[2048,128]{1,0:T(8,128)(2,1)S(1)}, u32[]{:S(2)}, u32[]{:S(2)}) collective-permute-start(bf16[2048,128]{1,0:T(8,128)(2,1)} %refs_0_), channel_id=1, source_target_pairs={{0,2},{1,3},{2,0},{3,1},{4,6},{5,7},{6,4},{7,5},{8,10},{9,11},{10,... | collective-permute-start | bytes 1572872 | tf_op jit(solution)/shard_map/ppermute | solution.py:349
  13.3 0.3 collective-permute-start
  13.6 2.4 %collective-permute-start.2 = (bf16[2048,128]{1,0:T(8,128)(2,1)}, bf16[2048,128]{1,0:T(8,128)(2,1)S(1)}, u32[]{:S(2)}, u32[]{:S(2)}) collective-permute-start(bf16[2048,128]{1,0:T(8,128)(2,1)} %refs_0_), channel_id=1, source_target_pairs={{0,3},{1,0},{2,1},{3,2},{4,7},{5,4},{6,5},{7,6},{8,11},{9,8},{10,9... | collective-permute-start | bytes 1572872 | tf_op jit(solution)/shard_map/ppermute | solution.py:349
  16.0 1.0 %slice.6.k_first = bf16[2,512,128]{2,1,0:T(8,128)(2,1)S(1)} slice(bf16[2,6144,128]{2,1,0:T(8,128)(2,1)} %k_hbm.1), slice={[0:2], [0:512], [0:128]} | slice | bytes 524288 | tf_op jit(solution)/shard_map/slice | solution.py:352
  17.0 1.0 %slice.7.v_first = bf16[2,512,128]{2,1,0:T(8,128)(2,1)S(1)} slice(bf16[2,6144,128]{2,1,0:T(8,128)(2,1)} %v_hbm.1), slice={[0:2], [0:512], [0:128]} | slice | bytes 524288 | tf_op jit(solution)/shard_map/slice | solution.py:352
  17.9 0.0 copy-start.1
  18.0 0.0 copy-start.2
  18.0 3.0 %all-to-all-done.all_q_ref = bf16[8,8,16,128]{3,2,1,0:T(8,128)(2,1)S(1)} async-done(((bf16[8,8,16,128]{3,2,1,0:T(8,128)(2,1)}), bf16[8,8,16,128]{3,2,1,0:T(8,128)(2,1)S(1)}, u32[]{:S(2)}, u32[]{:S(2)}) %all-to-all-start) | async-done | bytes 262176 | tf_op jit(solution)/shard_map/all_to_all | solution.py:345
  20.9 8.6 %prefix_attention.1 = bf16[8,136,128]{2,1,0:T(8,128)(2,1)} custom-call(bf16[8,8,16,128]{3,2,1,0:T(8,128)(2,1)S(1)} %all-to-all-done.all_q_ref, bf16[2,512,128]{2,1,0:T(8,128)(2,1)S(1)} %slice.6.k_first, bf16[2,512,128]{2,1,0:T(8,128)(2,1)S(1)} %slice.7.v_first, bf16[2,6144,128]{2,1,0:T(8,128)(2,1)} %k_hbm.1, bf16[2,6144,128]{2,1,0:T(8,128)(2,1)} %v_hbm.1), custom_call_target="tpu_custom_call" | custom-call | flops 3221225472 | bytes 6291456 | tf_op jit(solution)/shard_map/prefix_attention/pallas_call | solution.py:134
  29.5 3.7 %all-to-all-start.1 = ((bf16[8,136,128]{2,1,0:T(8,128)(2,1)}), bf16[8,136,128]{2,1,0:T(8,128)(2,1)S(1)}, u32[]{:S(2)}, u32[]{:S(2)}) async-start(bf16[8,136,128]{2,1,0:T(8,128)(2,1)} %prefix_attention.1), calls=%async_computation.1 | async-start | bytes 557056 | tf_op jit(solution)/shard_map/all_to_all | solution.py:356
  33.2 0.0 copy-done.1
  33.3 0.0 copy-done.2
  33.3 0.0 copy-start
  33.3 3.3 %suffix_attention.1 = (f32[128,128]{1,0:T(8,128)S(1)}, f32[128,128]{1,0:T(8,128)S(1)}) custom-call(s32[8]{0:T(128)S(1)} %copy-done.2, bf16[8,16,128]{2,1,0:T(8,128)(2,1)S(1)} %copy-done.1, bf16[8,2,512,128]{3,2,1,0:T(8,128)(2,1)} %k_ref.1, bf16[8,2,512,128]{3,2,1,0:T(8,128)(2,1)} %v_ref.1), custom_call_target="tpu_custom_call" | custom-call | flops 33554432 | bytes 4194304 | tf_op jit(solution)/shard_map/suffix_attention/pallas_call | solution.py:206
  36.6 6.4 %all-to-all-done.1.parts_ref = bf16[8,136,128]{2,1,0:T(8,128)(2,1)S(1)} async-done(((bf16[8,136,128]{2,1,0:T(8,128)(2,1)}), bf16[8,136,128]{2,1,0:T(8,128)(2,1)S(1)}, u32[]{:S(2)}, u32[]{:S(2)}) %all-to-all-start.1) | async-done | bytes 278560 | tf_op jit(solution)/shard_map/all_to_all | solution.py:356
  43.0 0.8 %merge_shards.1 = bf16[16,8,2048]{2,1,0:T(8,128)(2,1)S(1)} custom-call(bf16[8,136,128]{2,1,0:T(8,128)(2,1)S(1)} %all-to-all-done.1.parts_ref, f32[128,128]{1,0:T(8,128)S(1)} %get-tuple-element.18.suffix_ref, f32[128,128]{1,0:T(8,128)S(1)} %get-tuple-element.19.suffix_lse_ref), custom_call_target="tpu_custom_call" | custom-call | tf_op jit(solution)/shard_map/merge_shards/pallas_call | solution.py:265
  43.8 0.0 collective-permute-done.1.refs_2_
  43.8 0.0 collective-permute-done.refs_1_
  43.8 0.0 collective-permute-done.2.refs_3_
  43.8 16.5 %all_to_all.20 = bf16[16,8,2048]{2,1,0:T(8,128)(2,1)S(1)} all-to-all(bf16[16,8,2048]{2,1,0:T(8,128)(2,1)S(1)} %merge_shards.1), channel_id=1, replica_groups=mesh['ctx'=8,'yh'=2,'core'=2,'yl'=2,'x'=4] {'ctx','yl'}, dimensions={0} | all-to-all | bytes 1048576 | tf_op jit(solution)/shard_map/all_to_all | solution.py:362
  60.3 0.0 copy-done
  60.3 0.7 project.1
  61.0 18.2 %all_to_all.21 = bf16[16,32,128]{2,1,0:T(8,128)(2,1)S(1)} all-to-all(bf16[16,32,128]{2,1,0:T(8,128)(2,1)S(1)} %bitcast.6), channel_id=1, replica_groups=mesh['ctx'=8,'yh'=2,'core'=2,'yl'=2,'x'=4] {'yh','core','x'}, dimensions={0} | all-to-all | bytes 262144 | tf_op jit(solution)/shard_map/all_to_all | solution.py:366
  79.2 0.6 sum_heads.1
Async XLA Ops:
  1.5 19.4 %all-to-all-start = ((bf16[8,8,16,128]{3,2,1,0:T(8,128)(2,1)}), bf16[8,8,16,128]{3,2,1,0:T(8,128)(2,1)S(1)}, u32[]{:S(2)}, u32[]{:S(2)}) async-start(bf16[8,8,16,128]{3,2,1,0:T(8,128)(2,1)} %spread_queries.1), calls=%async_computation | async-start | bytes 524288 | tf_op jit(solution)/shard_map/all_to_all | solution.py:345
  10.6 33.2 %collective-permute-start.1 = (bf16[2048,128]{1,0:T(8,128)(2,1)}, bf16[2048,128]{1,0:T(8,128)(2,1)S(1)}, u32[]{:S(2)}, u32[]{:S(2)}) collective-permute-start(bf16[2048,128]{1,0:T(8,128)(2,1)} %refs_0_), channel_id=1, source_target_pairs={{0,2},{1,3},{2,0},{3,1},{4,6},{5,7},{6,4},{7,5},{8,10},{9,11},{10,... | collective-permute-start | bytes 1572872 | tf_op jit(solution)/shard_map/ppermute | solution.py:349
  13.3 30.5 %collective-permute-start = (bf16[2048,128]{1,0:T(8,128)(2,1)}, bf16[2048,128]{1,0:T(8,128)(2,1)S(1)}, u32[]{:S(2)}, u32[]{:S(2)}) collective-permute-start(bf16[2048,128]{1,0:T(8,128)(2,1)} %refs_0_), channel_id=1, source_target_pairs={{0,1},{1,2},{2,3},{3,0},{4,5},{5,6},{6,7},{7,4},{8,9},{9,10},{10,1... | collective-permute-start | bytes 1572872 | tf_op jit(solution)/shard_map/ppermute | solution.py:349
  13.6 30.2 %collective-permute-start.2 = (bf16[2048,128]{1,0:T(8,128)(2,1)}, bf16[2048,128]{1,0:T(8,128)(2,1)S(1)}, u32[]{:S(2)}, u32[]{:S(2)}) collective-permute-start(bf16[2048,128]{1,0:T(8,128)(2,1)} %refs_0_), channel_id=1, source_target_pairs={{0,3},{1,0},{2,1},{3,2},{4,7},{5,4},{6,5},{7,6},{8,11},{9,8},{10,9... | collective-permute-start | bytes 1572872 | tf_op jit(solution)/shard_map/ppermute | solution.py:349
  17.9 15.3 %copy-start.1 = (bf16[8,16,128]{2,1,0:T(8,128)(2,1)S(1)}, bf16[8,16,128]{2,1,0:T(8,128)(2,1)}, u32[]{:S(2)}) copy-start(bf16[8,16,128]{2,1,0:T(8,128)(2,1)} %q_ref.2) | copy-start | bytes 98308
  18.0 15.3 %copy-start.2 = (s32[8]{0:T(128)S(1)}, s32[8]{0:T(128)}, u32[]{:S(2)}) copy-start(s32[8]{0:T(128)} %lengths_ref.1) | copy-start | bytes 100
  29.5 13.4 %all-to-all-start.1 = ((bf16[8,136,128]{2,1,0:T(8,128)(2,1)}), bf16[8,136,128]{2,1,0:T(8,128)(2,1)S(1)}, u32[]{:S(2)}, u32[]{:S(2)}) async-start(bf16[8,136,128]{2,1,0:T(8,128)(2,1)} %prefix_attention.1), calls=%async_computation.1 | async-start | bytes 557056 | tf_op jit(solution)/shard_map/all_to_all | solution.py:356
  33.3 27.0 %copy-start = (bf16[2048,128]{1,0:T(8,128)(2,1)S(1)}, bf16[2048,128]{1,0:T(8,128)(2,1)}, u32[]{:S(2)}) copy-start(bf16[2048,128]{1,0:T(8,128)(2,1)} %refs_0_) | copy-start | bytes 1572868

commit v9 on v8

--- a/solution.py
+++ b/solution.py
@@ -22,14 +22,12 @@
 
 
 def prefix_kernel(
-    scale, tile, first, all_q_ref, k_first, v_first, k_hbm, v_hbm, o_ref, q_ref, k_ref, v_ref, acc_ref, top_ref,
+    scale, tile, first, q_ref, k_first, v_first, k_hbm, v_hbm, o_ref, k_ref, v_ref, acc_ref, top_ref,
     total_ref, lse_ref, k_sem, v_sem,
 ):
     head = pl.program_id(0)
-    sources, sessions, local_heads, dim = all_q_ref.shape
+    sources, _, rows, dim = q_ref.shape
     heads, length, _ = k_ref.shape
-    group = local_heads // heads
-    rows = sessions * group
     parts = [(tile, first - tile), (first, length - first)]
 
     def copy_of(source, target, sem, h, part):
@@ -42,14 +40,13 @@
             for part in range(len(parts)):
                 copy_of(k_hbm, k_ref, k_sem, h, part).start()
                 copy_of(v_hbm, v_ref, v_sem, h, part).start()
-        for h in range(heads):
-            part = all_q_ref[:, :, h * group : (h + 1) * group, :]
-            q_ref[h] = part.reshape(sources * rows, dim)
+
+    queries = q_ref[...].reshape(sources * rows, dim)
 
     def scores_of(start, keys=None):
         if keys is None:
             keys = k_ref[head, pl.ds(start, tile), :]
-        return lax.dot_general(keys, q_ref[head], NT, preferred_element_type=F32)
+        return lax.dot_general(keys, queries, NT, preferred_element_type=F32)
 
     def product_of(weights, start, values=None):
         if values is None:
@@ -127,15 +124,14 @@
 
 
 def prefix_attention(q, k_first, v_first, keys, values, scale):
-    sources, sessions, local_heads, dim = q.shape
-    heads, length, _ = keys.shape
-    rows = sessions * local_heads // heads
+    sources, heads, rows, dim = q.shape
+    length = keys.shape[1]
     total_rows = sources * rows
     return pl.pallas_call(
         functools.partial(prefix_kernel, scale, k_first.shape[1], 2 * k_first.shape[1]),
         grid=(heads,),
         in_specs=[
-            pl.BlockSpec(q.shape, lambda h: (0, 0, 0, 0)),
+            pl.BlockSpec((sources, 1, rows, dim), lambda h: (0, h, 0, 0)),
             pl.BlockSpec(k_first.shape, lambda h: (0, 0, 0)),
             pl.BlockSpec(v_first.shape, lambda h: (0, 0, 0)),
             pl.BlockSpec(memory_space=pltpu.HBM),
@@ -144,7 +140,6 @@
         out_specs=pl.BlockSpec((sources, heads * rows + 8, dim), lambda h: (0, 0, 0)),
         out_shape=jax.ShapeDtypeStruct((sources, heads * rows + 8, dim), BF16),
         scratch_shapes=[
-            pltpu.VMEM((heads, total_rows, dim), BF16),
             pltpu.VMEM(keys.shape, BF16),
             pltpu.VMEM(values.shape, BF16),
             pltpu.VMEM((dim, total_rows), F32),
@@ -312,23 +307,21 @@
     )(parts)
 
 
-def spread_kernel(q_ref, out_ref, sem):
-    copies = [
-        pltpu.make_async_copy(q_ref, out_ref.at[c], sem.at[c]) for c in range(out_ref.shape[0])
-    ]
-    for copy in copies:
-        copy.start()
-    for copy in copies:
-        copy.wait()
-
-
-def spread(queries, copies):
+def spread_kernel(q_ref, out_ref):
+    copies, heads, rows, dim = out_ref.shape
+    group = q_ref.shape[1] // heads
+    for h in range(heads):
+        q = q_ref[:, h * group : (h + 1) * group, :].reshape(rows, dim)
+        for c in range(copies):
+            out_ref[c, h] = q
+
+
+def spread(queries, copies, heads):
+    sessions, local_heads, dim = queries.shape
+    shape = (copies, heads, sessions * local_heads // heads, dim)
     return pl.pallas_call(
         spread_kernel,
-        in_specs=[pl.BlockSpec(memory_space=pltpu.VMEM)],
-        out_specs=pl.BlockSpec(memory_space=pl.ANY),
-        out_shape=jax.ShapeDtypeStruct((copies,) + queries.shape, queries.dtype),
-        scratch_shapes=[pltpu.SemaphoreType.DMA((copies,))],
+        out_shape=jax.ShapeDtypeStruct(shape, queries.dtype),
         name="spread_queries",
     )(queries)
 
@@ -342,7 +335,7 @@
     wide = lax.axis_size("x")
     low = lax.axis_size("yl")
 
-    gathered = lax.all_to_all(spread(queries, ctx), "ctx", 0, 0, tiled=False)
+    gathered = lax.all_to_all(spread(queries, ctx, kv_local), "ctx", 0, 0, tiled=False)
     weights = [out_weight]
     for k in range(1, wide):
         pairs = [(x, (x + k) % wide) for x in range(wide)]

time: 80.3 us -> 80.4 us (level)
  no operation moved by 1% of the time
where the time goes in v9:
time: 80.4 us; the launch traced here: 79.9 us
  blocking collectives  34.6 us (43%)
  starting transfers between devices  18.1 us (23%)
  Pallas kernels  15.7 us (20%)
  waiting for transfers between devices  9.38 us (12%)
  local copies, waits for them, and re-layouts  1.96 us (2%)
    all_to_all x1, blocking collectives, per_device(): lax.all_to_all(partial_out, ('yh', 'core', 'x'), 0, 0, tiled=True)  18.2 us
    all_to_all x1, blocking collectives, per_device(): everyone = lax.all_to_all(everyone, ('ctx', 'yl'), 0, 0, tiled=True)  16.4 us
    all_to_all x1, starting transfers between devices, per_device(): lax.all_to_all(spread(queries, ctx, kv_local), 'ctx', 0, 0, tiled=False)  9.01 us
    pallas_call x1, Pallas kernels, prefix_attention(): pl.pallas_call(functools.partial(prefix_kernel, scale, k_first.shape[1],...  8.69 us
    all_to_all x1, waiting for transfers between devices, per_device(): parts = lax.all_to_all(parts, 'ctx', 0, 0, tiled=True)  6.39 us
    ppermute x3, starting transfers between devices, per_device(): weights.append(lax.ppermute(out_weight, 'x', pairs))  5.42 us
    all_to_all x1, starting transfers between devices, per_device(): parts = lax.all_to_all(parts, 'ctx', 0, 0, tiled=True)  3.71 us
    pallas_call x1, Pallas kernels, suffix_attention(): pl.pallas_call(functools.partial(suffix_kernel, scale), grid_spec=pltpu.P...  3.31 us
  transfers between devices with their start and end apart: 5, of which 2 were waited for; matrix products, arithmetic and copies ran while one was open for 2% of the time, Pallas kernels for 16%

profile of v9, /device:TPU:1, one launch (start us, length us, event | category | flops | bytes accessed | tf_op | source)
XLA Modules:
  0.0 79.9 jit_solution(3017070251253745691)
XLA Ops:
  0.0 1.5 %spread_queries.1 = bf16[8,2,64,128]{3,2,1,0:T(8,128)(2,1)} custom-call(bf16[8,16,128]{2,1,0:T(8,128)(2,1)} %q_ref.2), custom_call_target="tpu_custom_call" | custom-call | tf_op jit(solution)/shard_map/spread_queries/pallas_call | solution.py:322
  1.5 9.0 %all-to-all-start = ((bf16[8,2,64,128]{3,2,1,0:T(8,128)(2,1)}), bf16[8,2,64,128]{3,2,1,0:T(8,128)(2,1)S(1)}, u32[]{:S(2)}, u32[]{:S(2)}) async-start(bf16[8,2,64,128]{3,2,1,0:T(8,128)(2,1)} %spread_queries.1), calls=%async_computation | async-start | bytes 524288 | tf_op jit(solution)/shard_map/all_to_all | solution.py:338
  10.5 2.7 %collective-permute-start.1 = (bf16[2048,128]{1,0:T(8,128)(2,1)}, bf16[2048,128]{1,0:T(8,128)(2,1)S(1)}, u32[]{:S(2)}, u32[]{:S(2)}) collective-permute-start(bf16[2048,128]{1,0:T(8,128)(2,1)} %refs_0_), channel_id=1, source_target_pairs={{0,2},{1,3},{2,0},{3,1},{4,6},{5,7},{6,4},{7,5},{8,10},{9,11},{10,... | collective-permute-start | bytes 1572872 | tf_op jit(solution)/shard_map/ppermute | solution.py:342
  13.3 0.3 collective-permute-start
  13.6 2.4 %collective-permute-start.2 = (bf16[2048,128]{1,0:T(8,128)(2,1)}, bf16[2048,128]{1,0:T(8,128)(2,1)S(1)}, u32[]{:S(2)}, u32[]{:S(2)}) collective-permute-start(bf16[2048,128]{1,0:T(8,128)(2,1)} %refs_0_), channel_id=1, source_target_pairs={{0,3},{1,0},{2,1},{3,2},{4,7},{5,4},{6,5},{7,6},{8,11},{9,8},{10,9... | collective-permute-start | bytes 1572872 | tf_op jit(solution)/shard_map/ppermute | solution.py:342
  15.9 1.0 %slice.6.k_first = bf16[2,512,128]{2,1,0:T(8,128)(2,1)S(1)} slice(bf16[2,6144,128]{2,1,0:T(8,128)(2,1)} %k_hbm.1), slice={[0:2], [0:512], [0:128]} | slice | bytes 524288 | tf_op jit(solution)/shard_map/slice | solution.py:345
  16.9 1.0 %slice.7.v_first = bf16[2,512,128]{2,1,0:T(8,128)(2,1)S(1)} slice(bf16[2,6144,128]{2,1,0:T(8,128)(2,1)} %v_hbm.1), slice={[0:2], [0:512], [0:128]} | slice | bytes 524288 | tf_op jit(solution)/shard_map/slice | solution.py:345
  17.9 0.0 copy-start.1
  17.9 0.0 copy-start.2
  17.9 3.0 %all-to-all-done.q_ref = bf16[8,2,64,128]{3,2,1,0:T(8,128)(2,1)S(1)} async-done(((bf16[8,2,64,128]{3,2,1,0:T(8,128)(2,1)}), bf16[8,2,64,128]{3,2,1,0:T(8,128)(2,1)S(1)}, u32[]{:S(2)}, u32[]{:S(2)}) %all-to-all-start) | async-done | bytes 262176 | tf_op jit(solution)/shard_map/all_to_all | solution.py:338
  20.9 8.7 %prefix_attention.1 = bf16[8,136,128]{2,1,0:T(8,128)(2,1)} custom-call(bf16[8,2,64,128]{3,2,1,0:T(8,128)(2,1)S(1)} %all-to-all-done.q_ref, bf16[2,512,128]{2,1,0:T(8,128)(2,1)S(1)} %slice.6.k_first, bf16[2,512,128]{2,1,0:T(8,128)(2,1)S(1)} %slice.7.v_first, bf16[2,6144,128]{2,1,0:T(8,128)(2,1)} %k_hbm.1, bf16[2,6144,128]{2,1,0:T(8,128)(2,1)} %v_hbm.1), custom_call_target="tpu_custom_call" | custom-call | flops 3221225472 | bytes 6291456 | tf_op jit(solution)/shard_map/prefix_attention/pallas_call | solution.py:130
  29.6 3.7 %all-to-all-start.1 = ((bf16[8,136,128]{2,1,0:T(8,128)(2,1)}), bf16[8,136,128]{2,1,0:T(8,128)(2,1)S(1)}, u32[]{:S(2)}, u32[]{:S(2)}) async-start(bf16[8,136,128]{2,1,0:T(8,128)(2,1)} %prefix_attention.1), calls=%async_computation.1 | async-start | bytes 557056 | tf_op jit(solution)/shard_map/all_to_all | solution.py:349
  33.3 0.0 copy-done.1
  33.3 0.0 copy-done.2
  33.3 0.0 copy-start
  33.3 3.3 %suffix_attention.1 = (f32[128,128]{1,0:T(8,128)S(1)}, f32[128,128]{1,0:T(8,128)S(1)}) custom-call(s32[8]{0:T(128)S(1)} %copy-done.2, bf16[8,16,128]{2,1,0:T(8,128)(2,1)S(1)} %copy-done.1, bf16[8,2,512,128]{3,2,1,0:T(8,128)(2,1)} %k_ref.1, bf16[8,2,512,128]{3,2,1,0:T(8,128)(2,1)} %v_ref.1), custom_call_target="tpu_custom_call" | custom-call | flops 33554432 | bytes 4194304 | tf_op jit(solution)/shard_map/suffix_attention/pallas_call | solution.py:201
  36.6 6.4 %all-to-all-done.1.parts_ref = bf16[8,136,128]{2,1,0:T(8,128)(2,1)S(1)} async-done(((bf16[8,136,128]{2,1,0:T(8,128)(2,1)}), bf16[8,136,128]{2,1,0:T(8,128)(2,1)S(1)}, u32[]{:S(2)}, u32[]{:S(2)}) %all-to-all-start.1) | async-done | bytes 278560 | tf_op jit(solution)/shard_map/all_to_all | solution.py:349
  43.0 0.8 %merge_shards.1 = bf16[16,8,2048]{2,1,0:T(8,128)(2,1)S(1)} custom-call(bf16[8,136,128]{2,1,0:T(8,128)(2,1)S(1)} %all-to-all-done.1.parts_ref, f32[128,128]{1,0:T(8,128)S(1)} %get-tuple-element.18.suffix_ref, f32[128,128]{1,0:T(8,128)S(1)} %get-tuple-element.19.suffix_lse_ref), custom_call_target="tpu_custom_call" | custom-call | tf_op jit(solution)/shard_map/merge_shards/pallas_call | solution.py:260
  43.9 0.0 collective-permute-done.1.refs_2_
  43.9 0.0 collective-permute-done.refs_1_
  43.9 0.0 collective-permute-done.2.refs_3_
  43.9 16.4 %all_to_all.20 = bf16[16,8,2048]{2,1,0:T(8,128)(2,1)S(1)} all-to-all(bf16[16,8,2048]{2,1,0:T(8,128)(2,1)S(1)} %merge_shards.1), channel_id=1, replica_groups=mesh['ctx'=8,'yh'=2,'core'=2,'yl'=2,'x'=4] {'ctx','yl'}, dimensions={0} | all-to-all | bytes 1048576 | tf_op jit(solution)/shard_map/all_to_all | solution.py:355
  60.3 0.0 copy-done
  60.4 0.7 project.1
  61.1 18.2 %all_to_all.21 = bf16[16,32,128]{2,1,0:T(8,128)(2,1)S(1)} all-to-all(bf16[16,32,128]{2,1,0:T(8,128)(2,1)S(1)} %bitcast.6), channel_id=1, replica_groups=mesh['ctx'=8,'yh'=2,'core'=2,'yl'=2,'x'=4] {'yh','core','x'}, dimensions={0} | all-to-all | bytes 262144 | tf_op jit(solution)/shard_map/all_to_all | solution.py:359
  79.2 0.6 sum_heads.1
Async XLA Ops:
  1.5 19.4 %all-to-all-start = ((bf16[8,2,64,128]{3,2,1,0:T(8,128)(2,1)}), bf16[8,2,64,128]{3,2,1,0:T(8,128)(2,1)S(1)}, u32[]{:S(2)}, u32[]{:S(2)}) async-start(bf16[8,2,64,128]{3,2,1,0:T(8,128)(2,1)} %spread_queries.1), calls=%async_computation | async-start | bytes 524288 | tf_op jit(solution)/shard_map/all_to_all | solution.py:338
  10.5 33.4 %collective-permute-start.1 = (bf16[2048,128]{1,0:T(8,128)(2,1)}, bf16[2048,128]{1,0:T(8,128)(2,1)S(1)}, u32[]{:S(2)}, u32[]{:S(2)}) collective-permute-start(bf16[2048,128]{1,0:T(8,128)(2,1)} %refs_0_), channel_id=1, source_target_pairs={{0,2},{1,3},{2,0},{3,1},{4,6},{5,7},{6,4},{7,5},{8,10},{9,11},{10,... | collective-permute-start | bytes 1572872 | tf_op jit(solution)/shard_map/ppermute | solution.py:342
  13.3 30.6 %collective-permute-start = (bf16[2048,128]{1,0:T(8,128)(2,1)}, bf16[2048,128]{1,0:T(8,128)(2,1)S(1)}, u32[]{:S(2)}, u32[]{:S(2)}) collective-permute-start(bf16[2048,128]{1,0:T(8,128)(2,1)} %refs_0_), channel_id=1, source_target_pairs={{0,1},{1,2},{2,3},{3,0},{4,5},{5,6},{6,7},{7,4},{8,9},{9,10},{10,1... | collective-permute-start | bytes 1572872 | tf_op jit(solution)/shard_map/ppermute | solution.py:342
  13.6 30.3 %collective-permute-start.2 = (bf16[2048,128]{1,0:T(8,128)(2,1)}, bf16[2048,128]{1,0:T(8,128)(2,1)S(1)}, u32[]{:S(2)}, u32[]{:S(2)}) collective-permute-start(bf16[2048,128]{1,0:T(8,128)(2,1)} %refs_0_), channel_id=1, source_target_pairs={{0,3},{1,0},{2,1},{3,2},{4,7},{5,4},{6,5},{7,6},{8,11},{9,8},{10,9... | collective-permute-start | bytes 1572872 | tf_op jit(solution)/shard_map/ppermute | solution.py:342
  17.9 15.4 %copy-start.1 = (bf16[8,16,128]{2,1,0:T(8,128)(2,1)S(1)}, bf16[8,16,128]{2,1,0:T(8,128)(2,1)}, u32[]{:S(2)}) copy-start(bf16[8,16,128]{2,1,0:T(8,128)(2,1)} %q_ref.2) | copy-start | bytes 98308
  17.9 15.4 %copy-start.2 = (s32[8]{0:T(128)S(1)}, s32[8]{0:T(128)}, u32[]{:S(2)}) copy-start(s32[8]{0:T(128)} %lengths_ref.1) | copy-start | bytes 100
  29.6 13.5 %all-to-all-start.1 = ((bf16[8,136,128]{2,1,0:T(8,128)(2,1)}), bf16[8,136,128]{2,1,0:T(8,128)(2,1)S(1)}, u32[]{:S(2)}, u32[]{:S(2)}) async-start(bf16[8,136,128]{2,1,0:T(8,128)(2,1)} %prefix_attention.1), calls=%async_computation.1 | async-start | bytes 557056 | tf_op jit(solution)/shard_map/all_to_all | solution.py:349
  33.3 27.0 %copy-start = (bf16[2048,128]{1,0:T(8,128)(2,1)S(1)}, bf16[2048,128]{1,0:T(8,128)(2,1)}, u32[]{:S(2)}) copy-start(bf16[2048,128]{1,0:T(8,128)(2,1)} %refs_0_) | copy-start | bytes 1572868

commit v10 on v9

--- a/solution.py
+++ b/solution.py
@@ -22,13 +22,13 @@
 
 
 def prefix_kernel(
-    scale, tile, first, q_ref, k_first, v_first, k_hbm, v_hbm, o_ref, k_ref, v_ref, acc_ref, top_ref,
+    scale, tile, first, q_ref, k_hbm, v_hbm, o_ref, k_ref, v_ref, acc_ref, top_ref,
     total_ref, lse_ref, k_sem, v_sem,
 ):
     head = pl.program_id(0)
     sources, _, rows, dim = q_ref.shape
     heads, length, _ = k_ref.shape
-    parts = [(tile, first - tile), (first, length - first)]
+    parts = [(0, first), (first, length - first)]
 
     def copy_of(source, target, sem, h, part):
         span = pl.ds(*parts[part])
@@ -43,22 +43,19 @@
 
     queries = q_ref[...].reshape(sources * rows, dim)
 
-    def scores_of(start, keys=None):
-        if keys is None:
-            keys = k_ref[head, pl.ds(start, tile), :]
+    def scores_of(start):
+        keys = k_ref[head, pl.ds(start, tile), :]
         return lax.dot_general(keys, queries, NT, preferred_element_type=F32)
 
-    def product_of(weights, start, values=None):
-        if values is None:
-            values = v_ref[head, pl.ds(start, tile), :]
+    def product_of(weights, start):
+        values = v_ref[head, pl.ds(start, tile), :]
         return lax.dot_general(values, weights.astype(BF16), TN, preferred_element_type=F32)
 
-    scores = scores_of(0, k_first[head])
+    copy_of(k_hbm, k_ref, k_sem, head, 0).wait()
+    scores = scores_of(0)
     top = jnp.max(scores, axis=0, keepdims=True)
     for start in range(0, length, tile):
         if start == 0:
-            copy_of(k_hbm, k_ref, k_sem, head, 0).wait()
-        if start == tile:
             copy_of(v_hbm, v_ref, v_sem, head, 0).wait()
         if start == first:
             copy_of(v_hbm, v_ref, v_sem, head, 1).wait()
@@ -67,7 +64,7 @@
         ahead = scores_of(start + tile) if start + tile < length else None
         weights = jnp.exp2((scores - top) * scale)
         share = jnp.sum(weights, axis=0, keepdims=True)
-        product = product_of(weights, start, v_first[head] if start == 0 else None)
+        product = product_of(weights, start)
         if start == 0:
             total = share
             acc_ref[...] = product
@@ -85,8 +82,6 @@
         top_ref[...] = jnp.full_like(top_ref, -1e30)
         total_ref[...] = jnp.zeros_like(total_ref)
         acc_ref[...] = jnp.zeros_like(acc_ref)
-        k_ref[head, :tile] = k_first[head]
-        v_ref[head, :tile] = v_first[head]
 
         def step(index, carry):
             start = pl.multiple_of(index * tile, tile)
@@ -123,17 +118,15 @@
             o_ref[c, heads * rows : heads * rows + 8, :] = stats.astype(BF16)
 
 
-def prefix_attention(q, k_first, v_first, keys, values, scale):
+def prefix_attention(q, keys, values, scale):
     sources, heads, rows, dim = q.shape
     length = keys.shape[1]
     total_rows = sources * rows
     return pl.pallas_call(
-        functools.partial(prefix_kernel, scale, k_first.shape[1], 2 * k_first.shape[1]),
+        functools.partial(prefix_kernel, scale, length // 12, length // 6),
         grid=(heads,),
         in_specs=[
             pl.BlockSpec((sources, 1, rows, dim), lambda h: (0, h, 0, 0)),
-            pl.BlockSpec(k_first.shape, lambda h: (0, 0, 0)),
-            pl.BlockSpec(v_first.shape, lambda h: (0, 0, 0)),
             pl.BlockSpec(memory_space=pltpu.HBM),
             pl.BlockSpec(memory_space=pltpu.HBM),
         ],
@@ -160,8 +153,6 @@
         name="prefix_attention",
     )(
         q,
-        k_first,
-        v_first,
         pltpu.with_memory_space_constraint(keys, pltpu.HBM),
         pltpu.with_memory_space_constraint(values, pltpu.HBM),
     )
@@ -341,9 +332,7 @@
         pairs = [(x, (x + k) % wide) for x in range(wide)]
         weights.append(lax.ppermute(out_weight, "x", pairs))
 
-    tile = prefix_keys.shape[1] // 12
-    k_first, v_first = prefix_keys[:, :tile], prefix_values[:, :tile]
-    parts = prefix_attention(gathered, k_first, v_first, prefix_keys, prefix_values, scale)
+    parts = prefix_attention(gathered, prefix_keys, prefix_values, scale)
     place = lax.axis_index("x").astype(jnp.int32).reshape(1)
     parts, queries, place = lax.optimization_barrier((parts, queries, place))
     parts = lax.all_to_all(parts, "ctx", 0, 0, tiled=True)

time: 80.4 us -> 80.3 us (level)
  local copies, waits for them, and re-layouts: 1.96 us -> 0.01 us
  waiting for transfers between devices: 9.38 us -> 11.2 us
    all_to_all x1, waiting for transfers between devices: 2.98 us -> 4.94 us  [per_device(): lax.all_to_all(spread(queries, ctx, kv_local), 'ctx', 0, 0, tiled=False)]
    slice x2 -> x0, local copies, waits for them, and re-layouts: 1.94 us -> none  [per_device(): k_first, v_first = (prefix_keys[:, :tile], prefix_values[:, :tile])]
    all_to_all x1, blocking collectives: 18.2 us -> 19.3 us  [per_device(): lax.all_to_all(partial_out, ('yh', 'core', 'x'), 0, 0, tiled=True)]
  transfers between devices with their start and end apart: 5 -> 5, of which waited for: 2 -> 2; matrix products, arithmetic and copies ran while one was open for 2% -> 0% of each run, Pallas kernels for 16% -> 16%
where the time goes in v10:
time: 80.3 us; the launch traced here: 79.9 us
  blocking collectives  35.1 us (44%)
  starting transfers between devices  17.9 us (22%)
  Pallas kernels  15.7 us (20%)
  waiting for transfers between devices  11.2 us (14%)
    all_to_all x1, blocking collectives, per_device(): lax.all_to_all(partial_out, ('yh', 'core', 'x'), 0, 0, tiled=True)  19.3 us
    all_to_all x1, blocking collectives, per_device(): everyone = lax.all_to_all(everyone, ('ctx', 'yl'), 0, 0, tiled=True)  15.8 us
    all_to_all x1, starting transfers between devices, per_device(): lax.all_to_all(spread(queries, ctx, kv_local), 'ctx', 0, 0, tiled=False)  9.01 us
    pallas_call x1, Pallas kernels, prefix_attention(): pl.pallas_call(functools.partial(prefix_kernel, scale, length // 12, leng...  8.71 us
    all_to_all x1, waiting for transfers between devices, per_device(): parts = lax.all_to_all(parts, 'ctx', 0, 0, tiled=True)  6.22 us
    ppermute x3, starting transfers between devices, per_device(): weights.append(lax.ppermute(out_weight, 'x', pairs))  5.42 us
    all_to_all x1, waiting for transfers between devices, per_device(): lax.all_to_all(spread(queries, ctx, kv_local), 'ctx', 0, 0, tiled=False)  4.94 us
    all_to_all x1, starting transfers between devices, per_device(): parts = lax.all_to_all(parts, 'ctx', 0, 0, tiled=True)  3.43 us
  transfers between devices with their start and end apart: 5, of which 2 were waited for; matrix products, arithmetic and copies ran while one was open for 0% of the time, Pallas kernels for 16%

profile of v10, /device:TPU:1, one launch (start us, length us, event | category | flops | bytes accessed | tf_op | source)
XLA Modules:
  0.0 79.9 jit_solution(1465293402691584479)
XLA Ops:
  0.0 1.5 %spread_queries.1 = bf16[8,2,64,128]{3,2,1,0:T(8,128)(2,1)} custom-call(bf16[8,16,128]{2,1,0:T(8,128)(2,1)} %q_ref.2), custom_call_target="tpu_custom_call" | custom-call | tf_op jit(solution)/shard_map/spread_queries/pallas_call | solution.py:313
  1.5 9.0 %all-to-all-start = ((bf16[8,2,64,128]{3,2,1,0:T(8,128)(2,1)}), bf16[8,2,64,128]{3,2,1,0:T(8,128)(2,1)S(1)}, u32[]{:S(2)}, u32[]{:S(2)}) async-start(bf16[8,2,64,128]{3,2,1,0:T(8,128)(2,1)} %spread_queries.1), calls=%async_computation | async-start | bytes 524288 | tf_op jit(solution)/shard_map/all_to_all | solution.py:329
  10.5 2.7 %collective-permute-start.1 = (bf16[2048,128]{1,0:T(8,128)(2,1)}, bf16[2048,128]{1,0:T(8,128)(2,1)S(1)}, u32[]{:S(2)}, u32[]{:S(2)}) collective-permute-start(bf16[2048,128]{1,0:T(8,128)(2,1)} %refs_0_), channel_id=1, source_target_pairs={{0,2},{1,3},{2,0},{3,1},{4,6},{5,7},{6,4},{7,5},{8,10},{9,11},{10,... | collective-permute-start | bytes 1572872 | tf_op jit(solution)/shard_map/ppermute | solution.py:333
  13.3 0.3 collective-permute-start
  13.6 2.4 %collective-permute-start.2 = (bf16[2048,128]{1,0:T(8,128)(2,1)}, bf16[2048,128]{1,0:T(8,128)(2,1)S(1)}, u32[]{:S(2)}, u32[]{:S(2)}) collective-permute-start(bf16[2048,128]{1,0:T(8,128)(2,1)} %refs_0_), channel_id=1, source_target_pairs={{0,3},{1,0},{2,1},{3,2},{4,7},{5,4},{6,5},{7,6},{8,11},{9,8},{10,9... | collective-permute-start | bytes 1572872 | tf_op jit(solution)/shard_map/ppermute | solution.py:333
  15.9 0.0 copy-start.1
  15.9 0.0 copy-start.2
  15.9 4.9 %all-to-all-done.q_ref = bf16[8,2,64,128]{3,2,1,0:T(8,128)(2,1)S(1)} async-done(((bf16[8,2,64,128]{3,2,1,0:T(8,128)(2,1)}), bf16[8,2,64,128]{3,2,1,0:T(8,128)(2,1)S(1)}, u32[]{:S(2)}, u32[]{:S(2)}) %all-to-all-start) | async-done | bytes 262176 | tf_op jit(solution)/shard_map/all_to_all | solution.py:329
  20.9 8.7 %prefix_attention.1 = bf16[8,136,128]{2,1,0:T(8,128)(2,1)} custom-call(bf16[8,2,64,128]{3,2,1,0:T(8,128)(2,1)S(1)} %all-to-all-done.q_ref, bf16[2,6144,128]{2,1,0:T(8,128)(2,1)} %k_hbm.1, bf16[2,6144,128]{2,1,0:T(8,128)(2,1)} %v_hbm.1), custom_call_target="tpu_custom_call" | custom-call | flops 3221225472 | bytes 6291456 | tf_op jit(solution)/shard_map/prefix_attention/pallas_call | solution.py:125
  29.6 3.4 %all-to-all-start.1 = ((bf16[8,136,128]{2,1,0:T(8,128)(2,1)}), bf16[8,136,128]{2,1,0:T(8,128)(2,1)S(1)}, u32[]{:S(2)}, u32[]{:S(2)}) async-start(bf16[8,136,128]{2,1,0:T(8,128)(2,1)} %prefix_attention.1), calls=%async_computation.1 | async-start | bytes 557056 | tf_op jit(solution)/shard_map/all_to_all | solution.py:338
  33.0 0.0 copy-done.1
  33.0 0.0 copy-done.2
  33.1 0.0 copy-start
  33.1 3.3 %suffix_attention.1 = (f32[128,128]{1,0:T(8,128)S(1)}, f32[128,128]{1,0:T(8,128)S(1)}) custom-call(s32[8]{0:T(128)S(1)} %copy-done.2, bf16[8,16,128]{2,1,0:T(8,128)(2,1)S(1)} %copy-done.1, bf16[8,2,512,128]{3,2,1,0:T(8,128)(2,1)} %k_ref.1, bf16[8,2,512,128]{3,2,1,0:T(8,128)(2,1)} %v_ref.1), custom_call_target="tpu_custom_call" | custom-call | flops 33554432 | bytes 4194304 | tf_op jit(solution)/shard_map/suffix_attention/pallas_call | solution.py:192
  36.4 6.2 %all-to-all-done.1.parts_ref = bf16[8,136,128]{2,1,0:T(8,128)(2,1)S(1)} async-done(((bf16[8,136,128]{2,1,0:T(8,128)(2,1)}), bf16[8,136,128]{2,1,0:T(8,128)(2,1)S(1)}, u32[]{:S(2)}, u32[]{:S(2)}) %all-to-all-start.1) | async-done | bytes 278560 | tf_op jit(solution)/shard_map/all_to_all | solution.py:338
  42.6 0.8 %merge_shards.1 = bf16[16,8,2048]{2,1,0:T(8,128)(2,1)S(1)} custom-call(bf16[8,136,128]{2,1,0:T(8,128)(2,1)S(1)} %all-to-all-done.1.parts_ref, f32[128,128]{1,0:T(8,128)S(1)} %get-tuple-element.18.suffix_ref, f32[128,128]{1,0:T(8,128)S(1)} %get-tuple-element.19.suffix_lse_ref), custom_call_target="tpu_custom_call" | custom-call | tf_op jit(solution)/shard_map/merge_shards/pallas_call | solution.py:251
  43.4 0.0 collective-permute-done.1.refs_2_
  43.4 0.0 collective-permute-done.refs_1_
  43.5 0.0 collective-permute-done.2.refs_3_
  43.5 15.8 %all_to_all.20 = bf16[16,8,2048]{2,1,0:T(8,128)(2,1)S(1)} all-to-all(bf16[16,8,2048]{2,1,0:T(8,128)(2,1)S(1)} %merge_shards.1), channel_id=1, replica_groups=mesh['ctx'=8,'yh'=2,'core'=2,'yl'=2,'x'=4] {'ctx','yl'}, dimensions={0} | all-to-all | bytes 1048576 | tf_op jit(solution)/shard_map/all_to_all | solution.py:344
  59.3 0.0 copy-done
  59.3 0.7 project.1
  60.0 19.3 %all_to_all.21 = bf16[16,32,128]{2,1,0:T(8,128)(2,1)S(1)} all-to-all(bf16[16,32,128]{2,1,0:T(8,128)(2,1)S(1)} %bitcast.6), channel_id=1, replica_groups=mesh['ctx'=8,'yh'=2,'core'=2,'yl'=2,'x'=4] {'yh','core','x'}, dimensions={0} | all-to-all | bytes 262144 | tf_op jit(solution)/shard_map/all_to_all | solution.py:348
  79.3 0.6 sum_heads.1
Async XLA Ops:
  1.5 19.4 %all-to-all-start = ((bf16[8,2,64,128]{3,2,1,0:T(8,128)(2,1)}), bf16[8,2,64,128]{3,2,1,0:T(8,128)(2,1)S(1)}, u32[]{:S(2)}, u32[]{:S(2)}) async-start(bf16[8,2,64,128]{3,2,1,0:T(8,128)(2,1)} %spread_queries.1), calls=%async_computation | async-start | bytes 524288 | tf_op jit(solution)/shard_map/all_to_all | solution.py:329
  10.5 32.9 %collective-permute-start.1 = (bf16[2048,128]{1,0:T(8,128)(2,1)}, bf16[2048,128]{1,0:T(8,128)(2,1)S(1)}, u32[]{:S(2)}, u32[]{:S(2)}) collective-permute-start(bf16[2048,128]{1,0:T(8,128)(2,1)} %refs_0_), channel_id=1, source_target_pairs={{0,2},{1,3},{2,0},{3,1},{4,6},{5,7},{6,4},{7,5},{8,10},{9,11},{10,... | collective-permute-start | bytes 1572872 | tf_op jit(solution)/shard_map/ppermute | solution.py:333
  13.3 30.2 %collective-permute-start = (bf16[2048,128]{1,0:T(8,128)(2,1)}, bf16[2048,128]{1,0:T(8,128)(2,1)S(1)}, u32[]{:S(2)}, u32[]{:S(2)}) collective-permute-start(bf16[2048,128]{1,0:T(8,128)(2,1)} %refs_0_), channel_id=1, source_target_pairs={{0,1},{1,2},{2,3},{3,0},{4,5},{5,6},{6,7},{7,4},{8,9},{9,10},{10,1... | collective-permute-start | bytes 1572872 | tf_op jit(solution)/shard_map/ppermute | solution.py:333
  13.6 29.9 %collective-permute-start.2 = (bf16[2048,128]{1,0:T(8,128)(2,1)}, bf16[2048,128]{1,0:T(8,128)(2,1)S(1)}, u32[]{:S(2)}, u32[]{:S(2)}) collective-permute-start(bf16[2048,128]{1,0:T(8,128)(2,1)} %refs_0_), channel_id=1, source_target_pairs={{0,3},{1,0},{2,1},{3,2},{4,7},{5,4},{6,5},{7,6},{8,11},{9,8},{10,9... | collective-permute-start | bytes 1572872 | tf_op jit(solution)/shard_map/ppermute | solution.py:333
  15.9 17.1 %copy-start.1 = (bf16[8,16,128]{2,1,0:T(8,128)(2,1)S(1)}, bf16[8,16,128]{2,1,0:T(8,128)(2,1)}, u32[]{:S(2)}) copy-start(bf16[8,16,128]{2,1,0:T(8,128)(2,1)} %q_ref.2) | copy-start | bytes 98308
  15.9 17.1 %copy-start.2 = (s32[8]{0:T(128)S(1)}, s32[8]{0:T(128)}, u32[]{:S(2)}) copy-start(s32[8]{0:T(128)} %lengths_ref.1) | copy-start | bytes 100
  29.6 13.0 %all-to-all-start.1 = ((bf16[8,136,128]{2,1,0:T(8,128)(2,1)}), bf16[8,136,128]{2,1,0:T(8,128)(2,1)S(1)}, u32[]{:S(2)}, u32[]{:S(2)}) async-start(bf16[8,136,128]{2,1,0:T(8,128)(2,1)} %prefix_attention.1), calls=%async_computation.1 | async-start | bytes 557056 | tf_op jit(solution)/shard_map/all_to_all | solution.py:338
  33.1 26.2 %copy-start = (bf16[2048,128]{1,0:T(8,128)(2,1)S(1)}, bf16[2048,128]{1,0:T(8,128)(2,1)}, u32[]{:S(2)}) copy-start(bf16[2048,128]{1,0:T(8,128)(2,1)} %refs_0_) | copy-start | bytes 1572868
